TPU v7x, 32 devices: a whole 2x2x4 slice. The times are simulated.
32 devices in a mesh: row: 16 (over z, y, x), col: 2 (over core).
Axes of the slice: x: 2, y: 2, z: 4, core: 2. Of those that a mesh axis runs over, the one named last changes fastest.
Arguments:
- panel_u: bfloat16 [16, 2560, 128], P('row'), may hold values from -0.125 to 0.125
- panel_v: bfloat16 [16, 2560, 128], P('row', 'col'), may hold values from -0.25 to 0.25
- linv: bfloat16 [2560, 2560], P('row', 'col')
- trail_u: bfloat16 [16, 4, 2560, 128], P('row', 'col'), may hold values from -0.125 to 0.125
- trail_v: bfloat16 [16, 4, 2560, 128], P('row', 'col'), may hold values from -0.125 to 0.125
- rank_map: int32 [16, 16], replicated, may hold values from 32 to 128, as said below
- tile_of_slot: int32 [16], replicated, may hold values from 0 to 15, each once
- band_cols: int32 [4], P('col'), may hold values from 0 to 15, as said below
Outputs:
- gram_left: float32 [16, 4, 256, 256], P('row', 'col')
- gram_right: float32 [16, 4, 256, 256], P('row', 'col')
Inputs may be any that keep to these rules, and one draw needn't show every extreme that they name: rank_map[i, j] for j != i is the rank of trailing tile (i, j), including band tiles with j > i, whose core is zero; rank_map[i, i] is the rank of panel tile i; some panel tile has rank 128. `tile_of_slot`: a permutation. `band_cols`: distinct values.
All inputs are finite; a program needn't handle non-finite values.
Results may differ from a plain program's by a relative error of at most 0.0049.
Values may be sent and summed in bfloat16 or wider, within the bound.
No kernel may reach another device: no remote copies, remote signals or barrier semaphores. Data moves between devices by JAX's collectives and lax.ppermute only.
A program may use at most 64 MiB of HBM per device.

v0:
```python
import functools

import jax
import jax.numpy as jnp
from jax import lax
from jax.experimental import pallas as pl
from jax.experimental.pallas import tpu as pltpu
from jax.sharding import PartitionSpec as P


SCRATCH_BYTES = 16 * 1024 * 1024

VMEM = pl.BlockSpec(memory_space=pltpu.VMEM)
SMEM = pl.BlockSpec(memory_space=pltpu.SMEM)


def cross_rows(first, second):
    return lax.dot_general(
        first, second, (((0,), (0,)), ((), ())), preferred_element_type=jnp.float32
    )


def slot_of(tiles_ref, tile):
    slot = jnp.int32(0)
    for s in range(tiles_ref.shape[0]):
        slot = jnp.where(tiles_ref[s] == tile, jnp.int32(s), slot)
    return slot


def keep_mask(width, first_rank, second_rank):
    rows = lax.broadcasted_iota(jnp.int32, (2 * width, 2 * width), 0)
    cols = lax.broadcasted_iota(jnp.int32, (2 * width, 2 * width), 1)

    def kept(ids):
        return ids < jnp.where(ids < width, first_rank, second_rank + width)

    return kept(rows) & kept(cols)


def solve_kernel(ids_ref, *refs, pieces, cols):
    inner = len(pieces)
    count = sum(pieces)
    l_refs, v_refs, out_refs = refs[:count], refs[count : len(refs) - cols], refs[-cols:]
    per_col = inner // cols
    low, core = ids_ref[1], ids_ref[2]
    factors = jnp.concatenate([ref[...] for ref in v_refs], axis=1)
    rows = l_refs[0].shape[0]
    if rows % 16 == 0:
        lines = jnp.concatenate([ref[...] for ref in l_refs], axis=0)
        value = jnp.dot(lines, factors, preferred_element_type=jnp.float32)
        values = [value[k * rows : (k + 1) * rows] for k in range(inner)]
    else:
        values = [
            jnp.dot(ref[...], factors, preferred_element_type=jnp.float32) for ref in l_refs
        ]
    for k in range(inner):
        block = low ^ k
        owner = (block // per_col) ^ core
        at = pl.multiple_of((block % per_col) * rows, 8)
        for j in range(cols):

            @pl.when(owner == j)
            def _():
                out_refs[j][pl.ds(at, rows), :] = values[k]


def core_kernel(ids_ref, tiles_ref, *refs, inner, cols, width, first):
    bands_refs, s_refs = refs[:cols], refs[cols : cols + 2 * inner]
    out_refs, picked = refs[cols + 2 * inner : -1], refs[-1]
    high, low = ids_ref[0], ids_ref[1]
    per_col = bands_refs[0].shape[0]
    for j in range(cols):
        for b in range(per_col):
            source = slot_of(tiles_ref, bands_refs[j][b])
            block = low ^ (source % inner)
            slot = high ^ (source // inner)
            place = (j * per_col + b) * width
            for k in range(inner):

                @pl.when((block == k) & (slot < first))
                def _():
                    at = pl.multiple_of(slot * width, width)
                    picked[:, place : place + width] = s_refs[2 * k][:, pl.ds(at, width)]

                @pl.when((block == k) & (slot >= first))
                def _():
                    at = pl.multiple_of((slot - first) * width, width)
                    picked[:, place : place + width] = s_refs[2 * k + 1][:, pl.ds(at, width)]

    own = jnp.concatenate([s_refs[0][...], s_refs[1][...]], axis=1)
    value = cross_rows(own, picked[...])
    for j in range(cols):
        out_refs[j][...] = value[:, j * per_col * width : (j + 1) * per_col * width]


def split_kernel(*refs, outer):
    total = refs[0][...]
    for ref in refs[1:-outer]:
        total = total + ref[...]
    rows = total.shape[0] // outer
    for m in range(outer):
        refs[m - outer][...] = total[m * rows : (m + 1) * rows]


def round_kernel(*refs):
    total = refs[0][...]
    for ref in refs[1:-1]:
        total = total + ref[...]
    refs[-1][...] = total.astype(refs[-1].dtype)


def left_kernel(ids_ref, tiles_ref, ranks_ref, bands_ref, trail_ref, panel_ref, out_ref, *, width):
    own_tile = tiles_ref[ids_ref[3]]
    own_rank = ranks_ref[own_tile, own_tile]
    for b in range(bands_ref.shape[0]):
        stack = jnp.concatenate([trail_ref[0, b], panel_ref[0]], axis=1)
        mask = keep_mask(width, ranks_ref[own_tile, bands_ref[b]], own_rank)
        out_ref[0, b] = jnp.where(mask, cross_rows(stack, stack), 0.0)


def pick_kernel(ids_ref, tiles_ref, bands_ref, *refs, inner, outer):
    t_refs, out_refs = refs[:inner], refs[inner:]
    high, low = ids_ref[0], ids_ref[1]
    for b in range(bands_ref.shape[0]):
        block = low ^ (slot_of(tiles_ref, bands_ref[b]) % inner)
        for k in range(inner):

            @pl.when(block == k)
            def _():
                for m in range(outer):
                    out_refs[m][b] = t_refs[k][high ^ m]


def merge_kernel(ids_ref, tiles_ref, bands_ref, *refs, inner, outer):
    r_refs, out_ref = refs[:outer], refs[outer]
    high = ids_ref[0]
    for b in range(bands_ref.shape[0]):
        block = high ^ (slot_of(tiles_ref, bands_ref[b]) // inner)
        for m in range(outer):

            @pl.when(block == m)
            def _():
                out_ref[b] = r_refs[m][b]


def right_kernel(ids_ref, tiles_ref, ranks_ref, bands_ref, *refs, inner, outer, width):
    part_refs = refs[:outer]
    q_refs = refs[outer : outer + inner]
    trail_ref, out_ref, stack = refs[outer + inner :]
    high, low = ids_ref[0], ids_ref[1]
    own_tile = tiles_ref[ids_ref[3]]
    own_rank = ranks_ref[own_tile, own_tile]
    sub = q_refs[0].shape[2]
    rows = lax.broadcasted_iota(jnp.int32, (width, width), 0)
    cols = lax.broadcasted_iota(jnp.int32, (width, width), 1)
    for b in range(bands_ref.shape[0]):
        band_tile = bands_ref[b]
        lanes = slice(b * width, (b + 1) * width)
        total = part_refs[0][:, lanes]
        for m in range(1, outer):
            total = total + part_refs[m][:, lanes]
        live = (rows < own_rank) & (cols < ranks_ref[band_tile, band_tile])
        live = live & (band_tile < own_tile)
        core_mat = jnp.where(live, total, 0.0).astype(jnp.bfloat16)
        for p in range(inner * outer):
            stack[p, :, :width] = trail_ref[0, b, p]
        for k in range(inner):
            for m in range(outer):
                update = lax.dot_general(
                    q_refs[k][m, b],
                    core_mat,
                    (((1,), (1,)), ((), ())),
                    preferred_element_type=jnp.float32,
                )
                stack[(low ^ k) * outer + (high ^ m), :, width:] = -update.astype(jnp.bfloat16)
        if sub % 16 == 0:
            flat = stack[...].reshape(inner * outer * sub, 2 * width)
            gram = cross_rows(flat, flat)
        else:
            gram = jnp.zeros((2 * width, 2 * width), jnp.float32)
            for p in range(inner * outer):
                gram = gram + cross_rows(stack[p], stack[p])
        mask = keep_mask(width, ranks_ref[own_tile, band_tile], width)
        out_ref[0, b] = jnp.where(mask, gram, 0.0)


def call(kernel, outs, scalars, arrays, scratch=()):
    result = pl.pallas_call(
        kernel,
        out_shape=outs,
        in_specs=[SMEM] * len(scalars) + [VMEM] * len(arrays),
        out_specs=jax.tree.map(lambda _: VMEM, outs),
        scratch_shapes=scratch,
        compiler_params=pltpu.CompilerParams(vmem_limit_bytes=SCRATCH_BYTES),
    )(*scalars, *[pltpu.with_memory_space_constraint(x, pltpu.VMEM) for x in arrays])
    return list(result) if isinstance(outs, list) else result


def shards(panel_u, panel_v, linv, trail_u, trail_v, rank_map, tile_of_slot, band_cols, *, rows, cols):
    inner = 1
    while inner * inner < rows:
        inner *= 2
    outer = rows // inner
    points, width = panel_u.shape[1], panel_u.shape[2]
    per_col = band_cols.shape[0]
    sub = points // rows
    block_rows = linv.shape[0]
    kept_rows = inner // cols * block_rows
    f32, bf16 = jnp.float32, jnp.bfloat16
    row = lax.axis_index("row").astype(jnp.int32)
    core = lax.axis_index("col").astype(jnp.int32)
    high, low = row // inner, row % inner
    ids = jnp.stack([high, low, core, row])

    def swap(x, axis, distance, count):
        return lax.ppermute(x, axis, [(i, i ^ distance) for i in range(count)])

    def low_swap(x, k):
        return swap(x, "row", k, rows)

    def high_swap(x, m):
        return swap(x, "row", m * inner, rows)

    def core_swap(x, j):
        return swap(x, "col", j, cols)

    v_blocks = [panel_v[0]] + [None] * (outer - 1)
    for m in sorted(range(1, outer), key=lambda m: (m & (m - 1), -m)):
        low_bit = m & -m
        v_blocks[m] = lax.ppermute(
            v_blocks[m ^ low_bit], "row", [(r, r ^ (low_bit * inner)) for r in range(rows)]
        )
    if inner == 4:
        half = block_rows // 2
        first, second = linv[:half], linv[half:]
        y_first, x_second = low_swap(first, 2), low_swap(second, 1)
        x_first, y_second = low_swap(first, 1), low_swap(second, 2)
        far_first = lax.ppermute(y_first, "row", [(r, r ^ 1) for r in range(rows)])
        far_second = lax.ppermute(x_second, "row", [(r, r ^ 2) for r in range(rows)])
        l_blocks = [linv, x_first, x_second, y_first, y_second, far_first, far_second]
        pieces = (1, 2, 2, 2)
    else:
        l_blocks = [linv] + [low_swap(linv, k) for k in range(1, inner)]
        pieces = (1,) * inner
    bands = [band_cols] + [core_swap(band_cols, j) for j in range(1, cols)]

    gram_left = call(
        functools.partial(left_kernel, width=width),
        jax.ShapeDtypeStruct((1, per_col, 2 * width, 2 * width), f32),
        (ids, tile_of_slot, rank_map, band_cols),
        (trail_u, panel_u),
    )

    chunks = panel_u[0].reshape(inner, outer, sub, width)
    t_blocks = [
        lax.dynamic_index_in_dim(chunks, low ^ k, 0, keepdims=False) for k in range(inner)
    ]
    t_blocks = t_blocks[:1] + [low_swap(t_blocks[k], k) for k in range(1, inner)]
    small = pltpu.VMEM((per_col, sub, width), bf16)
    sends = call(
        functools.partial(pick_kernel, inner=inner, outer=outer),
        [small] * outer,
        (ids, tile_of_slot, band_cols),
        t_blocks,
    )
    got = sends[:1] + [high_swap(sends[m], m) for m in range(1, outer)]
    piece = call(
        functools.partial(merge_kernel, inner=inner, outer=outer),
        small,
        (ids, tile_of_slot, band_cols),
        got,
    )
    bases = jnp.stack([piece] + [high_swap(piece, m) for m in range(1, outer)])
    base_blocks = [bases] + [low_swap(bases, k) for k in range(1, inner)]

    early = outer - 1
    solved_blocks = []
    for slots in (v_blocks[:early], v_blocks[early:]):
        lanes = len(slots) * width
        parts = call(
            functools.partial(solve_kernel, pieces=pieces, cols=cols),
            [pltpu.VMEM((kept_rows, lanes), f32)] * cols,
            (ids,),
            (*l_blocks, *slots),
        )
        solved = call(
            round_kernel,
            pltpu.VMEM((kept_rows, lanes), bf16),
            (),
            parts[:1] + [core_swap(parts[j], j) for j in range(1, cols)],
        )
        solved_blocks.append([solved] + [low_swap(solved, k) for k in range(1, inner)])
    cores = call(
        functools.partial(core_kernel, inner=inner, cols=cols, width=width, first=early),
        [pltpu.VMEM((outer * width, per_col * width), f32)] * cols,
        (ids, tile_of_slot, *bands),
        [block for pair in zip(*solved_blocks) for block in pair],
        [pltpu.VMEM((kept_rows, cols * per_col * width), bf16)],
    )
    core_parts = call(
        functools.partial(split_kernel, outer=outer),
        [pltpu.VMEM((width, per_col * width), f32)] * outer,
        (),
        cores[:1] + [core_swap(cores[j], j) for j in range(1, cols)],
    )
    core_parts = core_parts[:1] + [high_swap(core_parts[m], m) for m in range(1, outer)]

    gram_right = call(
        functools.partial(right_kernel, inner=inner, outer=outer, width=width),
        jax.ShapeDtypeStruct((1, per_col, 2 * width, 2 * width), f32),
        (ids, tile_of_slot, rank_map, band_cols),
        (*core_parts, *base_blocks, trail_v.reshape(1, per_col, inner * outer, sub, width)),
        [pltpu.VMEM((inner * outer, sub, 2 * width), bf16)],
    )
    return gram_left, gram_right


def solution(mesh):
    rows, cols = mesh.shape["row"], mesh.shape["col"]

    def body(*args):
        return shards(*args, rows=rows, cols=cols)

    return jax.shard_map(
        body,
        mesh=mesh,
        in_specs=(
            P("row", None, None),
            P("row", "col", None),
            P("row", "col"),
            P("row", "col", None, None),
            P("row", "col", None, None),
            P(),
            P(),
            P("col"),
        ),
        out_specs=(P("row", "col", None, None), P("row", "col", None, None)),
        check_vma=False,
    )
```

profile of v0, /device:TPU:0, one launch (start us, length us, event | category | flops | bytes accessed | tf_op | source)
XLA Modules:
  0.0 93.8 jit_solution(542675192424982136)
XLA Ops:
  0.6 1.1 %fusion = (bf16[80,1280]{1,0:T(8,128)(2,1)S(1)}, bf16[80,1280]{1,0:T(8,128)(2,1)S(1)}) fusion(bf16[160,1280]{1,0:T(8,128)(2,1)} %refs_0_.4), kind=kLoop, calls=%fused_computation.6 | loop fusion | bytes 819200 | tf_op jit(solution)/shard_map/slice | solution.py:235
  1.7 3.1 %collective-permute-start.4 = (bf16[80,1280]{1,0:T(8,128)(2,1)S(1)}, bf16[80,1280]{1,0:T(8,128)(2,1)S(1)}, u32[]{:S(2)}, u32[]{:S(2)}) collective-permute-start(bf16[80,1280]{1,0:T(8,128)(2,1)S(1)} %get-tuple-element.34), channel_id=1, source_target_pairs={{0,4},{2,6},{4,0},{6,2},{8,12},{10,14},{12,8},{14,10},{16,20},{18,... | collective-permute-start | bytes 614408 | tf_op jit(solution)/shard_map/ppermute | solution.py:216
  4.8 1.5 %collective-permute-start.2 = (bf16[80,1280]{1,0:T(8,128)(2,1)S(1)}, bf16[80,1280]{1,0:T(8,128)(2,1)S(1)}, u32[]{:S(2)}, u32[]{:S(2)}) collective-permute-start(bf16[80,1280]{1,0:T(8,128)(2,1)S(1)} %get-tuple-element.34), channel_id=1, source_target_pairs={{0,2},{2,0},{4,6},{6,4},{8,10},{10,8},{12,14},{14,12},{16,18},{18,... | collective-permute-start | bytes 614408 | tf_op jit(solution)/shard_map/ppermute | solution.py:216
  6.2 0.5 collective-permute-start.3
  6.8 2.6 %collective-permute-start.8 = (bf16[1280,128]{1,0:T(8,128)(2,1)}, bf16[1280,128]{1,0:T(8,128)(2,1)S(1)}, u32[]{:S(2)}, u32[]{:S(2)}) collective-permute-start(bf16[1280,128]{1,0:T(8,128)(2,1)} %bitcast.22), channel_id=1, source_target_pairs={{0,16},{2,18},{4,20},{6,22},{8,24},{10,26},{12,28},{14,30},{16,0},... | collective-permute-start | bytes 983048 | tf_op jit(solution)/shard_map/ppermute | solution.py:230
  9.3 1.6 %collective-permute-start.7 = (bf16[1280,128]{1,0:T(8,128)(2,1)}, bf16[1280,128]{1,0:T(8,128)(2,1)S(1)}, u32[]{:S(2)}, u32[]{:S(2)}) collective-permute-start(bf16[1280,128]{1,0:T(8,128)(2,1)} %bitcast.23), channel_id=1, source_target_pairs={{0,8},{2,10},{4,12},{6,14},{8,0},{10,2},{12,4},{14,6},{16,24},{18,... | collective-permute-start | bytes 983048 | tf_op jit(solution)/shard_map/ppermute | solution.py:230
  10.9 1.8 %collective-permute-start.1 = (bf16[80,1280]{1,0:T(8,128)(2,1)S(1)}, bf16[80,1280]{1,0:T(8,128)(2,1)S(1)}, u32[]{:S(2)}, u32[]{:S(2)}) collective-permute-start(bf16[80,1280]{1,0:T(8,128)(2,1)S(1)} %get-tuple-element.35), channel_id=1, source_target_pairs={{0,2},{2,0},{4,6},{6,4},{8,10},{10,8},{12,14},{14,12},{16,18},{18,... | collective-permute-start | bytes 614408 | tf_op jit(solution)/shard_map/ppermute | solution.py:216
  12.7 1.5 %collective-permute-start.6 = (bf16[80,1280]{1,0:T(8,128)(2,1)S(1)}, bf16[80,1280]{1,0:T(8,128)(2,1)S(1)}, u32[]{:S(2)}, u32[]{:S(2)}) collective-permute-start(bf16[80,1280]{1,0:T(8,128)(2,1)S(1)} %collective-permute-done.2.refs_2_), channel_id=1, source_target_pairs={{0,4},{2,6},{4,0},{6,2},{8,12},{10,14},{12,8},{14,10},{16,20},{18,... | collective-permute-start | bytes 614408 | tf_op jit(solution)/shard_map/ppermute | solution.py:239
  14.2 0.9 collective-permute-done.3.refs_3_
  15.1 2.0 %collective-permute-start.5 = (bf16[80,1280]{1,0:T(8,128)(2,1)S(1)}, bf16[80,1280]{1,0:T(8,128)(2,1)S(1)}, u32[]{:S(2)}, u32[]{:S(2)}) collective-permute-start(bf16[80,1280]{1,0:T(8,128)(2,1)S(1)} %collective-permute-done.3.refs_3_), channel_id=1, source_target_pairs={{0,2},{2,0},{4,6},{6,4},{8,10},{10,8},{12,14},{14,12},{16,18},{18,... | collective-permute-start | bytes 614408 | tf_op jit(solution)/shard_map/ppermute | solution.py:238
  17.3 6.3 %collective-permute-done.8.refs_9_ = bf16[1280,128]{1,0:T(8,128)(2,1)S(1)} collective-permute-done((bf16[1280,128]{1,0:T(8,128)(2,1)}, bf16[1280,128]{1,0:T(8,128)(2,1)S(1)}, u32[]{:S(2)}, u32[]{:S(2)}) %collective-permute-start.8) | collective-permute-done | bytes 327712 | tf_op jit(solution)/shard_map/ppermute | solution.py:230
  23.8 1.0 %copy-done = bf16[160,1280]{1,0:T(8,128)(2,1)S(1)} copy-done((bf16[160,1280]{1,0:T(8,128)(2,1)S(1)}, bf16[160,1280]{1,0:T(8,128)(2,1)}, u32[]{:S(2)}) %copy-start) | copy-done | bytes 409624
  24.8 1.0 %copy-done.5 = bf16[1,1280,128]{2,1,0:T(8,128)(2,1)S(1)} copy-done((bf16[1,1280,128]{2,1,0:T(8,128)(2,1)S(1)}, bf16[1,1280,128]{2,1,0:T(8,128)(2,1)}, u32[]{:S(2)}) %copy-start.5) | copy-done | bytes 327704
  25.8 2.4 %shard_map.96 = (f32[320,384]{1,0:T(8,128)S(1)}, f32[320,384]{1,0:T(8,128)}) custom-call(s32[4]{0:T(128)S(1)} %pad_add_fusion.ids_ref, bf16[160,1280]{1,0:T(8,128)(2,1)S(1)} %copy-done, bf16[80,1280]{1,0:T(8,128)(2,1)S(1)} %collective-permute-done.1.refs_1_, bf16[80,1280]{1,0:T(8,128)(2,1)S(1)} %collective-permute-done.2.refs_2_, ...), custom_call_target="tpu_custom_call" | custom-call | tf_op jit(solution)/shard_map/pallas_call | solution.py:188
  28.2 1.5 %collective-permute-start.10 = (bf16[1280,128]{1,0:T(8,128)(2,1)}, bf16[1280,128]{1,0:T(8,128)(2,1)}, u32[]{:S(2)}, u32[]{:S(2)}) collective-permute-start(bf16[1280,128]{1,0:T(8,128)(2,1)} %copy-done.6), channel_id=1, source_target_pairs={{0,8},{2,10},{4,12},{6,14},{8,0},{10,2},{12,4},{14,6},{16,24},{18,... | collective-permute-start | bytes 983048 | tf_op jit(solution)/shard_map/ppermute | solution.py:230
  29.8 1.6 %collective-permute-start.24 = (bf16[4,160,128]{2,1,0:T(8,128)(2,1)S(1)}, bf16[4,160,128]{2,1,0:T(8,128)(2,1)S(1)}, u32[]{:S(2)}, u32[]{:S(2)}) collective-permute-start(bf16[4,160,128]{2,1,0:T(8,128)(2,1)S(1)} %get-tuple-element.30), channel_id=1, source_target_pairs={{0,6},{2,4},{4,2},{6,0},{8,14},{10,12},{12,10},{14,8},{16,22},{18,... | collective-permute-start | bytes 491528 | tf_op jit(solution)/shard_map/ppermute | solution.py:216
  31.4 0.5 collective-permute-start.23
  31.9 1.5 %collective-permute-start.22 = (bf16[4,160,128]{2,1,0:T(8,128)(2,1)S(1)}, bf16[4,160,128]{2,1,0:T(8,128)(2,1)S(1)}, u32[]{:S(2)}, u32[]{:S(2)}) collective-permute-start(bf16[4,160,128]{2,1,0:T(8,128)(2,1)S(1)} %get-tuple-element.32), channel_id=1, source_target_pairs={{0,2},{2,0},{4,6},{6,4},{8,10},{10,8},{12,14},{14,12},{16,18},{18,... | collective-permute-start | bytes 491528 | tf_op jit(solution)/shard_map/ppermute | solution.py:216
  33.3 5.3 %collective-permute-done.10.refs_7_ = bf16[1280,128]{1,0:T(8,128)(2,1)} collective-permute-done((bf16[1280,128]{1,0:T(8,128)(2,1)}, bf16[1280,128]{1,0:T(8,128)(2,1)}, u32[]{:S(2)}, u32[]{:S(2)}) %collective-permute-start.10) | collective-permute-done | bytes 327712 | tf_op jit(solution)/shard_map/ppermute | solution.py:230
  38.7 1.6 %shard_map.98 = (f32[320,128]{1,0:T(8,128)S(1)}, f32[320,128]{1,0:T(8,128)S(1)}) custom-call(s32[4]{0:T(128)S(1)} %pad_add_fusion.ids_ref, bf16[160,1280]{1,0:T(8,128)(2,1)S(1)} %copy-done.1, bf16[80,1280]{1,0:T(8,128)(2,1)S(1)} %collective-permute-done.1.refs_1_, bf16[80,1280]{1,0:T(8,128)(2,1)S(1)} %collective-permute-done.2.refs_2_, ...), custom_call_target="tpu_custom_call" | custom-call | tf_op jit(solution)/shard_map/pallas_call | solution.py:188
  40.6 0.6 shard_map.102
  41.3 1.3 %collective-permute-start.25 = (bf16[2,160,128]{2,1,0:T(8,128)(2,1)S(1)}, bf16[2,160,128]{2,1,0:T(8,128)(2,1)S(1)}, u32[]{:S(2)}, u32[]{:S(2)}) collective-permute-start(bf16[2,160,128]{2,1,0:T(8,128)(2,1)S(1)} %get-tuple-element.27), channel_id=1, source_target_pairs={{0,8},{2,10},{4,12},{6,14},{8,0},{10,2},{12,4},{14,6},{16,24},{18,... | collective-permute-start | bytes 245768 | tf_op jit(solution)/shard_map/ppermute | solution.py:216
  42.6 2.4 %collective-permute-start.26 = (bf16[2,160,128]{2,1,0:T(8,128)(2,1)S(1)}, bf16[2,160,128]{2,1,0:T(8,128)(2,1)S(1)}, u32[]{:S(2)}, u32[]{:S(2)}) collective-permute-start(bf16[2,160,128]{2,1,0:T(8,128)(2,1)S(1)} %get-tuple-element.28), channel_id=1, source_target_pairs={{0,16},{2,18},{4,20},{6,22},{8,24},{10,26},{12,28},{14,30},{16,0},... | collective-permute-start | bytes 245768 | tf_op jit(solution)/shard_map/ppermute | solution.py:216
  45.1 1.6 %collective-permute-start.16 = (bf16[320,384]{1,0:T(8,128)(2,1)S(1)}, bf16[320,384]{1,0:T(8,128)(2,1)S(1)}, u32[]{:S(2)}, u32[]{:S(2)}) collective-permute-start(bf16[320,384]{1,0:T(8,128)(2,1)S(1)} %shard_map.97.refs_2_), channel_id=1, source_target_pairs={{0,6},{2,4},{4,2},{6,0},{8,14},{10,12},{12,10},{14,8},{16,22},{18,... | collective-permute-start | bytes 737288 | tf_op jit(solution)/shard_map/ppermute | solution.py:216
  46.6 1.2 %collective-permute-done.refs_1_ = s32[2]{0:T(128)S(1)} collective-permute-done((s32[2]{0:T(128)S(1)}, s32[2]{0:T(128)S(1)}, u32[]{:S(2)}, u32[]{:S(2)}) %collective-permute-start) | collective-permute-done | bytes 40 | tf_op jit(solution)/shard_map/ppermute | solution.py:216
  47.8 0.5 collective-permute-start.14
  48.3 1.5 %collective-permute-start.12 = (bf16[320,384]{1,0:T(8,128)(2,1)S(1)}, bf16[320,384]{1,0:T(8,128)(2,1)S(1)}, u32[]{:S(2)}, u32[]{:S(2)}) collective-permute-start(bf16[320,384]{1,0:T(8,128)(2,1)S(1)} %shard_map.97.refs_2_), channel_id=1, source_target_pairs={{0,2},{2,0},{4,6},{6,4},{8,10},{10,8},{12,14},{14,12},{16,18},{18,... | collective-permute-start | bytes 737288 | tf_op jit(solution)/shard_map/ppermute | solution.py:216
  49.8 0.8 collective-permute-start.27
  50.6 1.4 %collective-permute-start.17 = (bf16[320,128]{1,0:T(8,128)(2,1)S(1)}, bf16[320,128]{1,0:T(8,128)(2,1)S(1)}, u32[]{:S(2)}, u32[]{:S(2)}) collective-permute-start(bf16[320,128]{1,0:T(8,128)(2,1)S(1)} %shard_map.99.refs_3_), channel_id=1, source_target_pairs={{0,6},{2,4},{4,2},{6,0},{8,14},{10,12},{12,10},{14,8},{16,22},{18,... | collective-permute-start | bytes 245768 | tf_op jit(solution)/shard_map/ppermute | solution.py:216
  52.0 4.1 %collective-permute-done.27.refs_3_ = bf16[2,160,128]{2,1,0:T(8,128)(2,1)S(1)} collective-permute-done((bf16[2,160,128]{2,1,0:T(8,128)(2,1)S(1)}, bf16[2,160,128]{2,1,0:T(8,128)(2,1)S(1)}, u32[]{:S(2)}, u32[]{:S(2)}) %collective-permute-start.27) | collective-permute-done | bytes 81952 | tf_op jit(solution)/shard_map/ppermute | solution.py:216
  56.1 1.5 %collective-permute-start.15 = (bf16[320,128]{1,0:T(8,128)(2,1)S(1)}, bf16[320,128]{1,0:T(8,128)(2,1)S(1)}, u32[]{:S(2)}, u32[]{:S(2)}) collective-permute-start(bf16[320,128]{1,0:T(8,128)(2,1)S(1)} %shard_map.99.refs_3_), channel_id=1, source_target_pairs={{0,4},{2,6},{4,0},{6,2},{8,12},{10,14},{12,8},{14,10},{16,20},{18,... | collective-permute-start | bytes 245768 | tf_op jit(solution)/shard_map/ppermute | solution.py:216
  57.7 3.3 %collective-permute-done.17.refs_9_ = bf16[320,128]{1,0:T(8,128)(2,1)S(1)} collective-permute-done((bf16[320,128]{1,0:T(8,128)(2,1)S(1)}, bf16[320,128]{1,0:T(8,128)(2,1)S(1)}, u32[]{:S(2)}, u32[]{:S(2)}) %collective-permute-start.17) | collective-permute-done | bytes 81952 | tf_op jit(solution)/shard_map/ppermute | solution.py:216
  61.5 0.6 shard_map.103
  62.6 0.5 collective-permute-start.30
  63.1 2.3 %collective-permute-done.13.refs_5_ = bf16[320,128]{1,0:T(8,128)(2,1)S(1)} collective-permute-done((bf16[320,128]{1,0:T(8,128)(2,1)S(1)}, bf16[320,128]{1,0:T(8,128)(2,1)S(1)}, u32[]{:S(2)}, u32[]{:S(2)}) %collective-permute-start.13) | collective-permute-done | bytes 81952 | tf_op jit(solution)/shard_map/ppermute | solution.py:216
  65.9 1.1 %collective-permute-start.28 = (bf16[2,160,128]{2,1,0:T(8,128)(2,1)S(1)}, bf16[2,160,128]{2,1,0:T(8,128)(2,1)S(1)}, u32[]{:S(2)}, u32[]{:S(2)}) collective-permute-start(bf16[2,160,128]{2,1,0:T(8,128)(2,1)S(1)} %shard_map.103), channel_id=1, source_target_pairs={{0,8},{2,10},{4,12},{6,14},{8,0},{10,2},{12,4},{14,6},{16,24},{18,... | collective-permute-start | bytes 245768 | tf_op jit(solution)/shard_map/ppermute | solution.py:216
  67.0 1.3 %shard_map.100 = (f32[512,256]{1,0:T(8,128)S(1)}, f32[512,256]{1,0:T(8,128)S(1)}) custom-call(s32[4]{0:T(128)S(1)} %pad_add_fusion.ids_ref, s32[16]{0:T(128)S(1)} %copy-done.8, s32[2]{0:T(128)S(1)} %copy-done.9, s32[2]{0:T(128)S(1)} %collective-permute-done.refs_1_, bf16[320,384]{1,0:T(8,128)(2,1)S(1)} %shard_map.97.refs_2_, ...), custom_call_target="tpu_custom_call" | custom-call | tf_op jit(solution)/shard_map/pallas_call | solution.py:188
  68.4 1.4 %collective-permute-done.30 = bf16[2,160,128]{2,1,0:T(8,128)(2,1)S(1)} collective-permute-done((bf16[2,160,128]{2,1,0:T(8,128)(2,1)S(1)}, bf16[2,160,128]{2,1,0:T(8,128)(2,1)S(1)}, u32[]{:S(2)}, u32[]{:S(2)}) %collective-permute-start.30) | collective-permute-done | bytes 81952 | tf_op jit(solution)/shard_map/ppermute | solution.py:216
  69.8 2.3 %collective-permute-done.29 = bf16[2,160,128]{2,1,0:T(8,128)(2,1)S(1)} collective-permute-done((bf16[2,160,128]{2,1,0:T(8,128)(2,1)S(1)}, bf16[2,160,128]{2,1,0:T(8,128)(2,1)S(1)}, u32[]{:S(2)}, u32[]{:S(2)}) %collective-permute-start.29) | collective-permute-done | bytes 81952 | tf_op jit(solution)/shard_map/ppermute | solution.py:216
  72.1 2.1 %collective-permute-start.33 = (bf16[4,2,160,128]{3,2,1,0:T(8,128)(2,1)S(1)}, bf16[4,2,160,128]{3,2,1,0:T(8,128)(2,1)S(1)}, u32[]{:S(2)}, u32[]{:S(2)}) collective-permute-start(bf16[4,2,160,128]{3,2,1,0:T(8,128)(2,1)S(1)} %pad_maximum_fusion.refs_4_), channel_id=1, source_target_pairs={{0,6},{2,4},{4,2},{6,0},{8,14},{10,12},{12,10},{14,8},{16,22},{18,... | collective-permute-start | bytes 983048 | tf_op jit(solution)/shard_map/ppermute | solution.py:216
  74.7 1.1 %collective-permute-start.31 = (bf16[4,2,160,128]{3,2,1,0:T(8,128)(2,1)S(1)}, bf16[4,2,160,128]{3,2,1,0:T(8,128)(2,1)S(1)}, u32[]{:S(2)}, u32[]{:S(2)}) collective-permute-start(bf16[4,2,160,128]{3,2,1,0:T(8,128)(2,1)S(1)} %pad_maximum_fusion.refs_4_), channel_id=1, source_target_pairs={{0,2},{2,0},{4,6},{6,4},{8,10},{10,8},{12,14},{14,12},{16,18},{18,... | collective-permute-start | bytes 983048 | tf_op jit(solution)/shard_map/ppermute | solution.py:216
  75.9 2.1 %collective-permute-start.20 = (f32[128,256]{1,0:T(8,128)S(1)}, f32[128,256]{1,0:T(8,128)S(1)}, u32[]{:S(2)}, u32[]{:S(2)}) collective-permute-start(f32[128,256]{1,0:T(8,128)S(1)} %get-tuple-element.24), channel_id=1, source_target_pairs={{0,16},{2,18},{4,20},{6,22},{8,24},{10,26},{12,28},{14,30},{16,0},... | collective-permute-start | bytes 393224 | tf_op jit(solution)/shard_map/ppermute | solution.py:216
  78.0 5.7 %collective-permute-done.33.refs_7_ = bf16[4,2,160,128]{3,2,1,0:T(8,128)(2,1)S(1)} collective-permute-done((bf16[4,2,160,128]{3,2,1,0:T(8,128)(2,1)S(1)}, bf16[4,2,160,128]{3,2,1,0:T(8,128)(2,1)S(1)}, u32[]{:S(2)}, u32[]{:S(2)}) %collective-permute-start.33) | collective-permute-done | bytes 327712 | tf_op jit(solution)/shard_map/ppermute | solution.py:216
  83.7 1.6 %collective-permute-start.21 = (f32[128,256]{1,0:T(8,128)S(1)}, f32[128,256]{1,0:T(8,128)S(1)}, u32[]{:S(2)}, u32[]{:S(2)}) collective-permute-start(f32[128,256]{1,0:T(8,128)S(1)} %get-tuple-element.25), channel_id=1, source_target_pairs={{0,24},{2,26},{4,28},{6,30},{8,16},{10,18},{12,20},{14,22},{16,8},... | collective-permute-start | bytes 393224 | tf_op jit(solution)/shard_map/ppermute | solution.py:216
  85.3 2.4 %shard_map.95 = f32[1,2,256,256]{3,2,1,0:T(8,128)} custom-call(s32[4]{0:T(128)S(1)} %pad_add_fusion.ids_ref, s32[16]{0:T(128)S(1)} %copy-done.8, s32[16,16]{1,0:T(8,128)S(1)} %copy-done.7, s32[2]{0:T(128)S(1)} %copy-done.9, bf16[1,2,2560,128]{3,2,1,0:T(8,128)(2,1)S(1)} %copy-done.3, bf16[1,2560,128]{2,1,0:T(8,128)(2,1)S(1)} %copy-done.2), custom_call_target="tpu_custom_call" | custom-call | tf_op jit(solution)/shard_map/pallas_call | solution.py:188
  87.7 1.7 %collective-permute-done.32.refs_6_ = bf16[4,2,160,128]{3,2,1,0:T(8,128)(2,1)S(1)} collective-permute-done((bf16[4,2,160,128]{3,2,1,0:T(8,128)(2,1)S(1)}, bf16[4,2,160,128]{3,2,1,0:T(8,128)(2,1)S(1)}, u32[]{:S(2)}, u32[]{:S(2)}) %collective-permute-start.32) | collective-permute-done | bytes 327712 | tf_op jit(solution)/shard_map/ppermute | solution.py:216
  89.6 0.9 collective-permute-done.21.refs_3_
  90.5 3.3 %shard_map.104 = f32[1,2,256,256]{3,2,1,0:T(8,128)} custom-call(s32[4]{0:T(128)S(1)} %pad_add_fusion.ids_ref, s32[16]{0:T(128)S(1)} %copy-done.8, s32[16,16]{1,0:T(8,128)S(1)} %copy-done.7, s32[2]{0:T(128)S(1)} %copy-done.9, f32[128,256]{1,0:T(8,128)S(1)} %get-tuple-element.22.refs_0_, f32[128,256]{1,0:T(8,128)S(1)} %collective-permute-done.19.refs_1_, ...), custom_call_target="tpu_custom_call" | custom-call | tf_op jit(solution)/shard_map/pallas_call | solution.py:188
  (54 shorter events, 3.3 us)
Async XLA Ops:
  1.7 9.2 %collective-permute-start.4 = (bf16[80,1280]{1,0:T(8,128)(2,1)S(1)}, bf16[80,1280]{1,0:T(8,128)(2,1)S(1)}, u32[]{:S(2)}, u32[]{:S(2)}) collective-permute-start(bf16[80,1280]{1,0:T(8,128)(2,1)S(1)} %get-tuple-element.34), channel_id=1, source_target_pairs={{0,4},{2,6},{4,0},{6,2},{8,12},{10,14},{12,8},{14,10},{16,20},{18,... | collective-permute-start | bytes 614408 | tf_op jit(solution)/shard_map/ppermute | solution.py:216
  4.8 7.9 %collective-permute-start.2 = (bf16[80,1280]{1,0:T(8,128)(2,1)S(1)}, bf16[80,1280]{1,0:T(8,128)(2,1)S(1)}, u32[]{:S(2)}, u32[]{:S(2)}) collective-permute-start(bf16[80,1280]{1,0:T(8,128)(2,1)S(1)} %get-tuple-element.34), channel_id=1, source_target_pairs={{0,2},{2,0},{4,6},{6,4},{8,10},{10,8},{12,14},{14,12},{16,18},{18,... | collective-permute-start | bytes 614408 | tf_op jit(solution)/shard_map/ppermute | solution.py:216
  6.2 8.8 %collective-permute-start.3 = (bf16[80,1280]{1,0:T(8,128)(2,1)S(1)}, bf16[80,1280]{1,0:T(8,128)(2,1)S(1)}, u32[]{:S(2)}, u32[]{:S(2)}) collective-permute-start(bf16[80,1280]{1,0:T(8,128)(2,1)S(1)} %get-tuple-element.35), channel_id=1, source_target_pairs={{0,4},{2,6},{4,0},{6,2},{8,12},{10,14},{12,8},{14,10},{16,20},{18,... | collective-permute-start | bytes 614408 | tf_op jit(solution)/shard_map/ppermute | solution.py:216
  6.8 16.8 %collective-permute-start.8 = (bf16[1280,128]{1,0:T(8,128)(2,1)}, bf16[1280,128]{1,0:T(8,128)(2,1)S(1)}, u32[]{:S(2)}, u32[]{:S(2)}) collective-permute-start(bf16[1280,128]{1,0:T(8,128)(2,1)} %bitcast.22), channel_id=1, source_target_pairs={{0,16},{2,18},{4,20},{6,22},{8,24},{10,26},{12,28},{14,30},{16,0},... | collective-permute-start | bytes 983048 | tf_op jit(solution)/shard_map/ppermute | solution.py:230
  9.3 14.4 %collective-permute-start.7 = (bf16[1280,128]{1,0:T(8,128)(2,1)}, bf16[1280,128]{1,0:T(8,128)(2,1)S(1)}, u32[]{:S(2)}, u32[]{:S(2)}) collective-permute-start(bf16[1280,128]{1,0:T(8,128)(2,1)} %bitcast.23), channel_id=1, source_target_pairs={{0,8},{2,10},{4,12},{6,14},{8,0},{10,2},{12,4},{14,6},{16,24},{18,... | collective-permute-start | bytes 983048 | tf_op jit(solution)/shard_map/ppermute | solution.py:230
  10.9 6.4 %collective-permute-start.1 = (bf16[80,1280]{1,0:T(8,128)(2,1)S(1)}, bf16[80,1280]{1,0:T(8,128)(2,1)S(1)}, u32[]{:S(2)}, u32[]{:S(2)}) collective-permute-start(bf16[80,1280]{1,0:T(8,128)(2,1)S(1)} %get-tuple-element.35), channel_id=1, source_target_pairs={{0,2},{2,0},{4,6},{6,4},{8,10},{10,8},{12,14},{14,12},{16,18},{18,... | collective-permute-start | bytes 614408 | tf_op jit(solution)/shard_map/ppermute | solution.py:216
  12.7 11.1 %collective-permute-start.6 = (bf16[80,1280]{1,0:T(8,128)(2,1)S(1)}, bf16[80,1280]{1,0:T(8,128)(2,1)S(1)}, u32[]{:S(2)}, u32[]{:S(2)}) collective-permute-start(bf16[80,1280]{1,0:T(8,128)(2,1)S(1)} %collective-permute-done.2.refs_2_), channel_id=1, source_target_pairs={{0,4},{2,6},{4,0},{6,2},{8,12},{10,14},{12,8},{14,10},{16,20},{18,... | collective-permute-start | bytes 614408 | tf_op jit(solution)/shard_map/ppermute | solution.py:239
  15.1 8.7 %collective-permute-start.5 = (bf16[80,1280]{1,0:T(8,128)(2,1)S(1)}, bf16[80,1280]{1,0:T(8,128)(2,1)S(1)}, u32[]{:S(2)}, u32[]{:S(2)}) collective-permute-start(bf16[80,1280]{1,0:T(8,128)(2,1)S(1)} %collective-permute-done.3.refs_3_), channel_id=1, source_target_pairs={{0,2},{2,0},{4,6},{6,4},{8,10},{10,8},{12,14},{14,12},{16,18},{18,... | collective-permute-start | bytes 614408 | tf_op jit(solution)/shard_map/ppermute | solution.py:238
  23.6 4.6 %copy-start.6 = (bf16[1280,128]{1,0:T(8,128)(2,1)}, bf16[1280,128]{1,0:T(8,128)(2,1)S(1)}, u32[]{:S(2)}) copy-start(bf16[1280,128]{1,0:T(8,128)(2,1)S(1)} %collective-permute-done.8.refs_9_) | copy-start | bytes 983044
  23.8 1.0 %copy-start = (bf16[160,1280]{1,0:T(8,128)(2,1)S(1)}, bf16[160,1280]{1,0:T(8,128)(2,1)}, u32[]{:S(2)}) copy-start(bf16[160,1280]{1,0:T(8,128)(2,1)} %refs_0_.4) | copy-start | bytes 1228804
  24.8 1.0 %copy-start.5 = (bf16[1,1280,128]{2,1,0:T(8,128)(2,1)S(1)}, bf16[1,1280,128]{2,1,0:T(8,128)(2,1)}, u32[]{:S(2)}) copy-start(bf16[1,1280,128]{2,1,0:T(8,128)(2,1)} %param.9) | copy-start | bytes 983044
  25.8 3.9 %copy-start.2 = (bf16[1,2560,128]{2,1,0:T(8,128)(2,1)S(1)}, bf16[1,2560,128]{2,1,0:T(8,128)(2,1)}, u32[]{:S(2)}) copy-start(bf16[1,2560,128]{2,1,0:T(8,128)(2,1)} %panel_ref.1) | copy-start | bytes 1966084
  28.2 10.4 %copy-start.1 = (bf16[160,1280]{1,0:T(8,128)(2,1)S(1)}, bf16[160,1280]{1,0:T(8,128)(2,1)}, u32[]{:S(2)}) copy-start(bf16[160,1280]{1,0:T(8,128)(2,1)} %refs_0_.4) | copy-start | bytes 1228804
  28.2 16.8 %collective-permute-start.9 = (f32[320,384]{1,0:T(8,128)}, f32[320,384]{1,0:T(8,128)S(1)}, u32[]{:S(2)}, u32[]{:S(2)}) collective-permute-start(f32[320,384]{1,0:T(8,128)} %get-tuple-element.17), channel_id=1, source_target_pairs={{0,1},{1,0},{2,3},{3,2},{4,5},{5,4},{6,7},{7,6},{8,9},{9,8},{10,11... | collective-permute-start | bytes 1474568 | tf_op jit(solution)/shard_map/ppermute | solution.py:216
  28.2 10.4 %collective-permute-start.10 = (bf16[1280,128]{1,0:T(8,128)(2,1)}, bf16[1280,128]{1,0:T(8,128)(2,1)}, u32[]{:S(2)}, u32[]{:S(2)}) collective-permute-start(bf16[1280,128]{1,0:T(8,128)(2,1)} %copy-done.6), channel_id=1, source_target_pairs={{0,8},{2,10},{4,12},{6,14},{8,0},{10,2},{12,4},{14,6},{16,24},{18,... | collective-permute-start | bytes 983048 | tf_op jit(solution)/shard_map/ppermute | solution.py:230
  29.8 10.9 %copy-start.8 = (s32[16]{0:T(128)S(1)}, s32[16]{0:T(128)}, u32[]{:S(2)}) copy-start(s32[16]{0:T(128)} %tiles_ref.9) | copy-start | bytes 196
  29.8 10.9 %copy-start.9 = (s32[2]{0:T(128)S(1)}, s32[2]{0:T(128)}, u32[]{:S(2)}) copy-start(s32[2]{0:T(128)} %bands_ref.7) | copy-start | bytes 28
  29.8 10.6 %collective-permute-start.24 = (bf16[4,160,128]{2,1,0:T(8,128)(2,1)S(1)}, bf16[4,160,128]{2,1,0:T(8,128)(2,1)S(1)}, u32[]{:S(2)}, u32[]{:S(2)}) collective-permute-start(bf16[4,160,128]{2,1,0:T(8,128)(2,1)S(1)} %get-tuple-element.30), channel_id=1, source_target_pairs={{0,6},{2,4},{4,2},{6,0},{8,14},{10,12},{12,10},{14,8},{16,22},{18,... | collective-permute-start | bytes 491528 | tf_op jit(solution)/shard_map/ppermute | solution.py:216
  31.4 9.2 %collective-permute-start.23 = (bf16[4,160,128]{2,1,0:T(8,128)(2,1)S(1)}, bf16[4,160,128]{2,1,0:T(8,128)(2,1)S(1)}, u32[]{:S(2)}, u32[]{:S(2)}) collective-permute-start(bf16[4,160,128]{2,1,0:T(8,128)(2,1)S(1)} %get-tuple-element.31), channel_id=1, source_target_pairs={{0,4},{2,6},{4,0},{6,2},{8,12},{10,14},{12,8},{14,10},{16,20},{18,... | collective-permute-start | bytes 491528 | tf_op jit(solution)/shard_map/ppermute | solution.py:216
  31.9 8.8 %collective-permute-start.22 = (bf16[4,160,128]{2,1,0:T(8,128)(2,1)S(1)}, bf16[4,160,128]{2,1,0:T(8,128)(2,1)S(1)}, u32[]{:S(2)}, u32[]{:S(2)}) collective-permute-start(bf16[4,160,128]{2,1,0:T(8,128)(2,1)S(1)} %get-tuple-element.32), channel_id=1, source_target_pairs={{0,2},{2,0},{4,6},{6,4},{8,10},{10,8},{12,14},{14,12},{16,18},{18,... | collective-permute-start | bytes 491528 | tf_op jit(solution)/shard_map/ppermute | solution.py:216
  40.3 8.0 %collective-permute-start.11 = (f32[320,128]{1,0:T(8,128)S(1)}, f32[320,128]{1,0:T(8,128)S(1)}, u32[]{:S(2)}, u32[]{:S(2)}) collective-permute-start(f32[320,128]{1,0:T(8,128)S(1)} %get-tuple-element.19), channel_id=1, source_target_pairs={{0,1},{1,0},{2,3},{3,2},{4,5},{5,4},{6,7},{7,6},{8,9},{9,8},{10,11... | collective-permute-start | bytes 491528 | tf_op jit(solution)/shard_map/ppermute | solution.py:216
  41.3 8.5 %collective-permute-start.25 = (bf16[2,160,128]{2,1,0:T(8,128)(2,1)S(1)}, bf16[2,160,128]{2,1,0:T(8,128)(2,1)S(1)}, u32[]{:S(2)}, u32[]{:S(2)}) collective-permute-start(bf16[2,160,128]{2,1,0:T(8,128)(2,1)S(1)} %get-tuple-element.27), channel_id=1, source_target_pairs={{0,8},{2,10},{4,12},{6,14},{8,0},{10,2},{12,4},{14,6},{16,24},{18,... | collective-permute-start | bytes 245768 | tf_op jit(solution)/shard_map/ppermute | solution.py:216
  42.6 8.1 %collective-permute-start.26 = (bf16[2,160,128]{2,1,0:T(8,128)(2,1)S(1)}, bf16[2,160,128]{2,1,0:T(8,128)(2,1)S(1)}, u32[]{:S(2)}, u32[]{:S(2)}) collective-permute-start(bf16[2,160,128]{2,1,0:T(8,128)(2,1)S(1)} %get-tuple-element.28), channel_id=1, source_target_pairs={{0,16},{2,18},{4,20},{6,22},{8,24},{10,26},{12,28},{14,30},{16,0},... | collective-permute-start | bytes 245768 | tf_op jit(solution)/shard_map/ppermute | solution.py:216
  45.1 20.8 %collective-permute-start.16 = (bf16[320,384]{1,0:T(8,128)(2,1)S(1)}, bf16[320,384]{1,0:T(8,128)(2,1)S(1)}, u32[]{:S(2)}, u32[]{:S(2)}) collective-permute-start(bf16[320,384]{1,0:T(8,128)(2,1)S(1)} %shard_map.97.refs_2_), channel_id=1, source_target_pairs={{0,6},{2,4},{4,2},{6,0},{8,14},{10,12},{12,10},{14,8},{16,22},{18,... | collective-permute-start | bytes 737288 | tf_op jit(solution)/shard_map/ppermute | solution.py:216
  46.6 1.2 %collective-permute-start = (s32[2]{0:T(128)S(1)}, s32[2]{0:T(128)S(1)}, u32[]{:S(2)}, u32[]{:S(2)}) collective-permute-start(s32[2]{0:T(128)S(1)} %copy-done.9), channel_id=1, source_target_pairs={{0,1},{1,0},{2,3},{3,2},{4,5},{5,4},{6,7},{7,6},{8,9},{9,8},{10,11... | collective-permute-start | bytes 32 | tf_op jit(solution)/shard_map/ppermute | solution.py:216
  47.8 19.2 %collective-permute-start.14 = (bf16[320,384]{1,0:T(8,128)(2,1)S(1)}, bf16[320,384]{1,0:T(8,128)(2,1)S(1)}, u32[]{:S(2)}, u32[]{:S(2)}) collective-permute-start(bf16[320,384]{1,0:T(8,128)(2,1)S(1)} %shard_map.97.refs_2_), channel_id=1, source_target_pairs={{0,4},{2,6},{4,0},{6,2},{8,12},{10,14},{12,8},{14,10},{16,20},{18,... | collective-permute-start | bytes 737288 | tf_op jit(solution)/shard_map/ppermute | solution.py:216
  48.3 18.7 %collective-permute-start.12 = (bf16[320,384]{1,0:T(8,128)(2,1)S(1)}, bf16[320,384]{1,0:T(8,128)(2,1)S(1)}, u32[]{:S(2)}, u32[]{:S(2)}) collective-permute-start(bf16[320,384]{1,0:T(8,128)(2,1)S(1)} %shard_map.97.refs_2_), channel_id=1, source_target_pairs={{0,2},{2,0},{4,6},{6,4},{8,10},{10,8},{12,14},{14,12},{16,18},{18,... | collective-permute-start | bytes 737288 | tf_op jit(solution)/shard_map/ppermute | solution.py:216
  49.8 6.3 %collective-permute-start.27 = (bf16[2,160,128]{2,1,0:T(8,128)(2,1)S(1)}, bf16[2,160,128]{2,1,0:T(8,128)(2,1)S(1)}, u32[]{:S(2)}, u32[]{:S(2)}) collective-permute-start(bf16[2,160,128]{2,1,0:T(8,128)(2,1)S(1)} %get-tuple-element.29), channel_id=1, source_target_pairs={{0,24},{2,26},{4,28},{6,30},{8,16},{10,18},{12,20},{14,22},{16,8},... | collective-permute-start | bytes 245768 | tf_op jit(solution)/shard_map/ppermute | solution.py:216
  50.6 10.4 %collective-permute-start.17 = (bf16[320,128]{1,0:T(8,128)(2,1)S(1)}, bf16[320,128]{1,0:T(8,128)(2,1)S(1)}, u32[]{:S(2)}, u32[]{:S(2)}) collective-permute-start(bf16[320,128]{1,0:T(8,128)(2,1)S(1)} %shard_map.99.refs_3_), channel_id=1, source_target_pairs={{0,6},{2,4},{4,2},{6,0},{8,14},{10,12},{12,10},{14,8},{16,22},{18,... | collective-permute-start | bytes 245768 | tf_op jit(solution)/shard_map/ppermute | solution.py:216
  56.1 6.5 %collective-permute-start.15 = (bf16[320,128]{1,0:T(8,128)(2,1)S(1)}, bf16[320,128]{1,0:T(8,128)(2,1)S(1)}, u32[]{:S(2)}, u32[]{:S(2)}) collective-permute-start(bf16[320,128]{1,0:T(8,128)(2,1)S(1)} %shard_map.99.refs_3_), channel_id=1, source_target_pairs={{0,4},{2,6},{4,0},{6,2},{8,12},{10,14},{12,8},{14,10},{16,20},{18,... | collective-permute-start | bytes 245768 | tf_op jit(solution)/shard_map/ppermute | solution.py:216
  61.0 4.4 %collective-permute-start.13 = (bf16[320,128]{1,0:T(8,128)(2,1)S(1)}, bf16[320,128]{1,0:T(8,128)(2,1)S(1)}, u32[]{:S(2)}, u32[]{:S(2)}) collective-permute-start(bf16[320,128]{1,0:T(8,128)(2,1)S(1)} %shard_map.99.refs_3_), channel_id=1, source_target_pairs={{0,2},{2,0},{4,6},{6,4},{8,10},{10,8},{12,14},{14,12},{16,18},{18,... | collective-permute-start | bytes 245768 | tf_op jit(solution)/shard_map/ppermute | solution.py:216
  62.1 23.2 %copy-start.3 = (bf16[1,2,2560,128]{3,2,1,0:T(8,128)(2,1)S(1)}, bf16[1,2,2560,128]{3,2,1,0:T(8,128)(2,1)}, u32[]{:S(2)}) copy-start(bf16[1,2,2560,128]{3,2,1,0:T(8,128)(2,1)} %trail_ref.1) | copy-start | bytes 3932164
  62.1 23.2 %copy-start.7 = (s32[16,16]{1,0:T(8,128)S(1)}, s32[16,16]{1,0:T(8,128)}, u32[]{:S(2)}) copy-start(s32[16,16]{1,0:T(8,128)} %ranks_ref.3) | copy-start | bytes 3076
  62.6 7.2 %collective-permute-start.30 = (bf16[2,160,128]{2,1,0:T(8,128)(2,1)S(1)}, bf16[2,160,128]{2,1,0:T(8,128)(2,1)S(1)}, u32[]{:S(2)}, u32[]{:S(2)}) collective-permute-start(bf16[2,160,128]{2,1,0:T(8,128)(2,1)S(1)} %shard_map.103), channel_id=1, source_target_pairs={{0,24},{2,26},{4,28},{6,30},{8,16},{10,18},{12,20},{14,22},{16,8},... | collective-permute-start | bytes 245768 | tf_op jit(solution)/shard_map/ppermute | solution.py:216
  65.4 6.7 %collective-permute-start.29 = (bf16[2,160,128]{2,1,0:T(8,128)(2,1)S(1)}, bf16[2,160,128]{2,1,0:T(8,128)(2,1)S(1)}, u32[]{:S(2)}, u32[]{:S(2)}) collective-permute-start(bf16[2,160,128]{2,1,0:T(8,128)(2,1)S(1)} %shard_map.103), channel_id=1, source_target_pairs={{0,16},{2,18},{4,20},{6,22},{8,24},{10,26},{12,28},{14,30},{16,0},... | collective-permute-start | bytes 245768 | tf_op jit(solution)/shard_map/ppermute | solution.py:216
  65.9 6.2 %collective-permute-start.28 = (bf16[2,160,128]{2,1,0:T(8,128)(2,1)S(1)}, bf16[2,160,128]{2,1,0:T(8,128)(2,1)S(1)}, u32[]{:S(2)}, u32[]{:S(2)}) collective-permute-start(bf16[2,160,128]{2,1,0:T(8,128)(2,1)S(1)} %shard_map.103), channel_id=1, source_target_pairs={{0,8},{2,10},{4,12},{6,14},{8,0},{10,2},{12,4},{14,6},{16,24},{18,... | collective-permute-start | bytes 245768 | tf_op jit(solution)/shard_map/ppermute | solution.py:216
  68.3 7.4 %collective-permute-start.18 = (f32[512,256]{1,0:T(8,128)S(1)}, f32[512,256]{1,0:T(8,128)S(1)}, u32[]{:S(2)}, u32[]{:S(2)}) collective-permute-start(f32[512,256]{1,0:T(8,128)S(1)} %get-tuple-element.21), channel_id=1, source_target_pairs={{0,1},{1,0},{2,3},{3,2},{4,5},{5,4},{6,7},{7,6},{8,9},{9,8},{10,11... | collective-permute-start | bytes 1572872 | tf_op jit(solution)/shard_map/ppermute | solution.py:216
  72.1 11.5 %collective-permute-start.33 = (bf16[4,2,160,128]{3,2,1,0:T(8,128)(2,1)S(1)}, bf16[4,2,160,128]{3,2,1,0:T(8,128)(2,1)S(1)}, u32[]{:S(2)}, u32[]{:S(2)}) collective-permute-start(bf16[4,2,160,128]{3,2,1,0:T(8,128)(2,1)S(1)} %pad_maximum_fusion.refs_4_), channel_id=1, source_target_pairs={{0,6},{2,4},{4,2},{6,0},{8,14},{10,12},{12,10},{14,8},{16,22},{18,... | collective-permute-start | bytes 983048 | tf_op jit(solution)/shard_map/ppermute | solution.py:216
  74.2 15.2 %collective-permute-start.32 = (bf16[4,2,160,128]{3,2,1,0:T(8,128)(2,1)S(1)}, bf16[4,2,160,128]{3,2,1,0:T(8,128)(2,1)S(1)}, u32[]{:S(2)}, u32[]{:S(2)}) collective-permute-start(bf16[4,2,160,128]{3,2,1,0:T(8,128)(2,1)S(1)} %pad_maximum_fusion.refs_4_), channel_id=1, source_target_pairs={{0,4},{2,6},{4,0},{6,2},{8,12},{10,14},{12,8},{14,10},{16,20},{18,... | collective-permute-start | bytes 983048 | tf_op jit(solution)/shard_map/ppermute | solution.py:216
  74.7 14.9 %collective-permute-start.31 = (bf16[4,2,160,128]{3,2,1,0:T(8,128)(2,1)S(1)}, bf16[4,2,160,128]{3,2,1,0:T(8,128)(2,1)S(1)}, u32[]{:S(2)}, u32[]{:S(2)}) collective-permute-start(bf16[4,2,160,128]{3,2,1,0:T(8,128)(2,1)S(1)} %pad_maximum_fusion.refs_4_), channel_id=1, source_target_pairs={{0,2},{2,0},{4,6},{6,4},{8,10},{10,8},{12,14},{14,12},{16,18},{18,... | collective-permute-start | bytes 983048 | tf_op jit(solution)/shard_map/ppermute | solution.py:216
  75.8 14.7 %copy-start.4 = (bf16[1,2,2560,128]{3,2,1,0:T(8,128)(2,1)S(1)}, bf16[1,2,2560,128]{3,2,1,0:T(8,128)(2,1)}, u32[]{:S(2)}) copy-start(bf16[1,2,2560,128]{3,2,1,0:T(8,128)(2,1)} %param.12) | copy-start | bytes 3932164
  75.8 13.8 %collective-permute-start.19 = (f32[128,256]{1,0:T(8,128)S(1)}, f32[128,256]{1,0:T(8,128)S(1)}, u32[]{:S(2)}, u32[]{:S(2)}) collective-permute-start(f32[128,256]{1,0:T(8,128)S(1)} %get-tuple-element.23), channel_id=1, source_target_pairs={{0,8},{2,10},{4,12},{6,14},{8,0},{10,2},{12,4},{14,6},{16,24},{18,... | collective-permute-start | bytes 393224 | tf_op jit(solution)/shard_map/ppermute | solution.py:216
  75.9 13.7 %collective-permute-start.20 = (f32[128,256]{1,0:T(8,128)S(1)}, f32[128,256]{1,0:T(8,128)S(1)}, u32[]{:S(2)}, u32[]{:S(2)}) collective-permute-start(f32[128,256]{1,0:T(8,128)S(1)} %get-tuple-element.24), channel_id=1, source_target_pairs={{0,16},{2,18},{4,20},{6,22},{8,24},{10,26},{12,28},{14,30},{16,0},... | collective-permute-start | bytes 393224 | tf_op jit(solution)/shard_map/ppermute | solution.py:216
  83.7 6.8 %collective-permute-start.21 = (f32[128,256]{1,0:T(8,128)S(1)}, f32[128,256]{1,0:T(8,128)S(1)}, u32[]{:S(2)}, u32[]{:S(2)}) collective-permute-start(f32[128,256]{1,0:T(8,128)S(1)} %get-tuple-element.25), channel_id=1, source_target_pairs={{0,24},{2,26},{4,28},{6,30},{8,16},{10,18},{12,20},{14,22},{16,8},... | collective-permute-start | bytes 393224 | tf_op jit(solution)/shard_map/ppermute | solution.py:216
where the time goes:
time: 94 us; the launch traced here: 93.8 us
  starting transfers between devices  40.7 us (43%)
  waiting for transfers between devices  36.6 us (39%)
  Pallas kernels  12.5 us (13%)
  local copies, waits for them, and re-layouts  3.12 us (3%)
    ppermute x29, starting transfers between devices, swap(): return lax.ppermute(x, axis, [(i, i ^ distance) for i in range(count)])  31.5 us
    ppermute x29, waiting for transfers between devices, swap(): return lax.ppermute(x, axis, [(i, i ^ distance) for i in range(count)])  24.8 us
    pallas_call x10, Pallas kernels, call(): pl.pallas_call(kernel, out_shape=outs, in_specs=[SMEM] * len(scalars) + [...  12.5 us
    ppermute x3, waiting for transfers between devices, shards(): lax.ppermute(v_blocks[m ^ low_bit], 'row', [(r, r ^ low_bit * inner) for...  11.8 us
    ppermute x3, starting transfers between devices, shards(): lax.ppermute(v_blocks[m ^ low_bit], 'row', [(r, r ^ low_bit * inner) for...  5.67 us
    unnamed x20, local copies, waits for them, and re-layouts  2.02 us
    ppermute x1, starting transfers between devices, shards(): far_first = lax.ppermute(y_first, 'row', [(r, r ^ 1) for r in range(rows)])  1.99 us
  transfers between devices with their start and end apart: 34, of which 18 were waited for; matrix products, arithmetic and copies ran while one was open for 0% of the time, Pallas kernels for 7%

commit v1 on v0

--- a/solution.py
+++ b/solution.py
@@ -118,39 +118,53 @@
         out_ref[0, b] = jnp.where(mask, cross_rows(stack, stack), 0.0)
 
 
-def pick_kernel(ids_ref, tiles_ref, bands_ref, *refs, inner, outer):
-    t_refs, out_refs = refs[:inner], refs[inner:]
-    high, low = ids_ref[0], ids_ref[1]
+def pick_kernel(ids_ref, tiles_ref, *refs, inner, share):
+    bands_refs, t_refs, out_refs = refs[:share], refs[share : share + inner], refs[share + inner :]
+    for j in range(share):
+        for b in range(bands_refs[j].shape[0]):
+            block = ids_ref[1] ^ (slot_of(tiles_ref, bands_refs[j][b]) % inner)
+            for k in range(inner):
+
+                @pl.when(block == k)
+                def _():
+                    out_refs[j][b] = t_refs[k][...]
+
+
+def join_kernel(*refs):
+    size = refs[0].shape[1]
+    for j, ref in enumerate(refs[:-1]):
+        refs[-1][:, j * size : (j + 1) * size] = ref[...]
+
+
+def halves_kernel(y_ref, x_ref, first_ref, second_ref):
+    half = first_ref.shape[1]
+    first_ref[...] = y_ref[:, :half]
+    second_ref[...] = x_ref[:, half:]
+
+
+def merge_kernel(ids_ref, tiles_ref, bands_ref, kept_ref, got_ref, out_ref, *, inner, bit):
     for b in range(bands_ref.shape[0]):
-        block = low ^ (slot_of(tiles_ref, bands_ref[b]) % inner)
-        for k in range(inner):
-
-            @pl.when(block == k)
-            def _():
-                for m in range(outer):
-                    out_refs[m][b] = t_refs[k][high ^ m]
-
-
-def merge_kernel(ids_ref, tiles_ref, bands_ref, *refs, inner, outer):
-    r_refs, out_ref = refs[:outer], refs[outer]
-    high = ids_ref[0]
-    for b in range(bands_ref.shape[0]):
-        block = high ^ (slot_of(tiles_ref, bands_ref[b]) // inner)
-        for m in range(outer):
-
-            @pl.when(block == m)
-            def _():
-                out_ref[b] = r_refs[m][b]
-
-
-def right_kernel(ids_ref, tiles_ref, ranks_ref, bands_ref, *refs, inner, outer, width):
+        other = ((slot_of(tiles_ref, bands_ref[b]) // inner) ^ ids_ref[0]) & bit
+
+        @pl.when(other == 0)
+        def _():
+            out_ref[b] = kept_ref[b]
+
+        @pl.when(other != 0)
+        def _():
+            out_ref[b] = got_ref[b]
+
+
+def right_kernel(
+    ids_ref, tiles_ref, ranks_ref, bands_ref, *refs, pieces, outer, width, share
+):
     part_refs = refs[:outer]
-    q_refs = refs[outer : outer + inner]
-    trail_ref, out_ref, stack = refs[outer + inner :]
-    high, low = ids_ref[0], ids_ref[1]
+    q_refs = refs[outer : outer + sum(pieces)]
+    trail_ref, out_ref, stack = refs[outer + sum(pieces) :]
+    low, core = ids_ref[1], ids_ref[2] if share > 1 else 0
     own_tile = tiles_ref[ids_ref[3]]
     own_rank = ranks_ref[own_tile, own_tile]
-    sub = q_refs[0].shape[2]
+    quarter = stack.shape[0] // len(pieces)
     rows = lax.broadcasted_iota(jnp.int32, (width, width), 0)
     cols = lax.broadcasted_iota(jnp.int32, (width, width), 1)
     for b in range(bands_ref.shape[0]):
@@ -162,24 +176,24 @@
         live = (rows < own_rank) & (cols < ranks_ref[band_tile, band_tile])
         live = live & (band_tile < own_tile)
         core_mat = jnp.where(live, total, 0.0).astype(jnp.bfloat16)
-        for p in range(inner * outer):
-            stack[p, :, :width] = trail_ref[0, b, p]
-        for k in range(inner):
-            for m in range(outer):
+        stack[:, :width] = trail_ref[0, b]
+        at = 0
+        for k, count in enumerate(pieces):
+            blocks = max(share, count)
+            size = quarter // blocks
+            for h in range(blocks):
+                part, j = h * count // blocks, h * share // blocks
                 update = lax.dot_general(
-                    q_refs[k][m, b],
+                    q_refs[at + part][b, pl.ds((h - part * blocks // count) * size, size), :],
                     core_mat,
                     (((1,), (1,)), ((), ())),
                     preferred_element_type=jnp.float32,
                 )
-                stack[(low ^ k) * outer + (high ^ m), :, width:] = -update.astype(jnp.bfloat16)
-        if sub % 16 == 0:
-            flat = stack[...].reshape(inner * outer * sub, 2 * width)
-            gram = cross_rows(flat, flat)
-        else:
-            gram = jnp.zeros((2 * width, 2 * width), jnp.float32)
-            for p in range(inner * outer):
-                gram = gram + cross_rows(stack[p], stack[p])
+                inside = (core ^ j) * (quarter // share) + (h - j * blocks // share) * size
+                place = pl.multiple_of((low ^ k) * quarter + inside, 16)
+                stack[pl.ds(place, size), width:] = -update.astype(jnp.bfloat16)
+            at += count
+        gram = cross_rows(stack[...], stack[...])
         mask = keep_mask(width, ranks_ref[own_tile, band_tile], width)
         out_ref[0, b] = jnp.where(mask, gram, 0.0)
 
@@ -203,7 +217,6 @@
     outer = rows // inner
     points, width = panel_u.shape[1], panel_u.shape[2]
     per_col = band_cols.shape[0]
-    sub = points // rows
     block_rows = linv.shape[0]
     kept_rows = inner // cols * block_rows
     f32, bf16 = jnp.float32, jnp.bfloat16
@@ -232,13 +245,11 @@
         )
     if inner == 4:
         half = block_rows // 2
-        first, second = linv[:half], linv[half:]
-        y_first, x_second = low_swap(first, 2), low_swap(second, 1)
-        x_first, y_second = low_swap(first, 1), low_swap(second, 2)
-        far_first = lax.ppermute(y_first, "row", [(r, r ^ 1) for r in range(rows)])
-        far_second = lax.ppermute(x_second, "row", [(r, r ^ 2) for r in range(rows)])
-        l_blocks = [linv, x_first, x_second, y_first, y_second, far_first, far_second]
-        pieces = (1, 2, 2, 2)
+        x_block, y_block = low_swap(linv, 1), low_swap(linv, 2)
+        far_first = lax.ppermute(y_block[:half], "row", [(r, r ^ 1) for r in range(rows)])
+        far_second = lax.ppermute(x_block[half:], "row", [(r, r ^ 2) for r in range(rows)])
+        l_blocks = [linv, x_block, y_block, far_first, far_second]
+        pieces = (1, 1, 1, 2)
     else:
         l_blocks = [linv] + [low_swap(linv, k) for k in range(1, inner)]
         pieces = (1,) * inner
@@ -251,27 +262,49 @@
         (trail_u, panel_u),
     )
 
-    chunks = panel_u[0].reshape(inner, outer, sub, width)
+    quarter = points // inner
+    share = cols if quarter % (cols * 16) == 0 else 1
+    size = quarter // share
+    mine = core * size if share > 1 else 0
     t_blocks = [
-        lax.dynamic_index_in_dim(chunks, low ^ k, 0, keepdims=False) for k in range(inner)
+        lax.dynamic_slice_in_dim(panel_u[0], (low ^ k) * quarter + mine, size)
+        for k in range(inner)
     ]
     t_blocks = t_blocks[:1] + [low_swap(t_blocks[k], k) for k in range(1, inner)]
-    small = pltpu.VMEM((per_col, sub, width), bf16)
-    sends = call(
-        functools.partial(pick_kernel, inner=inner, outer=outer),
-        [small] * outer,
-        (ids, tile_of_slot, band_cols),
+    picked = call(
+        functools.partial(pick_kernel, inner=inner, share=share),
+        [pltpu.VMEM((per_col, size, width), bf16)] * share,
+        (ids, tile_of_slot, *bands[:share]),
         t_blocks,
     )
-    got = sends[:1] + [high_swap(sends[m], m) for m in range(1, outer)]
-    piece = call(
-        functools.partial(merge_kernel, inner=inner, outer=outer),
-        small,
-        (ids, tile_of_slot, band_cols),
-        got,
-    )
-    bases = jnp.stack([piece] + [high_swap(piece, m) for m in range(1, outer)])
-    base_blocks = [bases] + [low_swap(bases, k) for k in range(1, inner)]
+    base = picked[0]
+    if share > 1:
+        base = call(
+            join_kernel,
+            pltpu.VMEM((per_col, quarter, width), bf16),
+            (),
+            picked[:1] + [core_swap(picked[j], j) for j in range(1, share)],
+        )
+    bit = outer // 2
+    while bit:
+        base = call(
+            functools.partial(merge_kernel, inner=inner, bit=bit),
+            pltpu.VMEM((per_col, quarter, width), bf16),
+            (ids, tile_of_slot, band_cols),
+            (base, high_swap(base, bit)),
+        )
+        bit //= 2
+    base_blocks = [base] + [low_swap(base, k) for k in range(1, 3 if inner == 4 else inner)]
+    base_pieces = (1,) * inner
+    if inner == 4:
+        far = call(
+            halves_kernel,
+            [pltpu.VMEM((per_col, quarter // 2, width), bf16)] * 2,
+            (),
+            (base_blocks[2], base_blocks[1]),
+        )
+        base_blocks += [swap(far[0], "row", 1, rows), swap(far[1], "row", 2, rows)]
+        base_pieces = (1, 1, 1, 2)
 
     early = outer - 1
     solved_blocks = []
@@ -306,11 +339,11 @@
     core_parts = core_parts[:1] + [high_swap(core_parts[m], m) for m in range(1, outer)]
 
     gram_right = call(
-        functools.partial(right_kernel, inner=inner, outer=outer, width=width),
+        functools.partial(right_kernel, pieces=base_pieces, outer=outer, width=width, share=share),
         jax.ShapeDtypeStruct((1, per_col, 2 * width, 2 * width), f32),
         (ids, tile_of_slot, rank_map, band_cols),
-        (*core_parts, *base_blocks, trail_v.reshape(1, per_col, inner * outer, sub, width)),
-        [pltpu.VMEM((inner * outer, sub, 2 * width), bf16)],
+        (*core_parts, *base_blocks, trail_v),
+        [pltpu.VMEM((points, 2 * width), bf16)],
     )
     return gram_left, gram_right
 

time: 94 us -> 89.4 us (0.951)
  starting transfers between devices: 40.7 us -> 29.7 us
  waiting for transfers between devices: 36.6 us -> 45.7 us
  local copies, waits for them, and re-layouts: 3.12 us -> 1.1 us
    ppermute x29 -> x25, waiting for transfers between devices: 24.8 us -> 41.1 us  [swap(): return lax.ppermute(x, axis, [(i, i ^ distance) for i in range(count)])]
    ppermute x29 -> x25, starting transfers between devices: 31.5 us -> 21.7 us  [swap(): return lax.ppermute(x, axis, [(i, i ^ distance) for i in range(count)])]
    ppermute x3, waiting for transfers between devices: 11.8 us -> 4.58 us  [shards(): lax.ppermute(v_blocks[m ^ low_bit], 'row', [(r, r ^ low_bit * inner) for...]
    unnamed x20 -> x16, local copies, waits for them, and re-layouts: 2.02 us -> 0.04 us
    ppermute x3, starting transfers between devices: 5.67 us -> 4.6 us  [shards(): lax.ppermute(v_blocks[m ^ low_bit], 'row', [(r, r ^ low_bit * inner) for...]
    slice x1 -> x2, local copies, waits for them, and re-layouts: 1.06 us -> 0.03 us  [the longest x1 0.01 us: shards(): y_block[:half]]
    dynamic_slice x0 -> x1, local copies, waits for them, and re-layouts: none -> 1.03 us  [shards(): lax.dynamic_slice_in_dim(panel_u[0], (low ^ k) * quarter + mine, size)]
    pallas_call x10 -> x13, Pallas kernels: 12.5 us -> 11.8 us  [call(): pl.pallas_call(kernel, out_shape=outs, in_specs=[SMEM] * len(scalars) + [...]
  transfers between devices with their start and end apart: 34 -> 30, of which waited for: 18 -> 12; matrix products, arithmetic and copies ran while one was open for 0% -> 1% of each run, Pallas kernels for 7% -> 10%
where the time goes in v1:
time: 89.4 us; the launch traced here: 89.3 us
  waiting for transfers between devices  45.7 us (51%)
  starting transfers between devices  29.7 us (33%)
  Pallas kernels  11.8 us (13%)
  local copies, waits for them, and re-layouts  1.1 us (1%)
    ppermute x25, waiting for transfers between devices, swap(): return lax.ppermute(x, axis, [(i, i ^ distance) for i in range(count)])  41.1 us
    ppermute x25, starting transfers between devices, swap(): return lax.ppermute(x, axis, [(i, i ^ distance) for i in range(count)])  21.7 us
    pallas_call x13, Pallas kernels, call(): pl.pallas_call(kernel, out_shape=outs, in_specs=[SMEM] * len(scalars) + [...  11.8 us
    ppermute x3, starting transfers between devices, shards(): lax.ppermute(v_blocks[m ^ low_bit], 'row', [(r, r ^ low_bit * inner) for...  4.6 us
    ppermute x3, waiting for transfers between devices, shards(): lax.ppermute(v_blocks[m ^ low_bit], 'row', [(r, r ^ low_bit * inner) for...  4.58 us
  transfers between devices with their start and end apart: 30, of which 12 were waited for; matrix products, arithmetic and copies ran while one was open for 1% of the time, Pallas kernels for 10%

profile of v1, /device:TPU:0, one launch (start us, length us, event | category | flops | bytes accessed | tf_op | source)
XLA Modules:
  0.0 89.3 jit_solution(3631087708804663794)
XLA Ops:
  0.7 3.1 %collective-permute-start.2 = (bf16[160,1280]{1,0:T(8,128)(2,1)}, bf16[160,1280]{1,0:T(8,128)(2,1)S(1)}, u32[]{:S(2)}, u32[]{:S(2)}) collective-permute-start(bf16[160,1280]{1,0:T(8,128)(2,1)} %refs_0_.5), channel_id=1, source_target_pairs={{0,4},{2,6},{4,0},{6,2},{8,12},{10,14},{12,8},{14,10},{16,20},{18,... | collective-permute-start | bytes 1228808 | tf_op jit(solution)/shard_map/ppermute | solution.py:229
  3.7 1.5 %collective-permute-start.1 = (bf16[160,1280]{1,0:T(8,128)(2,1)}, bf16[160,1280]{1,0:T(8,128)(2,1)S(1)}, u32[]{:S(2)}, u32[]{:S(2)}) collective-permute-start(bf16[160,1280]{1,0:T(8,128)(2,1)} %refs_0_.5), channel_id=1, source_target_pairs={{0,2},{2,0},{4,6},{6,4},{8,10},{10,8},{12,14},{14,12},{16,18},{18,... | collective-permute-start | bytes 1228808 | tf_op jit(solution)/shard_map/ppermute | solution.py:229
  5.2 1.6 %collective-permute-start.5 = (bf16[1280,128]{1,0:T(8,128)(2,1)}, bf16[1280,128]{1,0:T(8,128)(2,1)S(1)}, u32[]{:S(2)}, u32[]{:S(2)}) collective-permute-start(bf16[1280,128]{1,0:T(8,128)(2,1)} %bitcast.13), channel_id=1, source_target_pairs={{0,8},{2,10},{4,12},{6,14},{8,0},{10,2},{12,4},{14,6},{16,24},{18,... | collective-permute-start | bytes 983048 | tf_op jit(solution)/shard_map/ppermute | solution.py:243
  6.8 2.6 %collective-permute-start.6 = (bf16[1280,128]{1,0:T(8,128)(2,1)}, bf16[1280,128]{1,0:T(8,128)(2,1)S(1)}, u32[]{:S(2)}, u32[]{:S(2)}) collective-permute-start(bf16[1280,128]{1,0:T(8,128)(2,1)} %bitcast.14), channel_id=1, source_target_pairs={{0,16},{2,18},{4,20},{6,22},{8,24},{10,26},{12,28},{14,30},{16,0},... | collective-permute-start | bytes 983048 | tf_op jit(solution)/shard_map/ppermute | solution.py:243
  9.4 4.0 %collective-permute-done.2.refs_2_ = bf16[160,1280]{1,0:T(8,128)(2,1)S(1)} collective-permute-done((bf16[160,1280]{1,0:T(8,128)(2,1)}, bf16[160,1280]{1,0:T(8,128)(2,1)S(1)}, u32[]{:S(2)}, u32[]{:S(2)}) %collective-permute-start.2) | collective-permute-done | bytes 409632 | tf_op jit(solution)/shard_map/ppermute | solution.py:229
  13.4 1.8 %collective-permute-start.3 = (bf16[80,1280]{1,0:T(8,128)(2,1)S(1)}, bf16[80,1280]{1,0:T(8,128)(2,1)S(1)}, u32[]{:S(2)}, u32[]{:S(2)}) collective-permute-start(bf16[80,1280]{1,0:T(8,128)(2,1)S(1)} %slice.8), channel_id=1, source_target_pairs={{0,2},{2,0},{4,6},{6,4},{8,10},{10,8},{12,14},{14,12},{16,18},{18,... | collective-permute-start | bytes 614408 | tf_op jit(solution)/shard_map/ppermute | solution.py:249
  15.2 1.6 %collective-permute-start.4 = (bf16[80,1280]{1,0:T(8,128)(2,1)S(1)}, bf16[80,1280]{1,0:T(8,128)(2,1)S(1)}, u32[]{:S(2)}, u32[]{:S(2)}) collective-permute-start(bf16[80,1280]{1,0:T(8,128)(2,1)S(1)} %slice.9), channel_id=1, source_target_pairs={{0,4},{2,6},{4,0},{6,2},{8,12},{10,14},{12,8},{14,10},{16,20},{18,... | collective-permute-start | bytes 614408 | tf_op jit(solution)/shard_map/ppermute | solution.py:250
  16.8 1.0 %dynamic-slice_bitcast_fusion = (bf16[320,128]{1,0:T(8,128)(2,1)S(1)}, bf16[320,128]{1,0:T(8,128)(2,1)S(1)}, bf16[320,128]{1,0:T(8,128)(2,1)S(1)}, bf16[320,128]{1,0:T(8,128)(2,1)S(1)}) fusion(bf16[1,2560,128]{2,1,0:T(8,128)(2,1)} %panel_ref.1, s32[]{:T(128)S(6)} %select_n.28, s32[]{:T(128)S(6)} %select_n.26, s32[]{:T(128)S(6)} %select_n.25, s32[]{:T(128)S(6)} %select_n.27), kind=kLoop, calls=%fused_computation | loop fusion | bytes 655376 | tf_op jit(solution)/shard_map/dynamic_slice | solution.py:270
  17.8 0.6 collective-permute-start.20
  18.4 0.1 pad_add_fusion.ids_ref
  18.5 2.7 %collective-permute-done.5.refs_6_ = bf16[1280,128]{1,0:T(8,128)(2,1)S(1)} collective-permute-done((bf16[1280,128]{1,0:T(8,128)(2,1)}, bf16[1280,128]{1,0:T(8,128)(2,1)S(1)}, u32[]{:S(2)}, u32[]{:S(2)}) %collective-permute-start.5) | collective-permute-done | bytes 327712 | tf_op jit(solution)/shard_map/ppermute | solution.py:243
  21.2 0.5 collective-permute-start.21
  21.7 1.9 %collective-permute-done.6.refs_7_ = bf16[1280,128]{1,0:T(8,128)(2,1)S(1)} collective-permute-done((bf16[1280,128]{1,0:T(8,128)(2,1)}, bf16[1280,128]{1,0:T(8,128)(2,1)S(1)}, u32[]{:S(2)}, u32[]{:S(2)}) %collective-permute-start.6) | collective-permute-done | bytes 327712 | tf_op jit(solution)/shard_map/ppermute | solution.py:243
  23.6 0.5 collective-permute-start.22
  24.1 0.4 collective-permute-start.8
  24.5 1.7 %shard_map.96 = (f32[320,384]{1,0:T(8,128)S(1)}, f32[320,384]{1,0:T(8,128)S(1)}) custom-call(s32[4]{0:T(128)S(1)} %pad_add_fusion.ids_ref, bf16[160,1280]{1,0:T(8,128)(2,1)S(1)} %copy-done, bf16[160,1280]{1,0:T(8,128)(2,1)S(1)} %collective-permute-done.1.refs_1_, bf16[160,1280]{1,0:T(8,128)(2,1)S(1)} %collective-permute-done.2.refs_2_, ...), custom_call_target="tpu_custom_call" | custom-call | tf_op jit(solution)/shard_map/pallas_call | solution.py:202
  26.2 0.6 collective-permute-start.7
  26.8 2.2 %collective-permute-done.22.refs_5_ = bf16[320,128]{1,0:T(8,128)(2,1)S(1)} collective-permute-done((bf16[320,128]{1,0:T(8,128)(2,1)S(1)}, bf16[320,128]{1,0:T(8,128)(2,1)S(1)}, u32[]{:S(2)}, u32[]{:S(2)}) %collective-permute-start.22) | collective-permute-done | bytes 81952 | tf_op jit(solution)/shard_map/ppermute | solution.py:229
  28.9 0.7 shard_map.102
  29.7 1.4 %collective-permute-done.23.refs_1_ = bf16[2,320,128]{2,1,0:T(8,128)(2,1)S(1)} collective-permute-done((bf16[2,320,128]{2,1,0:T(8,128)(2,1)S(1)}, bf16[2,320,128]{2,1,0:T(8,128)(2,1)S(1)}, u32[]{:S(2)}, u32[]{:S(2)}) %collective-permute-start.23) | collective-permute-done | bytes 163872 | tf_op jit(solution)/shard_map/ppermute | solution.py:229
  31.1 0.5 collective-permute-start.24
  31.7 1.2 %shard_map.98 = (f32[320,128]{1,0:T(8,128)S(1)}, f32[320,128]{1,0:T(8,128)S(1)}) custom-call(s32[4]{0:T(128)S(1)} %pad_add_fusion.ids_ref, bf16[160,1280]{1,0:T(8,128)(2,1)S(1)} %copy-done, bf16[160,1280]{1,0:T(8,128)(2,1)S(1)} %collective-permute-done.1.refs_1_, bf16[160,1280]{1,0:T(8,128)(2,1)S(1)} %collective-permute-done.2.refs_2_, ...), custom_call_target="tpu_custom_call" | custom-call | tf_op jit(solution)/shard_map/pallas_call | solution.py:202
  32.9 1.4 %collective-permute-done.9.refs_1_ = f32[320,128]{1,0:T(8,128)S(1)} collective-permute-done((f32[320,128]{1,0:T(8,128)S(1)}, f32[320,128]{1,0:T(8,128)S(1)}, u32[]{:S(2)}, u32[]{:S(2)}) %collective-permute-start.9) | collective-permute-done | bytes 163872 | tf_op jit(solution)/shard_map/ppermute | solution.py:229
  34.3 1.6 %collective-permute-start.11 = (bf16[320,128]{1,0:T(8,128)(2,1)S(1)}, bf16[320,128]{1,0:T(8,128)(2,1)S(1)}, u32[]{:S(2)}, u32[]{:S(2)}) collective-permute-start(bf16[320,128]{1,0:T(8,128)(2,1)S(1)} %shard_map.99.refs_3_), channel_id=1, source_target_pairs={{0,2},{2,0},{4,6},{6,4},{8,10},{10,8},{12,14},{14,12},{16,18},{18,... | collective-permute-start | bytes 245768 | tf_op jit(solution)/shard_map/ppermute | solution.py:229
  35.9 0.1 shard_map.97.refs_2_
  36.0 0.6 collective-permute-start.10
  36.6 1.5 %collective-permute-start.12 = (bf16[320,384]{1,0:T(8,128)(2,1)S(1)}, bf16[320,384]{1,0:T(8,128)(2,1)S(1)}, u32[]{:S(2)}, u32[]{:S(2)}) collective-permute-start(bf16[320,384]{1,0:T(8,128)(2,1)S(1)} %shard_map.97.refs_2_), channel_id=1, source_target_pairs={{0,4},{2,6},{4,0},{6,2},{8,12},{10,14},{12,8},{14,10},{16,20},{18,... | collective-permute-start | bytes 737288 | tf_op jit(solution)/shard_map/ppermute | solution.py:229
  38.1 1.4 %collective-permute-start.14 = (bf16[320,384]{1,0:T(8,128)(2,1)S(1)}, bf16[320,384]{1,0:T(8,128)(2,1)S(1)}, u32[]{:S(2)}, u32[]{:S(2)}) collective-permute-start(bf16[320,384]{1,0:T(8,128)(2,1)S(1)} %shard_map.97.refs_2_), channel_id=1, source_target_pairs={{0,6},{2,4},{4,2},{6,0},{8,14},{10,12},{12,10},{14,8},{16,22},{18,... | collective-permute-start | bytes 737288 | tf_op jit(solution)/shard_map/ppermute | solution.py:229
  39.5 9.2 %collective-permute-done.24.got_ref = bf16[2,640,128]{2,1,0:T(8,128)(2,1)S(1)} collective-permute-done((bf16[2,640,128]{2,1,0:T(8,128)(2,1)S(1)}, bf16[2,640,128]{2,1,0:T(8,128)(2,1)S(1)}, u32[]{:S(2)}, u32[]{:S(2)}) %collective-permute-start.24) | collective-permute-done | bytes 327712 | tf_op jit(solution)/shard_map/ppermute | solution.py:229
  48.8 0.5 collective-permute-start.13
  49.3 0.6 shard_map.104.kept_ref
  50.0 3.2 %collective-permute-done.13.refs_7_ = bf16[320,128]{1,0:T(8,128)(2,1)S(1)} collective-permute-done((bf16[320,128]{1,0:T(8,128)(2,1)S(1)}, bf16[320,128]{1,0:T(8,128)(2,1)S(1)}, u32[]{:S(2)}, u32[]{:S(2)}) %collective-permute-start.13) | collective-permute-done | bytes 81952 | tf_op jit(solution)/shard_map/ppermute | solution.py:229
  53.2 0.6 collective-permute-start.15
  53.8 4.7 %collective-permute-done.15.refs_9_ = bf16[320,128]{1,0:T(8,128)(2,1)S(1)} collective-permute-done((bf16[320,128]{1,0:T(8,128)(2,1)S(1)}, bf16[320,128]{1,0:T(8,128)(2,1)S(1)}, u32[]{:S(2)}, u32[]{:S(2)}) %collective-permute-start.15) | collective-permute-done | bytes 81952 | tf_op jit(solution)/shard_map/ppermute | solution.py:229
  58.6 1.3 %shard_map.100 = (f32[512,256]{1,0:T(8,128)S(1)}, f32[512,256]{1,0:T(8,128)S(1)}) custom-call(s32[4]{0:T(128)S(1)} %pad_add_fusion.ids_ref, s32[16]{0:T(128)S(1)} %copy-done.6, s32[2]{0:T(128)S(1)} %copy-done.7, s32[2]{0:T(128)S(1)} %collective-permute-done.refs_1_, bf16[320,384]{1,0:T(8,128)(2,1)S(1)} %shard_map.97.refs_2_, ...), custom_call_target="tpu_custom_call" | custom-call | tf_op jit(solution)/shard_map/pallas_call | solution.py:202
  60.0 0.6 shard_map.105.refs_4_
  60.6 0.6 collective-permute-start.26
  61.2 0.8 collective-permute-start.27
  62.1 8.7 %collective-permute-done.26.x_ref.refs_5_ = bf16[2,640,128]{2,1,0:T(8,128)(2,1)S(1)} collective-permute-done((bf16[2,640,128]{2,1,0:T(8,128)(2,1)S(1)}, bf16[2,640,128]{2,1,0:T(8,128)(2,1)S(1)}, u32[]{:S(2)}, u32[]{:S(2)}) %collective-permute-start.26) | collective-permute-done | bytes 327712 | tf_op jit(solution)/shard_map/ppermute | solution.py:229
  70.8 0.3 collective-permute-done.27.y_ref.refs_6_
  71.1 1.6 %collective-permute-start.28 = (bf16[2,320,128]{2,1,0:T(8,128)(2,1)S(1)}, bf16[2,320,128]{2,1,0:T(8,128)(2,1)S(1)}, u32[]{:S(2)}, u32[]{:S(2)}) collective-permute-start(bf16[2,320,128]{2,1,0:T(8,128)(2,1)S(1)} %get-tuple-element.28), channel_id=1, source_target_pairs={{0,2},{2,0},{4,6},{6,4},{8,10},{10,8},{12,14},{14,12},{16,18},{18,... | collective-permute-start | bytes 491528 | tf_op jit(solution)/shard_map/ppermute | solution.py:229
  72.7 0.5 collective-permute-start.29
  73.3 1.6 %collective-permute-start.17 = (f32[128,256]{1,0:T(8,128)S(1)}, f32[128,256]{1,0:T(8,128)S(1)}, u32[]{:S(2)}, u32[]{:S(2)}) collective-permute-start(f32[128,256]{1,0:T(8,128)S(1)} %get-tuple-element.23), channel_id=1, source_target_pairs={{0,8},{2,10},{4,12},{6,14},{8,0},{10,2},{12,4},{14,6},{16,24},{18,... | collective-permute-start | bytes 393224 | tf_op jit(solution)/shard_map/ppermute | solution.py:229
  74.8 1.5 %collective-permute-start.18 = (f32[128,256]{1,0:T(8,128)S(1)}, f32[128,256]{1,0:T(8,128)S(1)}, u32[]{:S(2)}, u32[]{:S(2)}) collective-permute-start(f32[128,256]{1,0:T(8,128)S(1)} %get-tuple-element.24), channel_id=1, source_target_pairs={{0,16},{2,18},{4,20},{6,22},{8,24},{10,26},{12,28},{14,30},{16,0},... | collective-permute-start | bytes 393224 | tf_op jit(solution)/shard_map/ppermute | solution.py:229
  76.3 1.4 %collective-permute-start.19 = (f32[128,256]{1,0:T(8,128)S(1)}, f32[128,256]{1,0:T(8,128)S(1)}, u32[]{:S(2)}, u32[]{:S(2)}) collective-permute-start(f32[128,256]{1,0:T(8,128)S(1)} %get-tuple-element.25), channel_id=1, source_target_pairs={{0,24},{2,26},{4,28},{6,30},{8,16},{10,18},{12,20},{14,22},{16,8},... | collective-permute-start | bytes 393224 | tf_op jit(solution)/shard_map/ppermute | solution.py:229
  77.7 2.4 %shard_map.95 = f32[1,2,256,256]{3,2,1,0:T(8,128)} custom-call(s32[4]{0:T(128)S(1)} %pad_add_fusion.ids_ref, s32[16]{0:T(128)S(1)} %copy-done.6, s32[16,16]{1,0:T(8,128)S(1)} %copy-done.5, s32[2]{0:T(128)S(1)} %copy-done.7, bf16[1,2,2560,128]{3,2,1,0:T(8,128)(2,1)S(1)} %copy-done.2, bf16[1,2560,128]{2,1,0:T(8,128)(2,1)S(1)} %copy-done.1), custom_call_target="tpu_custom_call" | custom-call | tf_op jit(solution)/shard_map/pallas_call | solution.py:202
  80.1 6.0 %collective-permute-done.18.refs_2_ = f32[128,256]{1,0:T(8,128)S(1)} collective-permute-done((f32[128,256]{1,0:T(8,128)S(1)}, f32[128,256]{1,0:T(8,128)S(1)}, u32[]{:S(2)}, u32[]{:S(2)}) %collective-permute-start.18) | collective-permute-done | bytes 131104 | tf_op jit(solution)/shard_map/ppermute | solution.py:229
  86.2 3.1 %shard_map.107 = f32[1,2,256,256]{3,2,1,0:T(8,128)} custom-call(s32[4]{0:T(128)S(1)} %pad_add_fusion.ids_ref, s32[16]{0:T(128)S(1)} %copy-done.6, s32[16,16]{1,0:T(8,128)S(1)} %copy-done.5, s32[2]{0:T(128)S(1)} %copy-done.7, f32[128,256]{1,0:T(8,128)S(1)} %get-tuple-element.22.refs_0_, f32[128,256]{1,0:T(8,128)S(1)} %collective-permute-done.17.refs_1_, ...), custom_call_target="tpu_custom_call" | custom-call | tf_op jit(solution)/shard_map/pallas_call | solution.py:202
  (45 shorter events, 0.5 us)
Async XLA Ops:
  0.6 23.9 %copy-start = (bf16[160,1280]{1,0:T(8,128)(2,1)S(1)}, bf16[160,1280]{1,0:T(8,128)(2,1)}, u32[]{:S(2)}) copy-start(bf16[160,1280]{1,0:T(8,128)(2,1)} %refs_0_.5) | copy-start | bytes 1228804
  0.6 23.9 %copy-start.4 = (bf16[1,1280,128]{2,1,0:T(8,128)(2,1)S(1)}, bf16[1,1280,128]{2,1,0:T(8,128)(2,1)}, u32[]{:S(2)}) copy-start(bf16[1,1280,128]{2,1,0:T(8,128)(2,1)} %param.9) | copy-start | bytes 983044
  0.7 23.9 %copy-start.7 = (s32[2]{0:T(128)S(1)}, s32[2]{0:T(128)}, u32[]{:S(2)}) copy-start(s32[2]{0:T(128)} %bands_ref.7) | copy-start | bytes 28
  0.7 12.7 %collective-permute-start.2 = (bf16[160,1280]{1,0:T(8,128)(2,1)}, bf16[160,1280]{1,0:T(8,128)(2,1)S(1)}, u32[]{:S(2)}, u32[]{:S(2)}) collective-permute-start(bf16[160,1280]{1,0:T(8,128)(2,1)} %refs_0_.5), channel_id=1, source_target_pairs={{0,4},{2,6},{4,0},{6,2},{8,12},{10,14},{12,8},{14,10},{16,20},{18,... | collective-permute-start | bytes 1228808 | tf_op jit(solution)/shard_map/ppermute | solution.py:229
  3.7 11.5 %collective-permute-start.1 = (bf16[160,1280]{1,0:T(8,128)(2,1)}, bf16[160,1280]{1,0:T(8,128)(2,1)S(1)}, u32[]{:S(2)}, u32[]{:S(2)}) collective-permute-start(bf16[160,1280]{1,0:T(8,128)(2,1)} %refs_0_.5), channel_id=1, source_target_pairs={{0,2},{2,0},{4,6},{6,4},{8,10},{10,8},{12,14},{14,12},{16,18},{18,... | collective-permute-start | bytes 1228808 | tf_op jit(solution)/shard_map/ppermute | solution.py:229
  5.2 16.0 %collective-permute-start.5 = (bf16[1280,128]{1,0:T(8,128)(2,1)}, bf16[1280,128]{1,0:T(8,128)(2,1)S(1)}, u32[]{:S(2)}, u32[]{:S(2)}) collective-permute-start(bf16[1280,128]{1,0:T(8,128)(2,1)} %bitcast.13), channel_id=1, source_target_pairs={{0,8},{2,10},{4,12},{6,14},{8,0},{10,2},{12,4},{14,6},{16,24},{18,... | collective-permute-start | bytes 983048 | tf_op jit(solution)/shard_map/ppermute | solution.py:243
  6.8 16.8 %collective-permute-start.6 = (bf16[1280,128]{1,0:T(8,128)(2,1)}, bf16[1280,128]{1,0:T(8,128)(2,1)S(1)}, u32[]{:S(2)}, u32[]{:S(2)}) collective-permute-start(bf16[1280,128]{1,0:T(8,128)(2,1)} %bitcast.14), channel_id=1, source_target_pairs={{0,16},{2,18},{4,20},{6,22},{8,24},{10,26},{12,28},{14,30},{16,0},... | collective-permute-start | bytes 983048 | tf_op jit(solution)/shard_map/ppermute | solution.py:243
  13.4 10.7 %collective-permute-start.3 = (bf16[80,1280]{1,0:T(8,128)(2,1)S(1)}, bf16[80,1280]{1,0:T(8,128)(2,1)S(1)}, u32[]{:S(2)}, u32[]{:S(2)}) collective-permute-start(bf16[80,1280]{1,0:T(8,128)(2,1)S(1)} %slice.8), channel_id=1, source_target_pairs={{0,2},{2,0},{4,6},{6,4},{8,10},{10,8},{12,14},{14,12},{16,18},{18,... | collective-permute-start | bytes 614408 | tf_op jit(solution)/shard_map/ppermute | solution.py:249
  15.2 9.3 %collective-permute-start.4 = (bf16[80,1280]{1,0:T(8,128)(2,1)S(1)}, bf16[80,1280]{1,0:T(8,128)(2,1)S(1)}, u32[]{:S(2)}, u32[]{:S(2)}) collective-permute-start(bf16[80,1280]{1,0:T(8,128)(2,1)S(1)} %slice.9), channel_id=1, source_target_pairs={{0,4},{2,6},{4,0},{6,2},{8,12},{10,14},{12,8},{14,10},{16,20},{18,... | collective-permute-start | bytes 614408 | tf_op jit(solution)/shard_map/ppermute | solution.py:250
  17.8 9.0 %collective-permute-start.20 = (bf16[320,128]{1,0:T(8,128)(2,1)S(1)}, bf16[320,128]{1,0:T(8,128)(2,1)S(1)}, u32[]{:S(2)}, u32[]{:S(2)}) collective-permute-start(bf16[320,128]{1,0:T(8,128)(2,1)S(1)} %get-tuple-element.31), channel_id=1, source_target_pairs={{0,2},{2,0},{4,6},{6,4},{8,10},{10,8},{12,14},{14,12},{16,18},{18,... | collective-permute-start | bytes 245768 | tf_op jit(solution)/shard_map/ppermute | solution.py:229
  21.2 5.6 %collective-permute-start.21 = (bf16[320,128]{1,0:T(8,128)(2,1)S(1)}, bf16[320,128]{1,0:T(8,128)(2,1)S(1)}, u32[]{:S(2)}, u32[]{:S(2)}) collective-permute-start(bf16[320,128]{1,0:T(8,128)(2,1)S(1)} %get-tuple-element.33), channel_id=1, source_target_pairs={{0,4},{2,6},{4,0},{6,2},{8,12},{10,14},{12,8},{14,10},{16,20},{18,... | collective-permute-start | bytes 245768 | tf_op jit(solution)/shard_map/ppermute | solution.py:229
  23.6 5.3 %copy-start.6 = (s32[16]{0:T(128)S(1)}, s32[16]{0:T(128)}, u32[]{:S(2)}) copy-start(s32[16]{0:T(128)} %tiles_ref.11) | copy-start | bytes 196
  23.6 5.3 %collective-permute-start.22 = (bf16[320,128]{1,0:T(8,128)(2,1)S(1)}, bf16[320,128]{1,0:T(8,128)(2,1)S(1)}, u32[]{:S(2)}, u32[]{:S(2)}) collective-permute-start(bf16[320,128]{1,0:T(8,128)(2,1)S(1)} %get-tuple-element.30), channel_id=1, source_target_pairs={{0,6},{2,4},{4,2},{6,0},{8,14},{10,12},{12,10},{14,8},{16,22},{18,... | collective-permute-start | bytes 245768 | tf_op jit(solution)/shard_map/ppermute | solution.py:229
  24.1 7.6 %collective-permute-start.8 = (bf16[1280,128]{1,0:T(8,128)(2,1)S(1)}, bf16[1280,128]{1,0:T(8,128)(2,1)S(1)}, u32[]{:S(2)}, u32[]{:S(2)}) collective-permute-start(bf16[1280,128]{1,0:T(8,128)(2,1)S(1)} %collective-permute-done.6.refs_7_), channel_id=1, source_target_pairs={{0,8},{2,10},{4,12},{6,14},{8,0},{10,2},{12,4},{14,6},{16,24},{18,... | collective-permute-start | bytes 983048 | tf_op jit(solution)/shard_map/ppermute | solution.py:243
  24.5 1.7 %collective-permute-start = (s32[2]{0:T(128)S(1)}, s32[2]{0:T(128)S(1)}, u32[]{:S(2)}, u32[]{:S(2)}) collective-permute-start(s32[2]{0:T(128)S(1)} %copy-done.7), channel_id=1, source_target_pairs={{0,1},{1,0},{2,3},{3,2},{4,5},{5,4},{6,7},{7,6},{8,9},{9,8},{10,11... | collective-permute-start | bytes 32 | tf_op jit(solution)/shard_map/ppermute | solution.py:229
  26.2 9.7 %collective-permute-start.7 = (f32[320,384]{1,0:T(8,128)S(1)}, f32[320,384]{1,0:T(8,128)S(1)}, u32[]{:S(2)}, u32[]{:S(2)}) collective-permute-start(f32[320,384]{1,0:T(8,128)S(1)} %get-tuple-element.17), channel_id=1, source_target_pairs={{0,1},{1,0},{2,3},{3,2},{4,5},{5,4},{6,7},{7,6},{8,9},{9,8},{10,11... | collective-permute-start | bytes 1474568 | tf_op jit(solution)/shard_map/ppermute | solution.py:229
  29.7 1.5 %collective-permute-start.23 = (bf16[2,320,128]{2,1,0:T(8,128)(2,1)S(1)}, bf16[2,320,128]{2,1,0:T(8,128)(2,1)S(1)}, u32[]{:S(2)}, u32[]{:S(2)}) collective-permute-start(bf16[2,320,128]{2,1,0:T(8,128)(2,1)S(1)} %get-tuple-element.27), channel_id=1, source_target_pairs={{0,1},{1,0},{2,3},{3,2},{4,5},{5,4},{6,7},{7,6},{8,9},{9,8},{10,11... | collective-permute-start | bytes 491528 | tf_op jit(solution)/shard_map/ppermute | solution.py:229
  31.1 17.6 %collective-permute-start.24 = (bf16[2,640,128]{2,1,0:T(8,128)(2,1)S(1)}, bf16[2,640,128]{2,1,0:T(8,128)(2,1)S(1)}, u32[]{:S(2)}, u32[]{:S(2)}) collective-permute-start(bf16[2,640,128]{2,1,0:T(8,128)(2,1)S(1)} %shard_map.103.kept_ref), channel_id=1, source_target_pairs={{0,16},{2,18},{4,20},{6,22},{8,24},{10,26},{12,28},{14,30},{16,0},... | collective-permute-start | bytes 983048 | tf_op jit(solution)/shard_map/ppermute | solution.py:229
  32.9 1.5 %collective-permute-start.9 = (f32[320,128]{1,0:T(8,128)S(1)}, f32[320,128]{1,0:T(8,128)S(1)}, u32[]{:S(2)}, u32[]{:S(2)}) collective-permute-start(f32[320,128]{1,0:T(8,128)S(1)} %get-tuple-element.19), channel_id=1, source_target_pairs={{0,1},{1,0},{2,3},{3,2},{4,5},{5,4},{6,7},{7,6},{8,9},{9,8},{10,11... | collective-permute-start | bytes 491528 | tf_op jit(solution)/shard_map/ppermute | solution.py:229
  34.3 15.6 %collective-permute-start.11 = (bf16[320,128]{1,0:T(8,128)(2,1)S(1)}, bf16[320,128]{1,0:T(8,128)(2,1)S(1)}, u32[]{:S(2)}, u32[]{:S(2)}) collective-permute-start(bf16[320,128]{1,0:T(8,128)(2,1)S(1)} %shard_map.99.refs_3_), channel_id=1, source_target_pairs={{0,2},{2,0},{4,6},{6,4},{8,10},{10,8},{12,14},{14,12},{16,18},{18,... | collective-permute-start | bytes 245768 | tf_op jit(solution)/shard_map/ppermute | solution.py:229
  36.0 22.6 %collective-permute-start.10 = (bf16[320,384]{1,0:T(8,128)(2,1)S(1)}, bf16[320,384]{1,0:T(8,128)(2,1)S(1)}, u32[]{:S(2)}, u32[]{:S(2)}) collective-permute-start(bf16[320,384]{1,0:T(8,128)(2,1)S(1)} %shard_map.97.refs_2_), channel_id=1, source_target_pairs={{0,2},{2,0},{4,6},{6,4},{8,10},{10,8},{12,14},{14,12},{16,18},{18,... | collective-permute-start | bytes 737288 | tf_op jit(solution)/shard_map/ppermute | solution.py:229
  36.6 22.0 %collective-permute-start.12 = (bf16[320,384]{1,0:T(8,128)(2,1)S(1)}, bf16[320,384]{1,0:T(8,128)(2,1)S(1)}, u32[]{:S(2)}, u32[]{:S(2)}) collective-permute-start(bf16[320,384]{1,0:T(8,128)(2,1)S(1)} %shard_map.97.refs_2_), channel_id=1, source_target_pairs={{0,4},{2,6},{4,0},{6,2},{8,12},{10,14},{12,8},{14,10},{16,20},{18,... | collective-permute-start | bytes 737288 | tf_op jit(solution)/shard_map/ppermute | solution.py:229
  38.1 20.5 %collective-permute-start.14 = (bf16[320,384]{1,0:T(8,128)(2,1)S(1)}, bf16[320,384]{1,0:T(8,128)(2,1)S(1)}, u32[]{:S(2)}, u32[]{:S(2)}) collective-permute-start(bf16[320,384]{1,0:T(8,128)(2,1)S(1)} %shard_map.97.refs_2_), channel_id=1, source_target_pairs={{0,6},{2,4},{4,2},{6,0},{8,14},{10,12},{12,10},{14,8},{16,22},{18,... | collective-permute-start | bytes 737288 | tf_op jit(solution)/shard_map/ppermute | solution.py:229
  48.8 4.4 %collective-permute-start.13 = (bf16[320,128]{1,0:T(8,128)(2,1)S(1)}, bf16[320,128]{1,0:T(8,128)(2,1)S(1)}, u32[]{:S(2)}, u32[]{:S(2)}) collective-permute-start(bf16[320,128]{1,0:T(8,128)(2,1)S(1)} %shard_map.99.refs_3_), channel_id=1, source_target_pairs={{0,4},{2,6},{4,0},{6,2},{8,12},{10,14},{12,8},{14,10},{16,20},{18,... | collective-permute-start | bytes 245768 | tf_op jit(solution)/shard_map/ppermute | solution.py:229
  49.9 10.1 %collective-permute-start.25 = (bf16[2,640,128]{2,1,0:T(8,128)(2,1)S(1)}, bf16[2,640,128]{2,1,0:T(8,128)(2,1)S(1)}, u32[]{:S(2)}, u32[]{:S(2)}) collective-permute-start(bf16[2,640,128]{2,1,0:T(8,128)(2,1)S(1)} %shard_map.104.kept_ref), channel_id=1, source_target_pairs={{0,8},{2,10},{4,12},{6,14},{8,0},{10,2},{12,4},{14,6},{16,24},{18,... | collective-permute-start | bytes 983048 | tf_op jit(solution)/shard_map/ppermute | solution.py:229
  53.2 5.3 %collective-permute-start.15 = (bf16[320,128]{1,0:T(8,128)(2,1)S(1)}, bf16[320,128]{1,0:T(8,128)(2,1)S(1)}, u32[]{:S(2)}, u32[]{:S(2)}) collective-permute-start(bf16[320,128]{1,0:T(8,128)(2,1)S(1)} %shard_map.99.refs_3_), channel_id=1, source_target_pairs={{0,6},{2,4},{4,2},{6,0},{8,14},{10,12},{12,10},{14,8},{16,22},{18,... | collective-permute-start | bytes 245768 | tf_op jit(solution)/shard_map/ppermute | solution.py:229
  59.9 17.8 %copy-start.1 = (bf16[1,2560,128]{2,1,0:T(8,128)(2,1)S(1)}, bf16[1,2560,128]{2,1,0:T(8,128)(2,1)}, u32[]{:S(2)}) copy-start(bf16[1,2560,128]{2,1,0:T(8,128)(2,1)} %panel_ref.1) | copy-start | bytes 1966084
  59.9 17.8 %copy-start.2 = (bf16[1,2,2560,128]{3,2,1,0:T(8,128)(2,1)S(1)}, bf16[1,2,2560,128]{3,2,1,0:T(8,128)(2,1)}, u32[]{:S(2)}) copy-start(bf16[1,2,2560,128]{3,2,1,0:T(8,128)(2,1)} %trail_ref.1) | copy-start | bytes 3932164
  59.9 17.8 %copy-start.5 = (s32[16,16]{1,0:T(8,128)S(1)}, s32[16,16]{1,0:T(8,128)}, u32[]{:S(2)}) copy-start(s32[16,16]{1,0:T(8,128)} %ranks_ref.3) | copy-start | bytes 3076
  59.9 13.3 %collective-permute-start.16 = (f32[512,256]{1,0:T(8,128)S(1)}, f32[512,256]{1,0:T(8,128)S(1)}, u32[]{:S(2)}, u32[]{:S(2)}) collective-permute-start(f32[512,256]{1,0:T(8,128)S(1)} %get-tuple-element.21), channel_id=1, source_target_pairs={{0,1},{1,0},{2,3},{3,2},{4,5},{5,4},{6,7},{7,6},{8,9},{9,8},{10,11... | collective-permute-start | bytes 1572872 | tf_op jit(solution)/shard_map/ppermute | solution.py:229
  60.6 10.2 %collective-permute-start.26 = (bf16[2,640,128]{2,1,0:T(8,128)(2,1)S(1)}, bf16[2,640,128]{2,1,0:T(8,128)(2,1)S(1)}, u32[]{:S(2)}, u32[]{:S(2)}) collective-permute-start(bf16[2,640,128]{2,1,0:T(8,128)(2,1)S(1)} %shard_map.105.refs_4_), channel_id=1, source_target_pairs={{0,2},{2,0},{4,6},{6,4},{8,10},{10,8},{12,14},{14,12},{16,18},{18,... | collective-permute-start | bytes 983048 | tf_op jit(solution)/shard_map/ppermute | solution.py:229
  61.2 9.8 %collective-permute-start.27 = (bf16[2,640,128]{2,1,0:T(8,128)(2,1)S(1)}, bf16[2,640,128]{2,1,0:T(8,128)(2,1)S(1)}, u32[]{:S(2)}, u32[]{:S(2)}) collective-permute-start(bf16[2,640,128]{2,1,0:T(8,128)(2,1)S(1)} %shard_map.105.refs_4_), channel_id=1, source_target_pairs={{0,4},{2,6},{4,0},{6,2},{8,12},{10,14},{12,8},{14,10},{16,20},{18,... | collective-permute-start | bytes 983048 | tf_op jit(solution)/shard_map/ppermute | solution.py:229
  71.1 9.0 %collective-permute-start.28 = (bf16[2,320,128]{2,1,0:T(8,128)(2,1)S(1)}, bf16[2,320,128]{2,1,0:T(8,128)(2,1)S(1)}, u32[]{:S(2)}, u32[]{:S(2)}) collective-permute-start(bf16[2,320,128]{2,1,0:T(8,128)(2,1)S(1)} %get-tuple-element.28), channel_id=1, source_target_pairs={{0,2},{2,0},{4,6},{6,4},{8,10},{10,8},{12,14},{14,12},{16,18},{18,... | collective-permute-start | bytes 491528 | tf_op jit(solution)/shard_map/ppermute | solution.py:229
  72.7 7.5 %collective-permute-start.29 = (bf16[2,320,128]{2,1,0:T(8,128)(2,1)S(1)}, bf16[2,320,128]{2,1,0:T(8,128)(2,1)S(1)}, u32[]{:S(2)}, u32[]{:S(2)}) collective-permute-start(bf16[2,320,128]{2,1,0:T(8,128)(2,1)S(1)} %get-tuple-element.29), channel_id=1, source_target_pairs={{0,4},{2,6},{4,0},{6,2},{8,12},{10,14},{12,8},{14,10},{16,20},{18,... | collective-permute-start | bytes 491528 | tf_op jit(solution)/shard_map/ppermute | solution.py:229
  73.3 12.9 %copy-start.3 = (bf16[1,2,2560,128]{3,2,1,0:T(8,128)(2,1)S(1)}, bf16[1,2,2560,128]{3,2,1,0:T(8,128)(2,1)}, u32[]{:S(2)}) copy-start(bf16[1,2,2560,128]{3,2,1,0:T(8,128)(2,1)} %refs_9_.1) | copy-start | bytes 3932164
  73.3 6.8 %collective-permute-start.17 = (f32[128,256]{1,0:T(8,128)S(1)}, f32[128,256]{1,0:T(8,128)S(1)}, u32[]{:S(2)}, u32[]{:S(2)}) collective-permute-start(f32[128,256]{1,0:T(8,128)S(1)} %get-tuple-element.23), channel_id=1, source_target_pairs={{0,8},{2,10},{4,12},{6,14},{8,0},{10,2},{12,4},{14,6},{16,24},{18,... | collective-permute-start | bytes 393224 | tf_op jit(solution)/shard_map/ppermute | solution.py:229
  74.8 11.3 %collective-permute-start.18 = (f32[128,256]{1,0:T(8,128)S(1)}, f32[128,256]{1,0:T(8,128)S(1)}, u32[]{:S(2)}, u32[]{:S(2)}) collective-permute-start(f32[128,256]{1,0:T(8,128)S(1)} %get-tuple-element.24), channel_id=1, source_target_pairs={{0,16},{2,18},{4,20},{6,22},{8,24},{10,26},{12,28},{14,30},{16,0},... | collective-permute-start | bytes 393224 | tf_op jit(solution)/shard_map/ppermute | solution.py:229
  76.3 9.8 %collective-permute-start.19 = (f32[128,256]{1,0:T(8,128)S(1)}, f32[128,256]{1,0:T(8,128)S(1)}, u32[]{:S(2)}, u32[]{:S(2)}) collective-permute-start(f32[128,256]{1,0:T(8,128)S(1)} %get-tuple-element.25), channel_id=1, source_target_pairs={{0,24},{2,26},{4,28},{6,30},{8,16},{10,18},{12,20},{14,22},{16,8},... | collective-permute-start | bytes 393224 | tf_op jit(solution)/shard_map/ppermute | solution.py:229

commit v2 on v1

--- a/solution.py
+++ b/solution.py
@@ -109,13 +109,18 @@
     refs[-1][...] = total.astype(refs[-1].dtype)
 
 
-def left_kernel(ids_ref, tiles_ref, ranks_ref, bands_ref, trail_ref, panel_ref, out_ref, *, width):
+def left_kernel(
+    ids_ref, tiles_ref, ranks_ref, bands_ref, trail_ref, panel_ref, right_ref, out_ref, kept_ref, *, width
+):
     own_tile = tiles_ref[ids_ref[3]]
     own_rank = ranks_ref[own_tile, own_tile]
     for b in range(bands_ref.shape[0]):
         stack = jnp.concatenate([trail_ref[0, b], panel_ref[0]], axis=1)
         mask = keep_mask(width, ranks_ref[own_tile, bands_ref[b]], own_rank)
         out_ref[0, b] = jnp.where(mask, cross_rows(stack, stack), 0.0)
+        kept_ref[b] = jnp.where(
+            mask[:width, :width], cross_rows(right_ref[0, b], right_ref[0, b]), 0.0
+        )
 
 
 def pick_kernel(ids_ref, tiles_ref, *refs, inner, share):
@@ -136,10 +141,18 @@
         refs[-1][:, j * size : (j + 1) * size] = ref[...]
 
 
-def halves_kernel(y_ref, x_ref, first_ref, second_ref):
-    half = first_ref.shape[1]
-    first_ref[...] = y_ref[:, :half]
-    second_ref[...] = x_ref[:, half:]
+def sort_kernel(ids_ref, own_ref, other_ref, kept_ref, sent_ref):
+    same = (ids_ref[2] ^ ids_ref[4]) == 0
+
+    @pl.when(same)
+    def _():
+        kept_ref[...] = own_ref[...]
+        sent_ref[...] = other_ref[...]
+
+    @pl.when(jnp.logical_not(same))
+    def _():
+        kept_ref[...] = other_ref[...]
+        sent_ref[...] = own_ref[...]
 
 
 def merge_kernel(ids_ref, tiles_ref, bands_ref, kept_ref, got_ref, out_ref, *, inner, bit):
@@ -160,8 +173,8 @@
 ):
     part_refs = refs[:outer]
     q_refs = refs[outer : outer + sum(pieces)]
-    trail_ref, out_ref, stack = refs[outer + sum(pieces) :]
-    low, core = ids_ref[1], ids_ref[2] if share > 1 else 0
+    kept_ref, trail_ref, out_ref, stack = refs[outer + sum(pieces) :]
+    low, flip = ids_ref[1], ids_ref[4] if share > 1 else 0
     own_tile = tiles_ref[ids_ref[3]]
     own_rank = ranks_ref[own_tile, own_tile]
     quarter = stack.shape[0] // len(pieces)
@@ -176,7 +189,6 @@
         live = (rows < own_rank) & (cols < ranks_ref[band_tile, band_tile])
         live = live & (band_tile < own_tile)
         core_mat = jnp.where(live, total, 0.0).astype(jnp.bfloat16)
-        stack[:, :width] = trail_ref[0, b]
         at = 0
         for k, count in enumerate(pieces):
             blocks = max(share, count)
@@ -189,13 +201,18 @@
                     (((1,), (1,)), ((), ())),
                     preferred_element_type=jnp.float32,
                 )
-                inside = (core ^ j) * (quarter // share) + (h - j * blocks // share) * size
+                inside = (flip ^ j) * (quarter // share) + (h - j * blocks // share) * size
                 place = pl.multiple_of((low ^ k) * quarter + inside, 16)
-                stack[pl.ds(place, size), width:] = -update.astype(jnp.bfloat16)
+                stack[pl.ds(place, size), :] = -update.astype(jnp.bfloat16)
             at += count
-        gram = cross_rows(stack[...], stack[...])
-        mask = keep_mask(width, ranks_ref[own_tile, band_tile], width)
-        out_ref[0, b] = jnp.where(mask, gram, 0.0)
+        change = stack[...]
+        both = cross_rows(change, jnp.concatenate([trail_ref[0, b], change], axis=1))
+        rank = ranks_ref[own_tile, band_tile]
+        mixed = jnp.where(cols < rank, both[:, :width], 0.0)
+        out_ref[0, b, :width, :width] = kept_ref[b]
+        out_ref[0, b, :width, width:] = mixed.T
+        out_ref[0, b, width:, :width] = mixed
+        out_ref[0, b, width:, width:] = both[:, width:]
 
 
 def call(kernel, outs, scalars, arrays, scratch=()):
@@ -223,7 +240,8 @@
     row = lax.axis_index("row").astype(jnp.int32)
     core = lax.axis_index("col").astype(jnp.int32)
     high, low = row // inner, row % inner
-    ids = jnp.stack([high, low, core, row])
+    halved = inner == 4 and outer == 4 and cols == 2
+    ids = jnp.stack([high, low, core, row, high % 2 if halved else core])
 
     def swap(x, axis, distance, count):
         return lax.ppermute(x, axis, [(i, i ^ distance) for i in range(count)])
@@ -255,16 +273,20 @@
         pieces = (1,) * inner
     bands = [band_cols] + [core_swap(band_cols, j) for j in range(1, cols)]
 
-    gram_left = call(
+    gram_left, gram_kept = call(
         functools.partial(left_kernel, width=width),
-        jax.ShapeDtypeStruct((1, per_col, 2 * width, 2 * width), f32),
+        [
+            jax.ShapeDtypeStruct((1, per_col, 2 * width, 2 * width), f32),
+            pltpu.VMEM((per_col, width, width), f32),
+        ],
         (ids, tile_of_slot, rank_map, band_cols),
-        (trail_u, panel_u),
+        (trail_u, panel_u, trail_v),
     )
 
     quarter = points // inner
     share = cols if quarter % (cols * 16) == 0 else 1
     size = quarter // share
+    split_rows = halved and share == 2
     mine = core * size if share > 1 else 0
     t_blocks = [
         lax.dynamic_slice_in_dim(panel_u[0], (low ^ k) * quarter + mine, size)
@@ -277,34 +299,38 @@
         (ids, tile_of_slot, *bands[:share]),
         t_blocks,
     )
+
+    def merged(kept, got, bit):
+        return call(
+            functools.partial(merge_kernel, inner=inner, bit=bit),
+            pltpu.VMEM(kept.shape, bf16),
+            (ids, tile_of_slot, band_cols),
+            (kept, got),
+        )
+
     base = picked[0]
-    if share > 1:
-        base = call(
-            join_kernel,
-            pltpu.VMEM((per_col, quarter, width), bf16),
-            (),
-            picked[:1] + [core_swap(picked[j], j) for j in range(1, share)],
-        )
-    bit = outer // 2
-    while bit:
-        base = call(
-            functools.partial(merge_kernel, inner=inner, bit=bit),
-            pltpu.VMEM((per_col, quarter, width), bf16),
-            (ids, tile_of_slot, band_cols),
-            (base, high_swap(base, bit)),
-        )
-        bit //= 2
-    base_blocks = [base] + [low_swap(base, k) for k in range(1, 3 if inner == 4 else inner)]
-    base_pieces = (1,) * inner
-    if inner == 4:
-        far = call(
-            halves_kernel,
-            [pltpu.VMEM((per_col, quarter // 2, width), bf16)] * 2,
-            (),
-            (base_blocks[2], base_blocks[1]),
-        )
-        base_blocks += [swap(far[0], "row", 1, rows), swap(far[1], "row", 2, rows)]
-        base_pieces = (1, 1, 1, 2)
+    exchanged = picked[:1] + [core_swap(picked[j], j) for j in range(1, share)]
+    if split_rows:
+        kept, sent = call(
+            sort_kernel, [pltpu.VMEM((per_col, size, width), bf16)] * 2, (ids,), exchanged
+        )
+        kept = merged(kept, high_swap(sent, 1), 1)
+        kept = merged(kept, high_swap(kept, 2), 2)
+        rest = high_swap(kept, 1)
+        kept_y, rest_x = low_swap(kept, 2), low_swap(rest, 1)
+        kept_x, rest_y = low_swap(kept, 1), low_swap(rest, 2)
+        far = [swap(kept_y, "row", 1, rows), swap(rest_x, "row", 2, rows)]
+        base_blocks = [kept, rest, kept_x, rest_x, kept_y, rest_y, *far]
+        base_pieces = (2,) * inner
+    else:
+        if share > 1:
+            base = call(join_kernel, pltpu.VMEM((per_col, quarter, width), bf16), (), exchanged)
+        bit = outer // 2
+        while bit:
+            base = merged(base, high_swap(base, bit), bit)
+            bit //= 2
+        base_blocks = [base] + [low_swap(base, k) for k in range(1, inner)]
+        base_pieces = (1,) * inner
 
     early = outer - 1
     solved_blocks = []
@@ -342,8 +368,8 @@
         functools.partial(right_kernel, pieces=base_pieces, outer=outer, width=width, share=share),
         jax.ShapeDtypeStruct((1, per_col, 2 * width, 2 * width), f32),
         (ids, tile_of_slot, rank_map, band_cols),
-        (*core_parts, *base_blocks, trail_v),
-        [pltpu.VMEM((points, 2 * width), bf16)],
+        (*core_parts, *base_blocks, gram_kept, trail_v),
+        [pltpu.VMEM((points, width), bf16)],
     )
     return gram_left, gram_right
 

time: 89.4 us -> 102 us (1.14)
  starting transfers between devices: 29.7 us -> 39.1 us
  Pallas kernels: 11.8 us -> 14.2 us
  local copies, waits for them, and re-layouts: 1.1 us -> 2.15 us
    ppermute x25 -> x28, starting transfers between devices: 21.7 us -> 31 us  [swap(): return lax.ppermute(x, axis, [(i, i ^ distance) for i in range(count)])]
    pallas_call x13 -> x12, Pallas kernels: 11.8 us -> 14.2 us  [call(): pl.pallas_call(kernel, out_shape=outs, in_specs=[SMEM] * len(scalars) + [...]
    unnamed x16 -> x18, local copies, waits for them, and re-layouts: 0.04 us -> 2 us
    ppermute x25 -> x28, waiting for transfers between devices: 41.1 us -> 39.8 us  [swap(): return lax.ppermute(x, axis, [(i, i ^ distance) for i in range(count)])]
  transfers between devices with their start and end apart: 30 -> 33, of which waited for: 12 -> 11; matrix products, arithmetic and copies ran while one was open for 1% -> 0% of each run, Pallas kernels for 10% -> 11%
where the time goes in v2:
time: 102 us
  waiting for transfers between devices  45.3 us (44%)
  starting transfers between devices  39.1 us (38%)
  Pallas kernels  14.2 us (14%)
  local copies, waits for them, and re-layouts  2.15 us (2%)
    ppermute x28, waiting for transfers between devices, swap(): return lax.ppermute(x, axis, [(i, i ^ distance) for i in range(count)])  39.8 us
    ppermute x28, starting transfers between devices, swap(): return lax.ppermute(x, axis, [(i, i ^ distance) for i in range(count)])  31 us
    pallas_call x12, Pallas kernels, call(): pl.pallas_call(kernel, out_shape=outs, in_specs=[SMEM] * len(scalars) + [...  14.2 us
    ppermute x3, waiting for transfers between devices, shards(): lax.ppermute(v_blocks[m ^ low_bit], 'row', [(r, r ^ low_bit * inner) for...  5.56 us
    ppermute x3, starting transfers between devices, shards(): lax.ppermute(v_blocks[m ^ low_bit], 'row', [(r, r ^ low_bit * inner) for...  4.74 us
  transfers between devices with their start and end apart: 33, of which 11 were waited for; matrix products, arithmetic and copies ran while one was open for 0% of the time, Pallas kernels for 11%

profile of v2, /device:TPU:0, one launch (start us, length us, event | category | flops | bytes accessed | tf_op | source)
XLA Modules:
  0.0 101.6 jit_solution(1409502708105175300)
XLA Ops:
  0.6 3.1 %collective-permute-start.2 = (bf16[160,1280]{1,0:T(8,128)(2,1)}, bf16[160,1280]{1,0:T(8,128)(2,1)S(1)}, u32[]{:S(2)}, u32[]{:S(2)}) collective-permute-start(bf16[160,1280]{1,0:T(8,128)(2,1)} %refs_0_.5), channel_id=1, source_target_pairs={{0,4},{2,6},{4,0},{6,2},{8,12},{10,14},{12,8},{14,10},{16,20},{18,... | collective-permute-start | bytes 1228808 | tf_op jit(solution)/shard_map/ppermute | solution.py:247
  3.7 1.5 %collective-permute-start.1 = (bf16[160,1280]{1,0:T(8,128)(2,1)}, bf16[160,1280]{1,0:T(8,128)(2,1)S(1)}, u32[]{:S(2)}, u32[]{:S(2)}) collective-permute-start(bf16[160,1280]{1,0:T(8,128)(2,1)} %refs_0_.5), channel_id=1, source_target_pairs={{0,2},{2,0},{4,6},{6,4},{8,10},{10,8},{12,14},{14,12},{16,18},{18,... | collective-permute-start | bytes 1228808 | tf_op jit(solution)/shard_map/ppermute | solution.py:247
  5.2 2.6 %collective-permute-start.6 = (bf16[1280,128]{1,0:T(8,128)(2,1)}, bf16[1280,128]{1,0:T(8,128)(2,1)}, u32[]{:S(2)}, u32[]{:S(2)}) collective-permute-start(bf16[1280,128]{1,0:T(8,128)(2,1)} %bitcast.14), channel_id=1, source_target_pairs={{0,16},{2,18},{4,20},{6,22},{8,24},{10,26},{12,28},{14,30},{16,0},... | collective-permute-start | bytes 983048 | tf_op jit(solution)/shard_map/ppermute | solution.py:261
  7.8 1.6 %collective-permute-start.5 = (bf16[1280,128]{1,0:T(8,128)(2,1)}, bf16[1280,128]{1,0:T(8,128)(2,1)S(1)}, u32[]{:S(2)}, u32[]{:S(2)}) collective-permute-start(bf16[1280,128]{1,0:T(8,128)(2,1)} %bitcast.15), channel_id=1, source_target_pairs={{0,8},{2,10},{4,12},{6,14},{8,0},{10,2},{12,4},{14,6},{16,24},{18,... | collective-permute-start | bytes 983048 | tf_op jit(solution)/shard_map/ppermute | solution.py:261
  9.3 4.0 %collective-permute-done.2.refs_2_ = bf16[160,1280]{1,0:T(8,128)(2,1)S(1)} collective-permute-done((bf16[160,1280]{1,0:T(8,128)(2,1)}, bf16[160,1280]{1,0:T(8,128)(2,1)S(1)}, u32[]{:S(2)}, u32[]{:S(2)}) %collective-permute-start.2) | collective-permute-done | bytes 409632 | tf_op jit(solution)/shard_map/ppermute | solution.py:247
  13.4 1.8 %collective-permute-start.3 = (bf16[80,1280]{1,0:T(8,128)(2,1)S(1)}, bf16[80,1280]{1,0:T(8,128)(2,1)S(1)}, u32[]{:S(2)}, u32[]{:S(2)}) collective-permute-start(bf16[80,1280]{1,0:T(8,128)(2,1)S(1)} %slice.8), channel_id=1, source_target_pairs={{0,2},{2,0},{4,6},{6,4},{8,10},{10,8},{12,14},{14,12},{16,18},{18,... | collective-permute-start | bytes 614408 | tf_op jit(solution)/shard_map/ppermute | solution.py:267
  15.2 1.6 %collective-permute-start.4 = (bf16[80,1280]{1,0:T(8,128)(2,1)S(1)}, bf16[80,1280]{1,0:T(8,128)(2,1)S(1)}, u32[]{:S(2)}, u32[]{:S(2)}) collective-permute-start(bf16[80,1280]{1,0:T(8,128)(2,1)S(1)} %slice.9), channel_id=1, source_target_pairs={{0,4},{2,6},{4,0},{6,2},{8,12},{10,14},{12,8},{14,10},{16,20},{18,... | collective-permute-start | bytes 614408 | tf_op jit(solution)/shard_map/ppermute | solution.py:268
  16.9 5.6 %collective-permute-done.6.refs_7_ = bf16[1280,128]{1,0:T(8,128)(2,1)} collective-permute-done((bf16[1280,128]{1,0:T(8,128)(2,1)}, bf16[1280,128]{1,0:T(8,128)(2,1)}, u32[]{:S(2)}, u32[]{:S(2)}) %collective-permute-start.6) | collective-permute-done | bytes 327712 | tf_op jit(solution)/shard_map/ppermute | solution.py:261
  22.4 0.6 collective-permute-start.8
  23.0 1.0 copy-done.1
  24.0 1.0 copy-done.5
  25.0 3.0 %shard_map.96 = (f32[320,384]{1,0:T(8,128)S(1)}, f32[320,384]{1,0:T(8,128)}) custom-call(s32[5]{0:T(128)S(1)} %stack.23.ids_ref, bf16[160,1280]{1,0:T(8,128)(2,1)S(1)} %copy-done.1, bf16[160,1280]{1,0:T(8,128)(2,1)S(1)} %collective-permute-done.1.refs_1_, bf16[160,1280]{1,0:T(8,128)(2,1)S(1)} %collective-permute-done.2.refs_2_, ...), custom_call_target="tpu_custom_call" | custom-call | tf_op jit(solution)/shard_map/pallas_call | solution.py:219
  28.0 0.6 collective-permute-start.20
  28.6 0.5 collective-permute-start.21
  29.1 2.4 %collective-permute-start.22 = (bf16[320,128]{1,0:T(8,128)(2,1)S(1)}, bf16[320,128]{1,0:T(8,128)(2,1)S(1)}, u32[]{:S(2)}, u32[]{:S(2)}) collective-permute-start(bf16[320,128]{1,0:T(8,128)(2,1)S(1)} %get-tuple-element.34), channel_id=1, source_target_pairs={{0,6},{2,4},{4,2},{6,0},{8,14},{10,12},{12,10},{14,8},{16,22},{18,... | collective-permute-start | bytes 245768 | tf_op jit(solution)/shard_map/ppermute | solution.py:247
  31.6 1.6 %shard_map.98 = (f32[320,128]{1,0:T(8,128)S(1)}, f32[320,128]{1,0:T(8,128)S(1)}) custom-call(s32[5]{0:T(128)S(1)} %stack.23.ids_ref, bf16[160,1280]{1,0:T(8,128)(2,1)S(1)} %copy-done.2, bf16[160,1280]{1,0:T(8,128)(2,1)S(1)} %collective-permute-done.1.refs_1_, bf16[160,1280]{1,0:T(8,128)(2,1)S(1)} %collective-permute-done.2.refs_2_, ...), custom_call_target="tpu_custom_call" | custom-call | tf_op jit(solution)/shard_map/pallas_call | solution.py:219
  33.2 0.6 collective-permute-start.9
  33.8 1.1 %collective-permute-done.21.refs_4_ = bf16[320,128]{1,0:T(8,128)(2,1)S(1)} collective-permute-done((bf16[320,128]{1,0:T(8,128)(2,1)S(1)}, bf16[320,128]{1,0:T(8,128)(2,1)S(1)}, u32[]{:S(2)}, u32[]{:S(2)}) %collective-permute-start.21) | collective-permute-done | bytes 81952 | tf_op jit(solution)/shard_map/ppermute | solution.py:247
  34.9 0.7 shard_map.102
  35.8 1.6 %collective-permute-start.10 = (bf16[320,384]{1,0:T(8,128)(2,1)S(1)}, bf16[320,384]{1,0:T(8,128)(2,1)S(1)}, u32[]{:S(2)}, u32[]{:S(2)}) collective-permute-start(bf16[320,384]{1,0:T(8,128)(2,1)S(1)} %shard_map.97.refs_2_), channel_id=1, source_target_pairs={{0,2},{2,0},{4,6},{6,4},{8,10},{10,8},{12,14},{14,12},{16,18},{18,... | collective-permute-start | bytes 737288 | tf_op jit(solution)/shard_map/ppermute | solution.py:247
  37.3 1.0 %collective-permute-start.12 = (bf16[320,384]{1,0:T(8,128)(2,1)S(1)}, bf16[320,384]{1,0:T(8,128)(2,1)S(1)}, u32[]{:S(2)}, u32[]{:S(2)}) collective-permute-start(bf16[320,384]{1,0:T(8,128)(2,1)S(1)} %shard_map.97.refs_2_), channel_id=1, source_target_pairs={{0,4},{2,6},{4,0},{6,2},{8,12},{10,14},{12,8},{14,10},{16,20},{18,... | collective-permute-start | bytes 737288 | tf_op jit(solution)/shard_map/ppermute | solution.py:247
  38.4 1.0 collective-permute-start.14
  39.4 1.6 %collective-permute-start.11 = (bf16[320,128]{1,0:T(8,128)(2,1)S(1)}, bf16[320,128]{1,0:T(8,128)(2,1)S(1)}, u32[]{:S(2)}, u32[]{:S(2)}) collective-permute-start(bf16[320,128]{1,0:T(8,128)(2,1)S(1)} %shard_map.99.refs_3_), channel_id=1, source_target_pairs={{0,2},{2,0},{4,6},{6,4},{8,10},{10,8},{12,14},{14,12},{16,18},{18,... | collective-permute-start | bytes 245768 | tf_op jit(solution)/shard_map/ppermute | solution.py:247
  40.9 1.0 %collective-permute-start.13 = (bf16[320,128]{1,0:T(8,128)(2,1)S(1)}, bf16[320,128]{1,0:T(8,128)(2,1)S(1)}, u32[]{:S(2)}, u32[]{:S(2)}) collective-permute-start(bf16[320,128]{1,0:T(8,128)(2,1)S(1)} %shard_map.99.refs_3_), channel_id=1, source_target_pairs={{0,4},{2,6},{4,0},{6,2},{8,12},{10,14},{12,8},{14,10},{16,20},{18,... | collective-permute-start | bytes 245768 | tf_op jit(solution)/shard_map/ppermute | solution.py:247
  42.0 0.6 shard_map.103
  42.5 8.7 %collective-permute-done.11.refs_5_ = bf16[320,128]{1,0:T(8,128)(2,1)S(1)} collective-permute-done((bf16[320,128]{1,0:T(8,128)(2,1)S(1)}, bf16[320,128]{1,0:T(8,128)(2,1)S(1)}, u32[]{:S(2)}, u32[]{:S(2)}) %collective-permute-start.11) | collective-permute-done | bytes 81952 | tf_op jit(solution)/shard_map/ppermute | solution.py:247
  51.3 1.4 %collective-permute-start.24 = (bf16[2,320,128]{2,1,0:T(8,128)(2,1)S(1)}, bf16[2,320,128]{2,1,0:T(8,128)(2,1)S(1)}, u32[]{:S(2)}, u32[]{:S(2)}) collective-permute-start(bf16[2,320,128]{2,1,0:T(8,128)(2,1)S(1)} %get-tuple-element.32), channel_id=1, source_target_pairs={{0,8},{2,10},{4,12},{6,14},{8,0},{10,2},{12,4},{14,6},{16,24},{18,... | collective-permute-start | bytes 491528 | tf_op jit(solution)/shard_map/ppermute | solution.py:247
  52.7 2.0 %collective-permute-start.15 = (bf16[320,128]{1,0:T(8,128)(2,1)S(1)}, bf16[320,128]{1,0:T(8,128)(2,1)S(1)}, u32[]{:S(2)}, u32[]{:S(2)}) collective-permute-start(bf16[320,128]{1,0:T(8,128)(2,1)S(1)} %shard_map.99.refs_3_), channel_id=1, source_target_pairs={{0,6},{2,4},{4,2},{6,0},{8,14},{10,12},{12,10},{14,8},{16,22},{18,... | collective-permute-start | bytes 245768 | tf_op jit(solution)/shard_map/ppermute | solution.py:247
  54.7 3.4 %collective-permute-done.15.refs_9_ = bf16[320,128]{1,0:T(8,128)(2,1)S(1)} collective-permute-done((bf16[320,128]{1,0:T(8,128)(2,1)S(1)}, bf16[320,128]{1,0:T(8,128)(2,1)S(1)}, u32[]{:S(2)}, u32[]{:S(2)}) %collective-permute-start.15) | collective-permute-done | bytes 81952 | tf_op jit(solution)/shard_map/ppermute | solution.py:247
  58.1 1.3 %shard_map.100 = (f32[512,256]{1,0:T(8,128)S(1)}, f32[512,256]{1,0:T(8,128)S(1)}) custom-call(s32[5]{0:T(128)S(1)} %stack.23.ids_ref, s32[16]{0:T(128)S(1)} %copy-done.7, s32[2]{0:T(128)S(1)} %copy-done.8, s32[2]{0:T(128)S(1)} %collective-permute-done.refs_1_, bf16[320,384]{1,0:T(8,128)(2,1)S(1)} %shard_map.97.refs_2_, ...), custom_call_target="tpu_custom_call" | custom-call | tf_op jit(solution)/shard_map/pallas_call | solution.py:219
  59.5 0.6 shard_map.104.kept_ref
  60.1 3.2 %collective-permute-start.25 = (bf16[2,320,128]{2,1,0:T(8,128)(2,1)S(1)}, bf16[2,320,128]{2,1,0:T(8,128)(2,1)S(1)}, u32[]{:S(2)}, u32[]{:S(2)}) collective-permute-start(bf16[2,320,128]{2,1,0:T(8,128)(2,1)S(1)} %shard_map.104.kept_ref), channel_id=1, source_target_pairs={{0,16},{2,18},{4,20},{6,22},{8,24},{10,26},{12,28},{14,30},{16,0},... | collective-permute-start | bytes 491528 | tf_op jit(solution)/shard_map/ppermute | solution.py:247
  63.3 8.4 %collective-permute-done.25.got_ref = bf16[2,320,128]{2,1,0:T(8,128)(2,1)S(1)} collective-permute-done((bf16[2,320,128]{2,1,0:T(8,128)(2,1)S(1)}, bf16[2,320,128]{2,1,0:T(8,128)(2,1)S(1)}, u32[]{:S(2)}, u32[]{:S(2)}) %collective-permute-start.25) | collective-permute-done | bytes 163872 | tf_op jit(solution)/shard_map/ppermute | solution.py:247
  71.7 0.6 shard_map.105.refs_4_
  72.5 1.2 %collective-permute-start.29 = (bf16[2,320,128]{2,1,0:T(8,128)(2,1)S(1)}, bf16[2,320,128]{2,1,0:T(8,128)(2,1)S(1)}, u32[]{:S(2)}, u32[]{:S(2)}) collective-permute-start(bf16[2,320,128]{2,1,0:T(8,128)(2,1)S(1)} %shard_map.105.refs_4_), channel_id=1, source_target_pairs={{0,4},{2,6},{4,0},{6,2},{8,12},{10,14},{12,8},{14,10},{16,20},{18,... | collective-permute-start | bytes 491528 | tf_op jit(solution)/shard_map/ppermute | solution.py:247
  73.7 4.7 %collective-permute-done.26.refs_5_ = bf16[2,320,128]{2,1,0:T(8,128)(2,1)S(1)} collective-permute-done((bf16[2,320,128]{2,1,0:T(8,128)(2,1)S(1)}, bf16[2,320,128]{2,1,0:T(8,128)(2,1)S(1)}, u32[]{:S(2)}, u32[]{:S(2)}) %collective-permute-start.26) | collective-permute-done | bytes 163872 | tf_op jit(solution)/shard_map/ppermute | solution.py:247
  78.4 0.8 collective-permute-start.28
  79.1 1.3 %collective-permute-start.27 = (bf16[2,320,128]{2,1,0:T(8,128)(2,1)S(1)}, bf16[2,320,128]{2,1,0:T(8,128)(2,1)S(1)}, u32[]{:S(2)}, u32[]{:S(2)}) collective-permute-start(bf16[2,320,128]{2,1,0:T(8,128)(2,1)S(1)} %shard_map.105.refs_4_), channel_id=1, source_target_pairs={{0,2},{2,0},{4,6},{6,4},{8,10},{10,8},{12,14},{14,12},{16,18},{18,... | collective-permute-start | bytes 491528 | tf_op jit(solution)/shard_map/ppermute | solution.py:247
  80.4 1.0 %collective-permute-start.30 = (bf16[2,320,128]{2,1,0:T(8,128)(2,1)S(1)}, bf16[2,320,128]{2,1,0:T(8,128)(2,1)S(1)}, u32[]{:S(2)}, u32[]{:S(2)}) collective-permute-start(bf16[2,320,128]{2,1,0:T(8,128)(2,1)S(1)} %collective-permute-done.26.refs_5_), channel_id=1, source_target_pairs={{0,4},{2,6},{4,0},{6,2},{8,12},{10,14},{12,8},{14,10},{16,20},{18,... | collective-permute-start | bytes 491528 | tf_op jit(solution)/shard_map/ppermute | solution.py:247
  81.4 0.8 collective-permute-start.31
  82.2 3.2 %collective-permute-done.28.refs_7_ = bf16[2,320,128]{2,1,0:T(8,128)(2,1)S(1)} collective-permute-done((bf16[2,320,128]{2,1,0:T(8,128)(2,1)S(1)}, bf16[2,320,128]{2,1,0:T(8,128)(2,1)S(1)}, u32[]{:S(2)}, u32[]{:S(2)}) %collective-permute-start.28) | collective-permute-done | bytes 163872 | tf_op jit(solution)/shard_map/ppermute | solution.py:247
  85.4 1.0 %collective-permute-start.32 = (bf16[2,320,128]{2,1,0:T(8,128)(2,1)S(1)}, bf16[2,320,128]{2,1,0:T(8,128)(2,1)S(1)}, u32[]{:S(2)}, u32[]{:S(2)}) collective-permute-start(bf16[2,320,128]{2,1,0:T(8,128)(2,1)S(1)} %collective-permute-done.28.refs_7_), channel_id=1, source_target_pairs={{0,4},{2,6},{4,0},{6,2},{8,12},{10,14},{12,8},{14,10},{16,20},{18,... | collective-permute-start | bytes 491528 | tf_op jit(solution)/shard_map/ppermute | solution.py:247
  86.9 1.9 %collective-permute-done.27.refs_6_ = bf16[2,320,128]{2,1,0:T(8,128)(2,1)S(1)} collective-permute-done((bf16[2,320,128]{2,1,0:T(8,128)(2,1)S(1)}, bf16[2,320,128]{2,1,0:T(8,128)(2,1)S(1)}, u32[]{:S(2)}, u32[]{:S(2)}) %collective-permute-start.27) | collective-permute-done | bytes 163872 | tf_op jit(solution)/shard_map/ppermute | solution.py:247
  88.8 1.6 %collective-permute-start.18 = (f32[128,256]{1,0:T(8,128)S(1)}, f32[128,256]{1,0:T(8,128)S(1)}, u32[]{:S(2)}, u32[]{:S(2)}) collective-permute-start(f32[128,256]{1,0:T(8,128)S(1)} %get-tuple-element.27), channel_id=1, source_target_pairs={{0,16},{2,18},{4,20},{6,22},{8,24},{10,26},{12,28},{14,30},{16,0},... | collective-permute-start | bytes 393224 | tf_op jit(solution)/shard_map/ppermute | solution.py:247
  90.4 1.2 %collective-permute-start.19 = (f32[128,256]{1,0:T(8,128)S(1)}, f32[128,256]{1,0:T(8,128)S(1)}, u32[]{:S(2)}, u32[]{:S(2)}) collective-permute-start(f32[128,256]{1,0:T(8,128)S(1)} %get-tuple-element.28), channel_id=1, source_target_pairs={{0,24},{2,26},{4,28},{6,30},{8,16},{10,18},{12,20},{14,22},{16,8},... | collective-permute-start | bytes 393224 | tf_op jit(solution)/shard_map/ppermute | solution.py:247
  91.6 2.7 %shard_map.95 = (f32[1,2,256,256]{3,2,1,0:T(8,128)}, f32[2,128,128]{2,1,0:T(8,128)S(1)}) custom-call(s32[5]{0:T(128)S(1)} %stack.23.ids_ref, s32[16]{0:T(128)S(1)} %copy-done.7, s32[16,16]{1,0:T(8,128)S(1)} %copy-done.6, s32[2]{0:T(128)S(1)} %copy-done.8, bf16[1,2,2560,128]{3,2,1,0:T(8,128)(2,1)S(1)} %copy-done.4, bf16[1,2560,128]{2,1,0:T(8,128)(2,1)S(1)} %copy-done.3, ...), custom_call_target="tpu_custom_call" | custom-call | tf_op jit(solution)/shard_map/pallas_call | solution.py:219
  94.4 4.2 %collective-permute-done.18.refs_2_ = f32[128,256]{1,0:T(8,128)S(1)} collective-permute-done((f32[128,256]{1,0:T(8,128)S(1)}, f32[128,256]{1,0:T(8,128)S(1)}, u32[]{:S(2)}, u32[]{:S(2)}) %collective-permute-start.18) | collective-permute-done | bytes 131104 | tf_op jit(solution)/shard_map/ppermute | solution.py:247
  98.6 3.0 %shard_map.106 = f32[1,2,256,256]{3,2,1,0:T(8,128)} custom-call(s32[5]{0:T(128)S(1)} %stack.23.ids_ref, s32[16]{0:T(128)S(1)} %copy-done.7, s32[16,16]{1,0:T(8,128)S(1)} %copy-done.6, s32[2]{0:T(128)S(1)} %copy-done.8, f32[128,256]{1,0:T(8,128)S(1)} %get-tuple-element.25.refs_0_, f32[128,256]{1,0:T(8,128)S(1)} %collective-permute-done.17.refs_1_, ...), custom_call_target="tpu_custom_call" | custom-call | tf_op jit(solution)/shard_map/pallas_call | solution.py:219
  (52 shorter events, 1.2 us)
Async XLA Ops:
  0.6 12.7 %collective-permute-start.2 = (bf16[160,1280]{1,0:T(8,128)(2,1)}, bf16[160,1280]{1,0:T(8,128)(2,1)S(1)}, u32[]{:S(2)}, u32[]{:S(2)}) collective-permute-start(bf16[160,1280]{1,0:T(8,128)(2,1)} %refs_0_.5), channel_id=1, source_target_pairs={{0,4},{2,6},{4,0},{6,2},{8,12},{10,14},{12,8},{14,10},{16,20},{18,... | collective-permute-start | bytes 1228808 | tf_op jit(solution)/shard_map/ppermute | solution.py:247
  3.7 11.5 %collective-permute-start.1 = (bf16[160,1280]{1,0:T(8,128)(2,1)}, bf16[160,1280]{1,0:T(8,128)(2,1)S(1)}, u32[]{:S(2)}, u32[]{:S(2)}) collective-permute-start(bf16[160,1280]{1,0:T(8,128)(2,1)} %refs_0_.5), channel_id=1, source_target_pairs={{0,2},{2,0},{4,6},{6,4},{8,10},{10,8},{12,14},{14,12},{16,18},{18,... | collective-permute-start | bytes 1228808 | tf_op jit(solution)/shard_map/ppermute | solution.py:247
  5.2 17.2 %collective-permute-start.6 = (bf16[1280,128]{1,0:T(8,128)(2,1)}, bf16[1280,128]{1,0:T(8,128)(2,1)}, u32[]{:S(2)}, u32[]{:S(2)}) collective-permute-start(bf16[1280,128]{1,0:T(8,128)(2,1)} %bitcast.14), channel_id=1, source_target_pairs={{0,16},{2,18},{4,20},{6,22},{8,24},{10,26},{12,28},{14,30},{16,0},... | collective-permute-start | bytes 983048 | tf_op jit(solution)/shard_map/ppermute | solution.py:261
  7.8 15.2 %collective-permute-start.5 = (bf16[1280,128]{1,0:T(8,128)(2,1)}, bf16[1280,128]{1,0:T(8,128)(2,1)S(1)}, u32[]{:S(2)}, u32[]{:S(2)}) collective-permute-start(bf16[1280,128]{1,0:T(8,128)(2,1)} %bitcast.15), channel_id=1, source_target_pairs={{0,8},{2,10},{4,12},{6,14},{8,0},{10,2},{12,4},{14,6},{16,24},{18,... | collective-permute-start | bytes 983048 | tf_op jit(solution)/shard_map/ppermute | solution.py:261
  13.4 9.6 %collective-permute-start.3 = (bf16[80,1280]{1,0:T(8,128)(2,1)S(1)}, bf16[80,1280]{1,0:T(8,128)(2,1)S(1)}, u32[]{:S(2)}, u32[]{:S(2)}) collective-permute-start(bf16[80,1280]{1,0:T(8,128)(2,1)S(1)} %slice.8), channel_id=1, source_target_pairs={{0,2},{2,0},{4,6},{6,4},{8,10},{10,8},{12,14},{14,12},{16,18},{18,... | collective-permute-start | bytes 614408 | tf_op jit(solution)/shard_map/ppermute | solution.py:267
  15.2 7.8 %collective-permute-start.4 = (bf16[80,1280]{1,0:T(8,128)(2,1)S(1)}, bf16[80,1280]{1,0:T(8,128)(2,1)S(1)}, u32[]{:S(2)}, u32[]{:S(2)}) collective-permute-start(bf16[80,1280]{1,0:T(8,128)(2,1)S(1)} %slice.9), channel_id=1, source_target_pairs={{0,4},{2,6},{4,0},{6,2},{8,12},{10,14},{12,8},{14,10},{16,20},{18,... | collective-permute-start | bytes 614408 | tf_op jit(solution)/shard_map/ppermute | solution.py:268
  16.8 14.8 %copy-start.8 = (s32[2]{0:T(128)S(1)}, s32[2]{0:T(128)}, u32[]{:S(2)}) copy-start(s32[2]{0:T(128)} %bands_ref.7) | copy-start | bytes 28
  22.4 9.1 %collective-permute-start.8 = (bf16[1280,128]{1,0:T(8,128)(2,1)}, bf16[1280,128]{1,0:T(8,128)(2,1)}, u32[]{:S(2)}, u32[]{:S(2)}) collective-permute-start(bf16[1280,128]{1,0:T(8,128)(2,1)} %collective-permute-done.6.refs_7_), channel_id=1, source_target_pairs={{0,8},{2,10},{4,12},{6,14},{8,0},{10,2},{12,4},{14,6},{16,24},{18,... | collective-permute-start | bytes 983048 | tf_op jit(solution)/shard_map/ppermute | solution.py:261
  23.0 1.0 copy-start.1
  24.0 1.0 copy-start.5
  25.0 3.0 %copy-start.3 = (bf16[1,2560,128]{2,1,0:T(8,128)(2,1)S(1)}, bf16[1,2560,128]{2,1,0:T(8,128)(2,1)}, u32[]{:S(2)}) copy-start(bf16[1,2560,128]{2,1,0:T(8,128)(2,1)} %panel_ref.1) | copy-start | bytes 1966084
  25.0 6.6 %copy-start.2 = (bf16[160,1280]{1,0:T(8,128)(2,1)S(1)}, bf16[160,1280]{1,0:T(8,128)(2,1)}, u32[]{:S(2)}) copy-start(bf16[160,1280]{1,0:T(8,128)(2,1)} %refs_0_.5) | copy-start | bytes 1228804
  27.9 7.8 %collective-permute-start.7 = (f32[320,384]{1,0:T(8,128)}, f32[320,384]{1,0:T(8,128)S(1)}, u32[]{:S(2)}, u32[]{:S(2)}) collective-permute-start(f32[320,384]{1,0:T(8,128)} %get-tuple-element.20), channel_id=1, source_target_pairs={{0,1},{1,0},{2,3},{3,2},{4,5},{5,4},{6,7},{7,6},{8,9},{9,8},{10,11... | collective-permute-start | bytes 1474568 | tf_op jit(solution)/shard_map/ppermute | solution.py:247
  27.9 7.0 %copy-start.7 = (s32[16]{0:T(128)S(1)}, s32[16]{0:T(128)}, u32[]{:S(2)}) copy-start(s32[16]{0:T(128)} %tiles_ref.11) | copy-start | bytes 196
  28.0 5.8 %collective-permute-start.20 = (bf16[320,128]{1,0:T(8,128)(2,1)S(1)}, bf16[320,128]{1,0:T(8,128)(2,1)S(1)}, u32[]{:S(2)}, u32[]{:S(2)}) collective-permute-start(bf16[320,128]{1,0:T(8,128)(2,1)S(1)} %get-tuple-element.35), channel_id=1, source_target_pairs={{0,2},{2,0},{4,6},{6,4},{8,10},{10,8},{12,14},{14,12},{16,18},{18,... | collective-permute-start | bytes 245768 | tf_op jit(solution)/shard_map/ppermute | solution.py:247
  28.6 6.3 %collective-permute-start.21 = (bf16[320,128]{1,0:T(8,128)(2,1)S(1)}, bf16[320,128]{1,0:T(8,128)(2,1)S(1)}, u32[]{:S(2)}, u32[]{:S(2)}) collective-permute-start(bf16[320,128]{1,0:T(8,128)(2,1)S(1)} %get-tuple-element.37), channel_id=1, source_target_pairs={{0,4},{2,6},{4,0},{6,2},{8,12},{10,14},{12,8},{14,10},{16,20},{18,... | collective-permute-start | bytes 245768 | tf_op jit(solution)/shard_map/ppermute | solution.py:247
  29.1 5.8 %collective-permute-start.22 = (bf16[320,128]{1,0:T(8,128)(2,1)S(1)}, bf16[320,128]{1,0:T(8,128)(2,1)S(1)}, u32[]{:S(2)}, u32[]{:S(2)}) collective-permute-start(bf16[320,128]{1,0:T(8,128)(2,1)S(1)} %get-tuple-element.34), channel_id=1, source_target_pairs={{0,6},{2,4},{4,2},{6,0},{8,14},{10,12},{12,10},{14,8},{16,22},{18,... | collective-permute-start | bytes 245768 | tf_op jit(solution)/shard_map/ppermute | solution.py:247
  31.5 1.7 %collective-permute-start = (s32[2]{0:T(128)S(1)}, s32[2]{0:T(128)S(1)}, u32[]{:S(2)}, u32[]{:S(2)}) collective-permute-start(s32[2]{0:T(128)S(1)} %copy-done.8), channel_id=1, source_target_pairs={{0,1},{1,0},{2,3},{3,2},{4,5},{5,4},{6,7},{7,6},{8,9},{9,8},{10,11... | collective-permute-start | bytes 32 | tf_op jit(solution)/shard_map/ppermute | solution.py:247
  33.2 6.1 %collective-permute-start.9 = (f32[320,128]{1,0:T(8,128)S(1)}, f32[320,128]{1,0:T(8,128)S(1)}, u32[]{:S(2)}, u32[]{:S(2)}) collective-permute-start(f32[320,128]{1,0:T(8,128)S(1)} %get-tuple-element.22), channel_id=1, source_target_pairs={{0,1},{1,0},{2,3},{3,2},{4,5},{5,4},{6,7},{7,6},{8,9},{9,8},{10,11... | collective-permute-start | bytes 491528 | tf_op jit(solution)/shard_map/ppermute | solution.py:247
  35.6 5.3 %collective-permute-start.23 = (bf16[2,320,128]{2,1,0:T(8,128)(2,1)S(1)}, bf16[2,320,128]{2,1,0:T(8,128)(2,1)S(1)}, u32[]{:S(2)}, u32[]{:S(2)}) collective-permute-start(bf16[2,320,128]{2,1,0:T(8,128)(2,1)S(1)} %get-tuple-element.30), channel_id=1, source_target_pairs={{0,1},{1,0},{2,3},{3,2},{4,5},{5,4},{6,7},{7,6},{8,9},{9,8},{10,11... | collective-permute-start | bytes 491528 | tf_op jit(solution)/shard_map/ppermute | solution.py:247
  35.8 22.3 %collective-permute-start.10 = (bf16[320,384]{1,0:T(8,128)(2,1)S(1)}, bf16[320,384]{1,0:T(8,128)(2,1)S(1)}, u32[]{:S(2)}, u32[]{:S(2)}) collective-permute-start(bf16[320,384]{1,0:T(8,128)(2,1)S(1)} %shard_map.97.refs_2_), channel_id=1, source_target_pairs={{0,2},{2,0},{4,6},{6,4},{8,10},{10,8},{12,14},{14,12},{16,18},{18,... | collective-permute-start | bytes 737288 | tf_op jit(solution)/shard_map/ppermute | solution.py:247
  37.3 20.7 %collective-permute-start.12 = (bf16[320,384]{1,0:T(8,128)(2,1)S(1)}, bf16[320,384]{1,0:T(8,128)(2,1)S(1)}, u32[]{:S(2)}, u32[]{:S(2)}) collective-permute-start(bf16[320,384]{1,0:T(8,128)(2,1)S(1)} %shard_map.97.refs_2_), channel_id=1, source_target_pairs={{0,4},{2,6},{4,0},{6,2},{8,12},{10,14},{12,8},{14,10},{16,20},{18,... | collective-permute-start | bytes 737288 | tf_op jit(solution)/shard_map/ppermute | solution.py:247
  38.4 19.7 %collective-permute-start.14 = (bf16[320,384]{1,0:T(8,128)(2,1)S(1)}, bf16[320,384]{1,0:T(8,128)(2,1)S(1)}, u32[]{:S(2)}, u32[]{:S(2)}) collective-permute-start(bf16[320,384]{1,0:T(8,128)(2,1)S(1)} %shard_map.97.refs_2_), channel_id=1, source_target_pairs={{0,6},{2,4},{4,2},{6,0},{8,14},{10,12},{12,10},{14,8},{16,22},{18,... | collective-permute-start | bytes 737288 | tf_op jit(solution)/shard_map/ppermute | solution.py:247
  39.4 11.9 %collective-permute-start.11 = (bf16[320,128]{1,0:T(8,128)(2,1)S(1)}, bf16[320,128]{1,0:T(8,128)(2,1)S(1)}, u32[]{:S(2)}, u32[]{:S(2)}) collective-permute-start(bf16[320,128]{1,0:T(8,128)(2,1)S(1)} %shard_map.99.refs_3_), channel_id=1, source_target_pairs={{0,2},{2,0},{4,6},{6,4},{8,10},{10,8},{12,14},{14,12},{16,18},{18,... | collective-permute-start | bytes 245768 | tf_op jit(solution)/shard_map/ppermute | solution.py:247
  40.9 11.8 %collective-permute-start.13 = (bf16[320,128]{1,0:T(8,128)(2,1)S(1)}, bf16[320,128]{1,0:T(8,128)(2,1)S(1)}, u32[]{:S(2)}, u32[]{:S(2)}) collective-permute-start(bf16[320,128]{1,0:T(8,128)(2,1)S(1)} %shard_map.99.refs_3_), channel_id=1, source_target_pairs={{0,4},{2,6},{4,0},{6,2},{8,12},{10,14},{12,8},{14,10},{16,20},{18,... | collective-permute-start | bytes 245768 | tf_op jit(solution)/shard_map/ppermute | solution.py:247
  51.3 8.3 %collective-permute-start.24 = (bf16[2,320,128]{2,1,0:T(8,128)(2,1)S(1)}, bf16[2,320,128]{2,1,0:T(8,128)(2,1)S(1)}, u32[]{:S(2)}, u32[]{:S(2)}) collective-permute-start(bf16[2,320,128]{2,1,0:T(8,128)(2,1)S(1)} %get-tuple-element.32), channel_id=1, source_target_pairs={{0,8},{2,10},{4,12},{6,14},{8,0},{10,2},{12,4},{14,6},{16,24},{18,... | collective-permute-start | bytes 491528 | tf_op jit(solution)/shard_map/ppermute | solution.py:247
  52.7 5.3 %collective-permute-start.15 = (bf16[320,128]{1,0:T(8,128)(2,1)S(1)}, bf16[320,128]{1,0:T(8,128)(2,1)S(1)}, u32[]{:S(2)}, u32[]{:S(2)}) collective-permute-start(bf16[320,128]{1,0:T(8,128)(2,1)S(1)} %shard_map.99.refs_3_), channel_id=1, source_target_pairs={{0,6},{2,4},{4,2},{6,0},{8,14},{10,12},{12,10},{14,8},{16,22},{18,... | collective-permute-start | bytes 245768 | tf_op jit(solution)/shard_map/ppermute | solution.py:247
  58.1 33.5 %copy-start.4 = (bf16[1,2,2560,128]{3,2,1,0:T(8,128)(2,1)S(1)}, bf16[1,2,2560,128]{3,2,1,0:T(8,128)(2,1)}, u32[]{:S(2)}) copy-start(bf16[1,2,2560,128]{3,2,1,0:T(8,128)(2,1)} %trail_ref.1) | copy-start | bytes 3932164
  59.4 32.2 %copy-start = (bf16[1,2,2560,128]{3,2,1,0:T(8,128)(2,1)S(1)}, bf16[1,2,2560,128]{3,2,1,0:T(8,128)(2,1)}, u32[]{:S(2)}) copy-start(bf16[1,2,2560,128]{3,2,1,0:T(8,128)(2,1)} %refs_13_.1) | copy-start | bytes 3932164
  59.4 32.2 %copy-start.6 = (s32[16,16]{1,0:T(8,128)S(1)}, s32[16,16]{1,0:T(8,128)}, u32[]{:S(2)}) copy-start(s32[16,16]{1,0:T(8,128)} %ranks_ref.3) | copy-start | bytes 3076
  59.4 27.0 %collective-permute-start.16 = (f32[512,256]{1,0:T(8,128)S(1)}, f32[512,256]{1,0:T(8,128)S(1)}, u32[]{:S(2)}, u32[]{:S(2)}) collective-permute-start(f32[512,256]{1,0:T(8,128)S(1)} %get-tuple-element.24), channel_id=1, source_target_pairs={{0,1},{1,0},{2,3},{3,2},{4,5},{5,4},{6,7},{7,6},{8,9},{9,8},{10,11... | collective-permute-start | bytes 1572872 | tf_op jit(solution)/shard_map/ppermute | solution.py:247
  60.1 11.5 %collective-permute-start.25 = (bf16[2,320,128]{2,1,0:T(8,128)(2,1)S(1)}, bf16[2,320,128]{2,1,0:T(8,128)(2,1)S(1)}, u32[]{:S(2)}, u32[]{:S(2)}) collective-permute-start(bf16[2,320,128]{2,1,0:T(8,128)(2,1)S(1)} %shard_map.104.kept_ref), channel_id=1, source_target_pairs={{0,16},{2,18},{4,20},{6,22},{8,24},{10,26},{12,28},{14,30},{16,0},... | collective-permute-start | bytes 491528 | tf_op jit(solution)/shard_map/ppermute | solution.py:247
  72.3 6.1 %collective-permute-start.26 = (bf16[2,320,128]{2,1,0:T(8,128)(2,1)S(1)}, bf16[2,320,128]{2,1,0:T(8,128)(2,1)S(1)}, u32[]{:S(2)}, u32[]{:S(2)}) collective-permute-start(bf16[2,320,128]{2,1,0:T(8,128)(2,1)S(1)} %shard_map.105.refs_4_), channel_id=1, source_target_pairs={{0,8},{2,10},{4,12},{6,14},{8,0},{10,2},{12,4},{14,6},{16,24},{18,... | collective-permute-start | bytes 491528 | tf_op jit(solution)/shard_map/ppermute | solution.py:247
  72.5 9.0 %collective-permute-start.29 = (bf16[2,320,128]{2,1,0:T(8,128)(2,1)S(1)}, bf16[2,320,128]{2,1,0:T(8,128)(2,1)S(1)}, u32[]{:S(2)}, u32[]{:S(2)}) collective-permute-start(bf16[2,320,128]{2,1,0:T(8,128)(2,1)S(1)} %shard_map.105.refs_4_), channel_id=1, source_target_pairs={{0,4},{2,6},{4,0},{6,2},{8,12},{10,14},{12,8},{14,10},{16,20},{18,... | collective-permute-start | bytes 491528 | tf_op jit(solution)/shard_map/ppermute | solution.py:247
  78.4 7.1 %collective-permute-start.28 = (bf16[2,320,128]{2,1,0:T(8,128)(2,1)S(1)}, bf16[2,320,128]{2,1,0:T(8,128)(2,1)S(1)}, u32[]{:S(2)}, u32[]{:S(2)}) collective-permute-start(bf16[2,320,128]{2,1,0:T(8,128)(2,1)S(1)} %collective-permute-done.26.refs_5_), channel_id=1, source_target_pairs={{0,2},{2,0},{4,6},{6,4},{8,10},{10,8},{12,14},{14,12},{16,18},{18,... | collective-permute-start | bytes 491528 | tf_op jit(solution)/shard_map/ppermute | solution.py:247
  79.1 9.7 %collective-permute-start.27 = (bf16[2,320,128]{2,1,0:T(8,128)(2,1)S(1)}, bf16[2,320,128]{2,1,0:T(8,128)(2,1)S(1)}, u32[]{:S(2)}, u32[]{:S(2)}) collective-permute-start(bf16[2,320,128]{2,1,0:T(8,128)(2,1)S(1)} %shard_map.105.refs_4_), channel_id=1, source_target_pairs={{0,2},{2,0},{4,6},{6,4},{8,10},{10,8},{12,14},{14,12},{16,18},{18,... | collective-permute-start | bytes 491528 | tf_op jit(solution)/shard_map/ppermute | solution.py:247
  80.4 10.0 %collective-permute-start.30 = (bf16[2,320,128]{2,1,0:T(8,128)(2,1)S(1)}, bf16[2,320,128]{2,1,0:T(8,128)(2,1)S(1)}, u32[]{:S(2)}, u32[]{:S(2)}) collective-permute-start(bf16[2,320,128]{2,1,0:T(8,128)(2,1)S(1)} %collective-permute-done.26.refs_5_), channel_id=1, source_target_pairs={{0,4},{2,6},{4,0},{6,2},{8,12},{10,14},{12,8},{14,10},{16,20},{18,... | collective-permute-start | bytes 491528 | tf_op jit(solution)/shard_map/ppermute | solution.py:247
  81.4 12.9 %collective-permute-start.31 = (bf16[2,320,128]{2,1,0:T(8,128)(2,1)S(1)}, bf16[2,320,128]{2,1,0:T(8,128)(2,1)S(1)}, u32[]{:S(2)}, u32[]{:S(2)}) collective-permute-start(bf16[2,320,128]{2,1,0:T(8,128)(2,1)S(1)} %collective-permute-done.29.refs_8_), channel_id=1, source_target_pairs={{0,2},{2,0},{4,6},{6,4},{8,10},{10,8},{12,14},{14,12},{16,18},{18,... | collective-permute-start | bytes 491528 | tf_op jit(solution)/shard_map/ppermute | solution.py:247
  85.4 8.9 %collective-permute-start.32 = (bf16[2,320,128]{2,1,0:T(8,128)(2,1)S(1)}, bf16[2,320,128]{2,1,0:T(8,128)(2,1)S(1)}, u32[]{:S(2)}, u32[]{:S(2)}) collective-permute-start(bf16[2,320,128]{2,1,0:T(8,128)(2,1)S(1)} %collective-permute-done.28.refs_7_), channel_id=1, source_target_pairs={{0,4},{2,6},{4,0},{6,2},{8,12},{10,14},{12,8},{14,10},{16,20},{18,... | collective-permute-start | bytes 491528 | tf_op jit(solution)/shard_map/ppermute | solution.py:247
  86.5 7.9 %collective-permute-start.17 = (f32[128,256]{1,0:T(8,128)S(1)}, f32[128,256]{1,0:T(8,128)S(1)}, u32[]{:S(2)}, u32[]{:S(2)}) collective-permute-start(f32[128,256]{1,0:T(8,128)S(1)} %get-tuple-element.26), channel_id=1, source_target_pairs={{0,8},{2,10},{4,12},{6,14},{8,0},{10,2},{12,4},{14,6},{16,24},{18,... | collective-permute-start | bytes 393224 | tf_op jit(solution)/shard_map/ppermute | solution.py:247
  88.8 9.8 %collective-permute-start.18 = (f32[128,256]{1,0:T(8,128)S(1)}, f32[128,256]{1,0:T(8,128)S(1)}, u32[]{:S(2)}, u32[]{:S(2)}) collective-permute-start(f32[128,256]{1,0:T(8,128)S(1)} %get-tuple-element.27), channel_id=1, source_target_pairs={{0,16},{2,18},{4,20},{6,22},{8,24},{10,26},{12,28},{14,30},{16,0},... | collective-permute-start | bytes 393224 | tf_op jit(solution)/shard_map/ppermute | solution.py:247
  90.4 8.2 %collective-permute-start.19 = (f32[128,256]{1,0:T(8,128)S(1)}, f32[128,256]{1,0:T(8,128)S(1)}, u32[]{:S(2)}, u32[]{:S(2)}) collective-permute-start(f32[128,256]{1,0:T(8,128)S(1)} %get-tuple-element.28), channel_id=1, source_target_pairs={{0,24},{2,26},{4,28},{6,30},{8,16},{10,18},{12,20},{14,22},{16,8},... | collective-permute-start | bytes 393224 | tf_op jit(solution)/shard_map/ppermute | solution.py:247

commit v3 on v2

--- a/solution.py
+++ b/solution.py
@@ -35,6 +35,14 @@
         return ids < jnp.where(ids < width, first_rank, second_rank + width)
 
     return kept(rows) & kept(cols)
+
+
+def table_kernel(tiles_ref, *refs):
+    at = 0
+    for bands_ref in refs[:-1]:
+        for b in range(bands_ref.shape[0]):
+            refs[-1][at] = slot_of(tiles_ref, bands_ref[b])
+            at += 1
 
 
 def solve_kernel(ids_ref, *refs, pieces, cols):
@@ -64,14 +72,14 @@
                 out_refs[j][pl.ds(at, rows), :] = values[k]
 
 
-def core_kernel(ids_ref, tiles_ref, *refs, inner, cols, width, first):
+def core_kernel(ids_ref, sources_ref, *refs, inner, cols, width, first):
     bands_refs, s_refs = refs[:cols], refs[cols : cols + 2 * inner]
     out_refs, picked = refs[cols + 2 * inner : -1], refs[-1]
     high, low = ids_ref[0], ids_ref[1]
     per_col = bands_refs[0].shape[0]
     for j in range(cols):
         for b in range(per_col):
-            source = slot_of(tiles_ref, bands_refs[j][b])
+            source = sources_ref[j * per_col + b]
             block = low ^ (source % inner)
             slot = high ^ (source // inner)
             place = (j * per_col + b) * width
@@ -123,11 +131,11 @@
         )
 
 
-def pick_kernel(ids_ref, tiles_ref, *refs, inner, share):
+def pick_kernel(ids_ref, sources_ref, *refs, inner, share):
     bands_refs, t_refs, out_refs = refs[:share], refs[share : share + inner], refs[share + inner :]
     for j in range(share):
         for b in range(bands_refs[j].shape[0]):
-            block = ids_ref[1] ^ (slot_of(tiles_ref, bands_refs[j][b]) % inner)
+            block = ids_ref[1] ^ (sources_ref[j * bands_refs[0].shape[0] + b] % inner)
             for k in range(inner):
 
                 @pl.when(block == k)
@@ -155,9 +163,9 @@
         sent_ref[...] = own_ref[...]
 
 
-def merge_kernel(ids_ref, tiles_ref, bands_ref, kept_ref, got_ref, out_ref, *, inner, bit):
+def merge_kernel(ids_ref, sources_ref, bands_ref, kept_ref, got_ref, out_ref, *, inner, bit):
     for b in range(bands_ref.shape[0]):
-        other = ((slot_of(tiles_ref, bands_ref[b]) // inner) ^ ids_ref[0]) & bit
+        other = ((sources_ref[b] // inner) ^ ids_ref[0]) & bit
 
         @pl.when(other == 0)
         def _():
@@ -178,9 +186,12 @@
     own_tile = tiles_ref[ids_ref[3]]
     own_rank = ranks_ref[own_tile, own_tile]
     quarter = stack.shape[0] // len(pieces)
+    per_col = bands_ref.shape[0]
     rows = lax.broadcasted_iota(jnp.int32, (width, width), 0)
     cols = lax.broadcasted_iota(jnp.int32, (width, width), 1)
-    for b in range(bands_ref.shape[0]):
+    nothing = jnp.zeros((width, width), jnp.bfloat16)
+    lines = []
+    for b in range(per_col):
         band_tile = bands_ref[b]
         lanes = slice(b * width, (b + 1) * width)
         total = part_refs[0][:, lanes]
@@ -189,26 +200,31 @@
         live = (rows < own_rank) & (cols < ranks_ref[band_tile, band_tile])
         live = live & (band_tile < own_tile)
         core_mat = jnp.where(live, total, 0.0).astype(jnp.bfloat16)
-        at = 0
-        for k, count in enumerate(pieces):
-            blocks = max(share, count)
-            size = quarter // blocks
-            for h in range(blocks):
-                part, j = h * count // blocks, h * share // blocks
-                update = lax.dot_general(
-                    q_refs[at + part][b, pl.ds((h - part * blocks // count) * size, size), :],
-                    core_mat,
-                    (((1,), (1,)), ((), ())),
-                    preferred_element_type=jnp.float32,
-                )
-                inside = (flip ^ j) * (quarter // share) + (h - j * blocks // share) * size
-                place = pl.multiple_of((low ^ k) * quarter + inside, 16)
-                stack[pl.ds(place, size), :] = -update.astype(jnp.bfloat16)
-            at += count
-        change = stack[...]
+        lines.append(
+            jnp.concatenate([core_mat if i == b else nothing for i in range(per_col)], axis=1)
+        )
+    core_all = jnp.concatenate(lines, axis=0)
+    at = 0
+    for k, count in enumerate(pieces):
+        blocks = max(share, count)
+        size = quarter // blocks
+        for h in range(blocks):
+            part, j = h * count // blocks, h * share // blocks
+            own = pl.ds((h - part * blocks // count) * size, size)
+            update = lax.dot_general(
+                jnp.concatenate([q_refs[at + part][b, own, :] for b in range(per_col)], axis=1),
+                core_all,
+                (((1,), (1,)), ((), ())),
+                preferred_element_type=jnp.float32,
+            )
+            inside = (flip ^ j) * (quarter // share) + (h - j * blocks // share) * size
+            place = pl.multiple_of((low ^ k) * quarter + inside, 16)
+            stack[pl.ds(place, size), :] = -update.astype(jnp.bfloat16)
+        at += count
+    for b in range(per_col):
+        change = stack[:, b * width : (b + 1) * width]
         both = cross_rows(change, jnp.concatenate([trail_ref[0, b], change], axis=1))
-        rank = ranks_ref[own_tile, band_tile]
-        mixed = jnp.where(cols < rank, both[:, :width], 0.0)
+        mixed = jnp.where(cols < ranks_ref[own_tile, bands_ref[b]], both[:, :width], 0.0)
         out_ref[0, b, :width, :width] = kept_ref[b]
         out_ref[0, b, :width, width:] = mixed.T
         out_ref[0, b, width:, :width] = mixed
@@ -272,6 +288,13 @@
         l_blocks = [linv] + [low_swap(linv, k) for k in range(1, inner)]
         pieces = (1,) * inner
     bands = [band_cols] + [core_swap(band_cols, j) for j in range(1, cols)]
+    sources = pl.pallas_call(
+        table_kernel,
+        out_shape=jax.ShapeDtypeStruct((cols * per_col,), jnp.int32),
+        in_specs=[SMEM] * (1 + cols),
+        out_specs=SMEM,
+        name="table",
+    )(tile_of_slot, *bands)
 
     gram_left, gram_kept = call(
         functools.partial(left_kernel, width=width),
@@ -296,7 +319,7 @@
     picked = call(
         functools.partial(pick_kernel, inner=inner, share=share),
         [pltpu.VMEM((per_col, size, width), bf16)] * share,
-        (ids, tile_of_slot, *bands[:share]),
+        (ids, sources, *bands[:share]),
         t_blocks,
     )
 
@@ -304,7 +327,7 @@
         return call(
             functools.partial(merge_kernel, inner=inner, bit=bit),
             pltpu.VMEM(kept.shape, bf16),
-            (ids, tile_of_slot, band_cols),
+            (ids, sources, band_cols),
             (kept, got),
         )
 
@@ -352,7 +375,7 @@
     cores = call(
         functools.partial(core_kernel, inner=inner, cols=cols, width=width, first=early),
         [pltpu.VMEM((outer * width, per_col * width), f32)] * cols,
-        (ids, tile_of_slot, *bands),
+        (ids, sources, *bands),
         [block for pair in zip(*solved_blocks) for block in pair],
         [pltpu.VMEM((kept_rows, cols * per_col * width), bf16)],
     )
@@ -369,7 +392,7 @@
         jax.ShapeDtypeStruct((1, per_col, 2 * width, 2 * width), f32),
         (ids, tile_of_slot, rank_map, band_cols),
         (*core_parts, *base_blocks, gram_kept, trail_v),
-        [pltpu.VMEM((points, width), bf16)],
+        [pltpu.VMEM((points, per_col * width), bf16)],
     )
     return gram_left, gram_right
 

time: 102 us -> 104 us (1.020)
  local copies, waits for them, and re-layouts: 2.15 us -> 4.1 us
  Pallas kernels: 14.2 us -> 16.1 us
  waiting for transfers between devices: 45.3 us -> 43.7 us
    ppermute x28, waiting for transfers between devices: 39.8 us -> 38.1 us  [swap(): return lax.ppermute(x, axis, [(i, i ^ distance) for i in range(count)])]
    unnamed x18 -> x26, local copies, waits for them, and re-layouts: 2 us -> 3.27 us
    pallas_call x0 -> x1, Pallas kernels: none -> 1.24 us  [shards(): pl.pallas_call(table_kernel, out_shape=jax.ShapeDtypeStruct((cols * per_c...]
  transfers between devices with their start and end apart: 33 -> 33, of which waited for: 11 -> 9; matrix products, arithmetic and copies ran while one was open for 0% -> 1% of each run, Pallas kernels for 11% -> 13%
where the time goes in v3:
time: 104 us
  waiting for transfers between devices  43.7 us (42%)
  starting transfers between devices  38.8 us (37%)
  Pallas kernels  16.1 us (15%)
  local copies, waits for them, and re-layouts  4.1 us (4%)
    ppermute x28, waiting for transfers between devices, swap(): return lax.ppermute(x, axis, [(i, i ^ distance) for i in range(count)])  38.1 us
    ppermute x28, starting transfers between devices, swap(): return lax.ppermute(x, axis, [(i, i ^ distance) for i in range(count)])  30.7 us
    pallas_call x12, Pallas kernels, call(): pl.pallas_call(kernel, out_shape=outs, in_specs=[SMEM] * len(scalars) + [...  14.9 us
    ppermute x3, waiting for transfers between devices, shards(): lax.ppermute(v_blocks[m ^ low_bit], 'row', [(r, r ^ low_bit * inner) for...  5.56 us
    ppermute x3, starting transfers between devices, shards(): lax.ppermute(v_blocks[m ^ low_bit], 'row', [(r, r ^ low_bit * inner) for...  4.74 us
    unnamed x26, local copies, waits for them, and re-layouts  3.27 us
  transfers between devices with their start and end apart: 33, of which 9 were waited for; matrix products, arithmetic and copies ran while one was open for 1% of the time, Pallas kernels for 13%

profile of v3, /device:TPU:0, one launch (start us, length us, event | category | flops | bytes accessed | tf_op | source)
XLA Modules:
  0.0 103.6 jit_solution(13618499132061827573)
XLA Ops:
  0.6 3.1 %collective-permute-start.2 = (bf16[160,1280]{1,0:T(8,128)(2,1)}, bf16[160,1280]{1,0:T(8,128)(2,1)S(1)}, u32[]{:S(2)}, u32[]{:S(2)}) collective-permute-start(bf16[160,1280]{1,0:T(8,128)(2,1)} %refs_0_.7), channel_id=1, source_target_pairs={{0,4},{2,6},{4,0},{6,2},{8,12},{10,14},{12,8},{14,10},{16,20},{18,... | collective-permute-start | bytes 1228808 | tf_op jit(solution)/shard_map/ppermute | solution.py:263
  3.7 1.5 %collective-permute-start.1 = (bf16[160,1280]{1,0:T(8,128)(2,1)}, bf16[160,1280]{1,0:T(8,128)(2,1)S(1)}, u32[]{:S(2)}, u32[]{:S(2)}) collective-permute-start(bf16[160,1280]{1,0:T(8,128)(2,1)} %refs_0_.7), channel_id=1, source_target_pairs={{0,2},{2,0},{4,6},{6,4},{8,10},{10,8},{12,14},{14,12},{16,18},{18,... | collective-permute-start | bytes 1228808 | tf_op jit(solution)/shard_map/ppermute | solution.py:263
  5.2 2.6 %collective-permute-start.6 = (bf16[1280,128]{1,0:T(8,128)(2,1)}, bf16[1280,128]{1,0:T(8,128)(2,1)}, u32[]{:S(2)}, u32[]{:S(2)}) collective-permute-start(bf16[1280,128]{1,0:T(8,128)(2,1)} %bitcast.14), channel_id=1, source_target_pairs={{0,16},{2,18},{4,20},{6,22},{8,24},{10,26},{12,28},{14,30},{16,0},... | collective-permute-start | bytes 983048 | tf_op jit(solution)/shard_map/ppermute | solution.py:277
  7.8 1.6 %collective-permute-start.5 = (bf16[1280,128]{1,0:T(8,128)(2,1)}, bf16[1280,128]{1,0:T(8,128)(2,1)S(1)}, u32[]{:S(2)}, u32[]{:S(2)}) collective-permute-start(bf16[1280,128]{1,0:T(8,128)(2,1)} %bitcast.15), channel_id=1, source_target_pairs={{0,8},{2,10},{4,12},{6,14},{8,0},{10,2},{12,4},{14,6},{16,24},{18,... | collective-permute-start | bytes 983048 | tf_op jit(solution)/shard_map/ppermute | solution.py:277
  9.3 4.0 %collective-permute-done.2.refs_2_ = bf16[160,1280]{1,0:T(8,128)(2,1)S(1)} collective-permute-done((bf16[160,1280]{1,0:T(8,128)(2,1)}, bf16[160,1280]{1,0:T(8,128)(2,1)S(1)}, u32[]{:S(2)}, u32[]{:S(2)}) %collective-permute-start.2) | collective-permute-done | bytes 409632 | tf_op jit(solution)/shard_map/ppermute | solution.py:263
  13.4 1.8 %collective-permute-start.3 = (bf16[80,1280]{1,0:T(8,128)(2,1)S(1)}, bf16[80,1280]{1,0:T(8,128)(2,1)S(1)}, u32[]{:S(2)}, u32[]{:S(2)}) collective-permute-start(bf16[80,1280]{1,0:T(8,128)(2,1)S(1)} %slice.8), channel_id=1, source_target_pairs={{0,2},{2,0},{4,6},{6,4},{8,10},{10,8},{12,14},{14,12},{16,18},{18,... | collective-permute-start | bytes 614408 | tf_op jit(solution)/shard_map/ppermute | solution.py:283
  15.2 1.6 %collective-permute-start.4 = (bf16[80,1280]{1,0:T(8,128)(2,1)S(1)}, bf16[80,1280]{1,0:T(8,128)(2,1)S(1)}, u32[]{:S(2)}, u32[]{:S(2)}) collective-permute-start(bf16[80,1280]{1,0:T(8,128)(2,1)S(1)} %slice.9), channel_id=1, source_target_pairs={{0,4},{2,6},{4,0},{6,2},{8,12},{10,14},{12,8},{14,10},{16,20},{18,... | collective-permute-start | bytes 614408 | tf_op jit(solution)/shard_map/ppermute | solution.py:284
  16.9 5.6 %collective-permute-done.6.refs_7_ = bf16[1280,128]{1,0:T(8,128)(2,1)} collective-permute-done((bf16[1280,128]{1,0:T(8,128)(2,1)}, bf16[1280,128]{1,0:T(8,128)(2,1)}, u32[]{:S(2)}, u32[]{:S(2)}) %collective-permute-start.6) | collective-permute-done | bytes 327712 | tf_op jit(solution)/shard_map/ppermute | solution.py:277
  22.4 0.6 collective-permute-start.8
  23.0 1.0 copy-done.1
  24.0 1.0 copy-done.5
  25.0 3.0 %shard_map.96 = (f32[320,384]{1,0:T(8,128)S(1)}, f32[320,384]{1,0:T(8,128)}) custom-call(s32[5]{0:T(128)S(1)} %stack.23.ids_ref, bf16[160,1280]{1,0:T(8,128)(2,1)S(1)} %copy-done.1, bf16[160,1280]{1,0:T(8,128)(2,1)S(1)} %collective-permute-done.1.refs_1_, bf16[160,1280]{1,0:T(8,128)(2,1)S(1)} %collective-permute-done.2.refs_2_, ...), custom_call_target="tpu_custom_call" | custom-call | tf_op jit(solution)/shard_map/pallas_call | solution.py:235
  27.9 0.7 dynamic-slice_bitcast_fusion
  29.7 2.4 %collective-permute-start.22 = (bf16[320,128]{1,0:T(8,128)(2,1)}, bf16[320,128]{1,0:T(8,128)(2,1)}, u32[]{:S(2)}, u32[]{:S(2)}) collective-permute-start(bf16[320,128]{1,0:T(8,128)(2,1)} %get-tuple-element.34), channel_id=1, source_target_pairs={{0,6},{2,4},{4,2},{6,0},{8,14},{10,12},{12,10},{14,8},{16,22},{18,... | collective-permute-start | bytes 245768 | tf_op jit(solution)/shard_map/ppermute | solution.py:263
  32.2 2.3 %shard_map.98 = (f32[320,128]{1,0:T(8,128)S(1)}, f32[320,128]{1,0:T(8,128)}) custom-call(s32[5]{0:T(128)S(1)} %stack.23.ids_ref, bf16[160,1280]{1,0:T(8,128)(2,1)S(1)} %copy-done.2, bf16[160,1280]{1,0:T(8,128)(2,1)S(1)} %collective-permute-done.1.refs_1_, bf16[160,1280]{1,0:T(8,128)(2,1)S(1)} %collective-permute-done.2.refs_2_, ...), custom_call_target="tpu_custom_call" | custom-call | tf_op jit(solution)/shard_map/pallas_call | solution.py:235
  35.0 1.2 %table.1.sources_ref = s32[4]{0:T(128)} custom-call(s32[16]{0:T(128)} %tiles_ref.5, s32[2]{0:T(128)} %bands_ref.7, s32[2]{0:T(128)} %copy-done.10), custom_call_target="tpu_custom_call" | custom-call | tf_op jit(solution)/shard_map/table/pallas_call | solution.py:291
  36.3 0.7 copy-done.9
  36.9 0.6 copy-done.11
  37.5 1.1 %shard_map.102 = (bf16[2,320,128]{2,1,0:T(8,128)(2,1)S(1)}, bf16[2,320,128]{2,1,0:T(8,128)(2,1)S(1)}) custom-call(s32[5]{0:T(128)S(1)} %stack.23.ids_ref, s32[4]{0:T(128)S(1)} %copy-done.9, s32[2]{0:T(128)S(1)} %copy-done.8, s32[2]{0:T(128)S(1)} %copy-done.11, bf16[320,128]{1,0:T(8,128)(2,1)S(1)} %get-tuple-element.36.refs_2_, ...), custom_call_target="tpu_custom_call" | custom-call | tf_op jit(solution)/shard_map/pallas_call | solution.py:235
  39.2 0.7 collective-permute-start.10
  39.9 1.0 %collective-permute-start.12 = (bf16[320,384]{1,0:T(8,128)(2,1)S(1)}, bf16[320,384]{1,0:T(8,128)(2,1)S(1)}, u32[]{:S(2)}, u32[]{:S(2)}) collective-permute-start(bf16[320,384]{1,0:T(8,128)(2,1)S(1)} %shard_map.97.refs_2_), channel_id=1, source_target_pairs={{0,4},{2,6},{4,0},{6,2},{8,12},{10,14},{12,8},{14,10},{16,20},{18,... | collective-permute-start | bytes 737288 | tf_op jit(solution)/shard_map/ppermute | solution.py:263
  40.9 1.8 %collective-permute-start.14 = (bf16[320,384]{1,0:T(8,128)(2,1)S(1)}, bf16[320,384]{1,0:T(8,128)(2,1)S(1)}, u32[]{:S(2)}, u32[]{:S(2)}) collective-permute-start(bf16[320,384]{1,0:T(8,128)(2,1)S(1)} %shard_map.97.refs_2_), channel_id=1, source_target_pairs={{0,6},{2,4},{4,2},{6,0},{8,14},{10,12},{12,10},{14,8},{16,22},{18,... | collective-permute-start | bytes 737288 | tf_op jit(solution)/shard_map/ppermute | solution.py:263
  42.8 0.7 collective-permute-start.11
  43.5 1.0 %collective-permute-start.13 = (bf16[320,128]{1,0:T(8,128)(2,1)S(1)}, bf16[320,128]{1,0:T(8,128)(2,1)S(1)}, u32[]{:S(2)}, u32[]{:S(2)}) collective-permute-start(bf16[320,128]{1,0:T(8,128)(2,1)S(1)} %shard_map.99.refs_3_), channel_id=1, source_target_pairs={{0,4},{2,6},{4,0},{6,2},{8,12},{10,14},{12,8},{14,10},{16,20},{18,... | collective-permute-start | bytes 245768 | tf_op jit(solution)/shard_map/ppermute | solution.py:263
  45.1 9.1 %collective-permute-done.11.refs_5_ = bf16[320,128]{1,0:T(8,128)(2,1)S(1)} collective-permute-done((bf16[320,128]{1,0:T(8,128)(2,1)S(1)}, bf16[320,128]{1,0:T(8,128)(2,1)S(1)}, u32[]{:S(2)}, u32[]{:S(2)}) %collective-permute-start.11) | collective-permute-done | bytes 81952 | tf_op jit(solution)/shard_map/ppermute | solution.py:263
  54.3 1.5 %collective-permute-start.24 = (bf16[2,320,128]{2,1,0:T(8,128)(2,1)S(1)}, bf16[2,320,128]{2,1,0:T(8,128)(2,1)S(1)}, u32[]{:S(2)}, u32[]{:S(2)}) collective-permute-start(bf16[2,320,128]{2,1,0:T(8,128)(2,1)S(1)} %get-tuple-element.32), channel_id=1, source_target_pairs={{0,8},{2,10},{4,12},{6,14},{8,0},{10,2},{12,4},{14,6},{16,24},{18,... | collective-permute-start | bytes 491528 | tf_op jit(solution)/shard_map/ppermute | solution.py:263
  55.7 1.5 %collective-permute-start.15 = (bf16[320,128]{1,0:T(8,128)(2,1)S(1)}, bf16[320,128]{1,0:T(8,128)(2,1)S(1)}, u32[]{:S(2)}, u32[]{:S(2)}) collective-permute-start(bf16[320,128]{1,0:T(8,128)(2,1)S(1)} %shard_map.99.refs_3_), channel_id=1, source_target_pairs={{0,6},{2,4},{4,2},{6,0},{8,14},{10,12},{12,10},{14,8},{16,22},{18,... | collective-permute-start | bytes 245768 | tf_op jit(solution)/shard_map/ppermute | solution.py:263
  57.3 3.8 %collective-permute-done.15.refs_9_ = bf16[320,128]{1,0:T(8,128)(2,1)S(1)} collective-permute-done((bf16[320,128]{1,0:T(8,128)(2,1)S(1)}, bf16[320,128]{1,0:T(8,128)(2,1)S(1)}, u32[]{:S(2)}, u32[]{:S(2)}) %collective-permute-start.15) | collective-permute-done | bytes 81952 | tf_op jit(solution)/shard_map/ppermute | solution.py:263
  61.1 1.3 %shard_map.100 = (f32[512,256]{1,0:T(8,128)S(1)}, f32[512,256]{1,0:T(8,128)S(1)}) custom-call(s32[5]{0:T(128)S(1)} %stack.23.ids_ref, s32[4]{0:T(128)S(1)} %copy-done.9, s32[2]{0:T(128)S(1)} %copy-done.8, s32[2]{0:T(128)S(1)} %copy-done.11, bf16[320,384]{1,0:T(8,128)(2,1)S(1)} %shard_map.97.refs_2_, bf16[320,128]{1,0:T(8,128)(2,1)S(1)} %shard_map.99.refs_3_, ...), custom_call_target="tpu_custom_call" | custom-call | tf_op jit(solution)/shard_map/pallas_call | solution.py:235
  62.5 0.6 shard_map.104.kept_ref
  63.1 2.8 %collective-permute-start.25 = (bf16[2,320,128]{2,1,0:T(8,128)(2,1)S(1)}, bf16[2,320,128]{2,1,0:T(8,128)(2,1)S(1)}, u32[]{:S(2)}, u32[]{:S(2)}) collective-permute-start(bf16[2,320,128]{2,1,0:T(8,128)(2,1)S(1)} %shard_map.104.kept_ref), channel_id=1, source_target_pairs={{0,16},{2,18},{4,20},{6,22},{8,24},{10,26},{12,28},{14,30},{16,0},... | collective-permute-start | bytes 491528 | tf_op jit(solution)/shard_map/ppermute | solution.py:263
  65.9 8.4 %collective-permute-done.25.got_ref = bf16[2,320,128]{2,1,0:T(8,128)(2,1)S(1)} collective-permute-done((bf16[2,320,128]{2,1,0:T(8,128)(2,1)S(1)}, bf16[2,320,128]{2,1,0:T(8,128)(2,1)S(1)}, u32[]{:S(2)}, u32[]{:S(2)}) %collective-permute-start.25) | collective-permute-done | bytes 163872 | tf_op jit(solution)/shard_map/ppermute | solution.py:263
  74.2 0.6 shard_map.105.refs_4_
  74.8 0.6 collective-permute-start.26
  75.4 0.8 collective-permute-start.29
  76.2 4.5 %collective-permute-done.26.refs_5_ = bf16[2,320,128]{2,1,0:T(8,128)(2,1)S(1)} collective-permute-done((bf16[2,320,128]{2,1,0:T(8,128)(2,1)S(1)}, bf16[2,320,128]{2,1,0:T(8,128)(2,1)S(1)}, u32[]{:S(2)}, u32[]{:S(2)}) %collective-permute-start.26) | collective-permute-done | bytes 163872 | tf_op jit(solution)/shard_map/ppermute | solution.py:263
  80.7 1.0 collective-permute-start.28
  81.6 1.1 %collective-permute-start.27 = (bf16[2,320,128]{2,1,0:T(8,128)(2,1)S(1)}, bf16[2,320,128]{2,1,0:T(8,128)(2,1)S(1)}, u32[]{:S(2)}, u32[]{:S(2)}) collective-permute-start(bf16[2,320,128]{2,1,0:T(8,128)(2,1)S(1)} %shard_map.105.refs_4_), channel_id=1, source_target_pairs={{0,2},{2,0},{4,6},{6,4},{8,10},{10,8},{12,14},{14,12},{16,18},{18,... | collective-permute-start | bytes 491528 | tf_op jit(solution)/shard_map/ppermute | solution.py:263
  82.7 1.2 %collective-permute-start.30 = (bf16[2,320,128]{2,1,0:T(8,128)(2,1)S(1)}, bf16[2,320,128]{2,1,0:T(8,128)(2,1)S(1)}, u32[]{:S(2)}, u32[]{:S(2)}) collective-permute-start(bf16[2,320,128]{2,1,0:T(8,128)(2,1)S(1)} %collective-permute-done.26.refs_5_), channel_id=1, source_target_pairs={{0,4},{2,6},{4,0},{6,2},{8,12},{10,14},{12,8},{14,10},{16,20},{18,... | collective-permute-start | bytes 491528 | tf_op jit(solution)/shard_map/ppermute | solution.py:263
  83.9 0.8 collective-permute-start.31
  84.7 3.0 %collective-permute-done.28.refs_7_ = bf16[2,320,128]{2,1,0:T(8,128)(2,1)S(1)} collective-permute-done((bf16[2,320,128]{2,1,0:T(8,128)(2,1)S(1)}, bf16[2,320,128]{2,1,0:T(8,128)(2,1)S(1)}, u32[]{:S(2)}, u32[]{:S(2)}) %collective-permute-start.28) | collective-permute-done | bytes 163872 | tf_op jit(solution)/shard_map/ppermute | solution.py:263
  87.8 1.2 %collective-permute-start.32 = (bf16[2,320,128]{2,1,0:T(8,128)(2,1)S(1)}, bf16[2,320,128]{2,1,0:T(8,128)(2,1)S(1)}, u32[]{:S(2)}, u32[]{:S(2)}) collective-permute-start(bf16[2,320,128]{2,1,0:T(8,128)(2,1)S(1)} %collective-permute-done.28.refs_7_), channel_id=1, source_target_pairs={{0,4},{2,6},{4,0},{6,2},{8,12},{10,14},{12,8},{14,10},{16,20},{18,... | collective-permute-start | bytes 491528 | tf_op jit(solution)/shard_map/ppermute | solution.py:263
  89.4 1.5 %collective-permute-done.27.refs_6_ = bf16[2,320,128]{2,1,0:T(8,128)(2,1)S(1)} collective-permute-done((bf16[2,320,128]{2,1,0:T(8,128)(2,1)S(1)}, bf16[2,320,128]{2,1,0:T(8,128)(2,1)S(1)}, u32[]{:S(2)}, u32[]{:S(2)}) %collective-permute-start.27) | collective-permute-done | bytes 163872 | tf_op jit(solution)/shard_map/ppermute | solution.py:263
  90.9 2.7 %collective-permute-start.18 = (f32[128,256]{1,0:T(8,128)S(1)}, f32[128,256]{1,0:T(8,128)S(1)}, u32[]{:S(2)}, u32[]{:S(2)}) collective-permute-start(f32[128,256]{1,0:T(8,128)S(1)} %get-tuple-element.27), channel_id=1, source_target_pairs={{0,16},{2,18},{4,20},{6,22},{8,24},{10,26},{12,28},{14,30},{16,0},... | collective-permute-start | bytes 393224 | tf_op jit(solution)/shard_map/ppermute | solution.py:263
  93.6 0.9 collective-permute-start.19
  94.5 2.7 %shard_map.95 = (f32[1,2,256,256]{3,2,1,0:T(8,128)}, f32[2,128,128]{2,1,0:T(8,128)S(1)}) custom-call(s32[5]{0:T(128)S(1)} %stack.23.ids_ref, s32[16]{0:T(128)S(1)} %copy-done.12, s32[16,16]{1,0:T(8,128)S(1)} %copy-done.6, s32[2]{0:T(128)S(1)} %copy-done.8, bf16[1,2,2560,128]{3,2,1,0:T(8,128)(2,1)S(1)} %copy-done.4, bf16[1,2560,128]{2,1,0:T(8,128)(2,1)S(1)} %copy-done.3, ...), custom_call_target="tpu_custom_call" | custom-call | tf_op jit(solution)/shard_map/pallas_call | solution.py:235
  97.2 3.7 %collective-permute-done.18.refs_2_ = f32[128,256]{1,0:T(8,128)S(1)} collective-permute-done((f32[128,256]{1,0:T(8,128)S(1)}, f32[128,256]{1,0:T(8,128)S(1)}, u32[]{:S(2)}, u32[]{:S(2)}) %collective-permute-start.18) | collective-permute-done | bytes 131104 | tf_op jit(solution)/shard_map/ppermute | solution.py:263
  100.9 2.7 %shard_map.106 = f32[1,2,256,256]{3,2,1,0:T(8,128)} custom-call(s32[5]{0:T(128)S(1)} %stack.23.ids_ref, s32[16]{0:T(128)S(1)} %copy-done.12, s32[16,16]{1,0:T(8,128)S(1)} %copy-done.6, s32[2]{0:T(128)S(1)} %copy-done.8, f32[128,256]{1,0:T(8,128)S(1)} %get-tuple-element.25.refs_0_, f32[128,256]{1,0:T(8,128)S(1)} %collective-permute-done.17.refs_1_, ...), custom_call_target="tpu_custom_call" | custom-call | tf_op jit(solution)/shard_map/pallas_call | solution.py:235
  (61 shorter events, 3.5 us)
Async XLA Ops:
  0.6 12.7 %collective-permute-start.2 = (bf16[160,1280]{1,0:T(8,128)(2,1)}, bf16[160,1280]{1,0:T(8,128)(2,1)S(1)}, u32[]{:S(2)}, u32[]{:S(2)}) collective-permute-start(bf16[160,1280]{1,0:T(8,128)(2,1)} %refs_0_.7), channel_id=1, source_target_pairs={{0,4},{2,6},{4,0},{6,2},{8,12},{10,14},{12,8},{14,10},{16,20},{18,... | collective-permute-start | bytes 1228808 | tf_op jit(solution)/shard_map/ppermute | solution.py:263
  3.7 11.5 %collective-permute-start.1 = (bf16[160,1280]{1,0:T(8,128)(2,1)}, bf16[160,1280]{1,0:T(8,128)(2,1)S(1)}, u32[]{:S(2)}, u32[]{:S(2)}) collective-permute-start(bf16[160,1280]{1,0:T(8,128)(2,1)} %refs_0_.7), channel_id=1, source_target_pairs={{0,2},{2,0},{4,6},{6,4},{8,10},{10,8},{12,14},{14,12},{16,18},{18,... | collective-permute-start | bytes 1228808 | tf_op jit(solution)/shard_map/ppermute | solution.py:263
  5.2 17.2 %collective-permute-start.6 = (bf16[1280,128]{1,0:T(8,128)(2,1)}, bf16[1280,128]{1,0:T(8,128)(2,1)}, u32[]{:S(2)}, u32[]{:S(2)}) collective-permute-start(bf16[1280,128]{1,0:T(8,128)(2,1)} %bitcast.14), channel_id=1, source_target_pairs={{0,16},{2,18},{4,20},{6,22},{8,24},{10,26},{12,28},{14,30},{16,0},... | collective-permute-start | bytes 983048 | tf_op jit(solution)/shard_map/ppermute | solution.py:277
  7.8 15.2 %collective-permute-start.5 = (bf16[1280,128]{1,0:T(8,128)(2,1)}, bf16[1280,128]{1,0:T(8,128)(2,1)S(1)}, u32[]{:S(2)}, u32[]{:S(2)}) collective-permute-start(bf16[1280,128]{1,0:T(8,128)(2,1)} %bitcast.15), channel_id=1, source_target_pairs={{0,8},{2,10},{4,12},{6,14},{8,0},{10,2},{12,4},{14,6},{16,24},{18,... | collective-permute-start | bytes 983048 | tf_op jit(solution)/shard_map/ppermute | solution.py:277
  13.4 9.6 %collective-permute-start.3 = (bf16[80,1280]{1,0:T(8,128)(2,1)S(1)}, bf16[80,1280]{1,0:T(8,128)(2,1)S(1)}, u32[]{:S(2)}, u32[]{:S(2)}) collective-permute-start(bf16[80,1280]{1,0:T(8,128)(2,1)S(1)} %slice.8), channel_id=1, source_target_pairs={{0,2},{2,0},{4,6},{6,4},{8,10},{10,8},{12,14},{14,12},{16,18},{18,... | collective-permute-start | bytes 614408 | tf_op jit(solution)/shard_map/ppermute | solution.py:283
  15.2 7.8 %collective-permute-start.4 = (bf16[80,1280]{1,0:T(8,128)(2,1)S(1)}, bf16[80,1280]{1,0:T(8,128)(2,1)S(1)}, u32[]{:S(2)}, u32[]{:S(2)}) collective-permute-start(bf16[80,1280]{1,0:T(8,128)(2,1)S(1)} %slice.9), channel_id=1, source_target_pairs={{0,4},{2,6},{4,0},{6,2},{8,12},{10,14},{12,8},{14,10},{16,20},{18,... | collective-permute-start | bytes 614408 | tf_op jit(solution)/shard_map/ppermute | solution.py:284
  16.8 15.4 %copy-start.7 = (s32[2]{0:T(128)S(1)}, s32[2]{0:T(128)}, u32[]{:S(2)}) copy-start(s32[2]{0:T(128)} %bands_ref.7) | copy-start | bytes 28
  22.4 9.8 %collective-permute-start.8 = (bf16[1280,128]{1,0:T(8,128)(2,1)}, bf16[1280,128]{1,0:T(8,128)(2,1)}, u32[]{:S(2)}, u32[]{:S(2)}) collective-permute-start(bf16[1280,128]{1,0:T(8,128)(2,1)} %collective-permute-done.6.refs_7_), channel_id=1, source_target_pairs={{0,8},{2,10},{4,12},{6,14},{8,0},{10,2},{12,4},{14,6},{16,24},{18,... | collective-permute-start | bytes 983048 | tf_op jit(solution)/shard_map/ppermute | solution.py:277
  23.0 1.0 copy-start.1
  24.0 1.0 copy-start.5
  25.0 3.0 %copy-start.3 = (bf16[1,2560,128]{2,1,0:T(8,128)(2,1)S(1)}, bf16[1,2560,128]{2,1,0:T(8,128)(2,1)}, u32[]{:S(2)}) copy-start(bf16[1,2560,128]{2,1,0:T(8,128)(2,1)} %panel_ref.1) | copy-start | bytes 1966084
  25.0 7.2 %copy-start.2 = (bf16[160,1280]{1,0:T(8,128)(2,1)S(1)}, bf16[160,1280]{1,0:T(8,128)(2,1)}, u32[]{:S(2)}) copy-start(bf16[160,1280]{1,0:T(8,128)(2,1)} %refs_0_.7) | copy-start | bytes 1228804
  27.9 11.3 %collective-permute-start.7 = (f32[320,384]{1,0:T(8,128)}, f32[320,384]{1,0:T(8,128)S(1)}, u32[]{:S(2)}, u32[]{:S(2)}) collective-permute-start(f32[320,384]{1,0:T(8,128)} %get-tuple-element.20), channel_id=1, source_target_pairs={{0,1},{1,0},{2,3},{3,2},{4,5},{5,4},{6,7},{7,6},{8,9},{9,8},{10,11... | collective-permute-start | bytes 1474568 | tf_op jit(solution)/shard_map/ppermute | solution.py:263
  27.9 8.3 %copy-start.8 = (s32[2]{0:T(128)S(1)}, s32[2]{0:T(128)}, u32[]{:S(2)}) copy-start(s32[2]{0:T(128)} %bands_ref.7) | copy-start | bytes 28
  28.7 7.6 %collective-permute-start.20 = (bf16[320,128]{1,0:T(8,128)(2,1)}, bf16[320,128]{1,0:T(8,128)(2,1)}, u32[]{:S(2)}, u32[]{:S(2)}) collective-permute-start(bf16[320,128]{1,0:T(8,128)(2,1)} %get-tuple-element.35), channel_id=1, source_target_pairs={{0,2},{2,0},{4,6},{6,4},{8,10},{10,8},{12,14},{14,12},{16,18},{18,... | collective-permute-start | bytes 245768 | tf_op jit(solution)/shard_map/ppermute | solution.py:263
  29.2 7.0 %collective-permute-start.21 = (bf16[320,128]{1,0:T(8,128)(2,1)}, bf16[320,128]{1,0:T(8,128)(2,1)}, u32[]{:S(2)}, u32[]{:S(2)}) collective-permute-start(bf16[320,128]{1,0:T(8,128)(2,1)} %get-tuple-element.37), channel_id=1, source_target_pairs={{0,4},{2,6},{4,0},{6,2},{8,12},{10,14},{12,8},{14,10},{16,20},{18,... | collective-permute-start | bytes 245768 | tf_op jit(solution)/shard_map/ppermute | solution.py:263
  29.7 6.5 %collective-permute-start.22 = (bf16[320,128]{1,0:T(8,128)(2,1)}, bf16[320,128]{1,0:T(8,128)(2,1)}, u32[]{:S(2)}, u32[]{:S(2)}) collective-permute-start(bf16[320,128]{1,0:T(8,128)(2,1)} %get-tuple-element.34), channel_id=1, source_target_pairs={{0,6},{2,4},{4,2},{6,0},{8,14},{10,12},{12,10},{14,8},{16,22},{18,... | collective-permute-start | bytes 245768 | tf_op jit(solution)/shard_map/ppermute | solution.py:263
  32.2 2.3 %collective-permute-start = (s32[2]{0:T(128)S(1)}, s32[2]{0:T(128)S(1)}, u32[]{:S(2)}, u32[]{:S(2)}) collective-permute-start(s32[2]{0:T(128)S(1)} %copy-done.7), channel_id=1, source_target_pairs={{0,1},{1,0},{2,3},{3,2},{4,5},{5,4},{6,7},{7,6},{8,9},{9,8},{10,11... | collective-permute-start | bytes 32 | tf_op jit(solution)/shard_map/ppermute | solution.py:263
  34.5 0.5 copy-start.10
  34.5 8.3 %collective-permute-start.9 = (f32[320,128]{1,0:T(8,128)}, f32[320,128]{1,0:T(8,128)S(1)}, u32[]{:S(2)}, u32[]{:S(2)}) collective-permute-start(f32[320,128]{1,0:T(8,128)} %get-tuple-element.22), channel_id=1, source_target_pairs={{0,1},{1,0},{2,3},{3,2},{4,5},{5,4},{6,7},{7,6},{8,9},{9,8},{10,11... | collective-permute-start | bytes 491528 | tf_op jit(solution)/shard_map/ppermute | solution.py:263
  36.3 0.7 copy-start.9
  36.9 0.6 copy-start.11
  38.6 4.9 %collective-permute-start.23 = (bf16[2,320,128]{2,1,0:T(8,128)(2,1)S(1)}, bf16[2,320,128]{2,1,0:T(8,128)(2,1)S(1)}, u32[]{:S(2)}, u32[]{:S(2)}) collective-permute-start(bf16[2,320,128]{2,1,0:T(8,128)(2,1)S(1)} %get-tuple-element.30), channel_id=1, source_target_pairs={{0,1},{1,0},{2,3},{3,2},{4,5},{5,4},{6,7},{7,6},{8,9},{9,8},{10,11... | collective-permute-start | bytes 491528 | tf_op jit(solution)/shard_map/ppermute | solution.py:263
  39.2 21.8 %collective-permute-start.10 = (bf16[320,384]{1,0:T(8,128)(2,1)S(1)}, bf16[320,384]{1,0:T(8,128)(2,1)S(1)}, u32[]{:S(2)}, u32[]{:S(2)}) collective-permute-start(bf16[320,384]{1,0:T(8,128)(2,1)S(1)} %shard_map.97.refs_2_), channel_id=1, source_target_pairs={{0,2},{2,0},{4,6},{6,4},{8,10},{10,8},{12,14},{14,12},{16,18},{18,... | collective-permute-start | bytes 737288 | tf_op jit(solution)/shard_map/ppermute | solution.py:263
  39.9 21.2 %collective-permute-start.12 = (bf16[320,384]{1,0:T(8,128)(2,1)S(1)}, bf16[320,384]{1,0:T(8,128)(2,1)S(1)}, u32[]{:S(2)}, u32[]{:S(2)}) collective-permute-start(bf16[320,384]{1,0:T(8,128)(2,1)S(1)} %shard_map.97.refs_2_), channel_id=1, source_target_pairs={{0,4},{2,6},{4,0},{6,2},{8,12},{10,14},{12,8},{14,10},{16,20},{18,... | collective-permute-start | bytes 737288 | tf_op jit(solution)/shard_map/ppermute | solution.py:263
  40.9 20.1 %collective-permute-start.14 = (bf16[320,384]{1,0:T(8,128)(2,1)S(1)}, bf16[320,384]{1,0:T(8,128)(2,1)S(1)}, u32[]{:S(2)}, u32[]{:S(2)}) collective-permute-start(bf16[320,384]{1,0:T(8,128)(2,1)S(1)} %shard_map.97.refs_2_), channel_id=1, source_target_pairs={{0,6},{2,4},{4,2},{6,0},{8,14},{10,12},{12,10},{14,8},{16,22},{18,... | collective-permute-start | bytes 737288 | tf_op jit(solution)/shard_map/ppermute | solution.py:263
  42.8 11.4 %collective-permute-start.11 = (bf16[320,128]{1,0:T(8,128)(2,1)S(1)}, bf16[320,128]{1,0:T(8,128)(2,1)S(1)}, u32[]{:S(2)}, u32[]{:S(2)}) collective-permute-start(bf16[320,128]{1,0:T(8,128)(2,1)S(1)} %shard_map.99.refs_3_), channel_id=1, source_target_pairs={{0,2},{2,0},{4,6},{6,4},{8,10},{10,8},{12,14},{14,12},{16,18},{18,... | collective-permute-start | bytes 245768 | tf_op jit(solution)/shard_map/ppermute | solution.py:263
  43.5 12.2 %collective-permute-start.13 = (bf16[320,128]{1,0:T(8,128)(2,1)S(1)}, bf16[320,128]{1,0:T(8,128)(2,1)S(1)}, u32[]{:S(2)}, u32[]{:S(2)}) collective-permute-start(bf16[320,128]{1,0:T(8,128)(2,1)S(1)} %shard_map.99.refs_3_), channel_id=1, source_target_pairs={{0,4},{2,6},{4,0},{6,2},{8,12},{10,14},{12,8},{14,10},{16,20},{18,... | collective-permute-start | bytes 245768 | tf_op jit(solution)/shard_map/ppermute | solution.py:263
  54.3 8.2 %collective-permute-start.24 = (bf16[2,320,128]{2,1,0:T(8,128)(2,1)S(1)}, bf16[2,320,128]{2,1,0:T(8,128)(2,1)S(1)}, u32[]{:S(2)}, u32[]{:S(2)}) collective-permute-start(bf16[2,320,128]{2,1,0:T(8,128)(2,1)S(1)} %get-tuple-element.32), channel_id=1, source_target_pairs={{0,8},{2,10},{4,12},{6,14},{8,0},{10,2},{12,4},{14,6},{16,24},{18,... | collective-permute-start | bytes 491528 | tf_op jit(solution)/shard_map/ppermute | solution.py:263
  55.7 5.3 %collective-permute-start.15 = (bf16[320,128]{1,0:T(8,128)(2,1)S(1)}, bf16[320,128]{1,0:T(8,128)(2,1)S(1)}, u32[]{:S(2)}, u32[]{:S(2)}) collective-permute-start(bf16[320,128]{1,0:T(8,128)(2,1)S(1)} %shard_map.99.refs_3_), channel_id=1, source_target_pairs={{0,6},{2,4},{4,2},{6,0},{8,14},{10,12},{12,10},{14,8},{16,22},{18,... | collective-permute-start | bytes 245768 | tf_op jit(solution)/shard_map/ppermute | solution.py:263
  61.1 33.4 %copy-start.4 = (bf16[1,2,2560,128]{3,2,1,0:T(8,128)(2,1)S(1)}, bf16[1,2,2560,128]{3,2,1,0:T(8,128)(2,1)}, u32[]{:S(2)}) copy-start(bf16[1,2,2560,128]{3,2,1,0:T(8,128)(2,1)} %trail_ref.1) | copy-start | bytes 3932164
  62.4 32.1 %copy-start = (bf16[1,2,2560,128]{3,2,1,0:T(8,128)(2,1)S(1)}, bf16[1,2,2560,128]{3,2,1,0:T(8,128)(2,1)}, u32[]{:S(2)}) copy-start(bf16[1,2,2560,128]{3,2,1,0:T(8,128)(2,1)} %refs_13_.1) | copy-start | bytes 3932164
  62.4 32.1 %copy-start.6 = (s32[16,16]{1,0:T(8,128)S(1)}, s32[16,16]{1,0:T(8,128)}, u32[]{:S(2)}) copy-start(s32[16,16]{1,0:T(8,128)} %ranks_ref.3) | copy-start | bytes 3076
  62.4 32.1 %copy-start.12 = (s32[16]{0:T(128)S(1)}, s32[16]{0:T(128)}, u32[]{:S(2)}) copy-start(s32[16]{0:T(128)} %tiles_ref.5) | copy-start | bytes 196
  62.4 26.6 %collective-permute-start.16 = (f32[512,256]{1,0:T(8,128)S(1)}, f32[512,256]{1,0:T(8,128)S(1)}, u32[]{:S(2)}, u32[]{:S(2)}) collective-permute-start(f32[512,256]{1,0:T(8,128)S(1)} %get-tuple-element.24), channel_id=1, source_target_pairs={{0,1},{1,0},{2,3},{3,2},{4,5},{5,4},{6,7},{7,6},{8,9},{9,8},{10,11... | collective-permute-start | bytes 1572872 | tf_op jit(solution)/shard_map/ppermute | solution.py:263
  63.1 11.1 %collective-permute-start.25 = (bf16[2,320,128]{2,1,0:T(8,128)(2,1)S(1)}, bf16[2,320,128]{2,1,0:T(8,128)(2,1)S(1)}, u32[]{:S(2)}, u32[]{:S(2)}) collective-permute-start(bf16[2,320,128]{2,1,0:T(8,128)(2,1)S(1)} %shard_map.104.kept_ref), channel_id=1, source_target_pairs={{0,16},{2,18},{4,20},{6,22},{8,24},{10,26},{12,28},{14,30},{16,0},... | collective-permute-start | bytes 491528 | tf_op jit(solution)/shard_map/ppermute | solution.py:263
  74.8 5.9 %collective-permute-start.26 = (bf16[2,320,128]{2,1,0:T(8,128)(2,1)S(1)}, bf16[2,320,128]{2,1,0:T(8,128)(2,1)S(1)}, u32[]{:S(2)}, u32[]{:S(2)}) collective-permute-start(bf16[2,320,128]{2,1,0:T(8,128)(2,1)S(1)} %shard_map.105.refs_4_), channel_id=1, source_target_pairs={{0,8},{2,10},{4,12},{6,14},{8,0},{10,2},{12,4},{14,6},{16,24},{18,... | collective-permute-start | bytes 491528 | tf_op jit(solution)/shard_map/ppermute | solution.py:263
  75.4 8.5 %collective-permute-start.29 = (bf16[2,320,128]{2,1,0:T(8,128)(2,1)S(1)}, bf16[2,320,128]{2,1,0:T(8,128)(2,1)S(1)}, u32[]{:S(2)}, u32[]{:S(2)}) collective-permute-start(bf16[2,320,128]{2,1,0:T(8,128)(2,1)S(1)} %shard_map.105.refs_4_), channel_id=1, source_target_pairs={{0,4},{2,6},{4,0},{6,2},{8,12},{10,14},{12,8},{14,10},{16,20},{18,... | collective-permute-start | bytes 491528 | tf_op jit(solution)/shard_map/ppermute | solution.py:263
  80.7 7.1 %collective-permute-start.28 = (bf16[2,320,128]{2,1,0:T(8,128)(2,1)S(1)}, bf16[2,320,128]{2,1,0:T(8,128)(2,1)S(1)}, u32[]{:S(2)}, u32[]{:S(2)}) collective-permute-start(bf16[2,320,128]{2,1,0:T(8,128)(2,1)S(1)} %collective-permute-done.26.refs_5_), channel_id=1, source_target_pairs={{0,2},{2,0},{4,6},{6,4},{8,10},{10,8},{12,14},{14,12},{16,18},{18,... | collective-permute-start | bytes 491528 | tf_op jit(solution)/shard_map/ppermute | solution.py:263
  81.6 9.2 %collective-permute-start.27 = (bf16[2,320,128]{2,1,0:T(8,128)(2,1)S(1)}, bf16[2,320,128]{2,1,0:T(8,128)(2,1)S(1)}, u32[]{:S(2)}, u32[]{:S(2)}) collective-permute-start(bf16[2,320,128]{2,1,0:T(8,128)(2,1)S(1)} %shard_map.105.refs_4_), channel_id=1, source_target_pairs={{0,2},{2,0},{4,6},{6,4},{8,10},{10,8},{12,14},{14,12},{16,18},{18,... | collective-permute-start | bytes 491528 | tf_op jit(solution)/shard_map/ppermute | solution.py:263
  82.7 10.8 %collective-permute-start.30 = (bf16[2,320,128]{2,1,0:T(8,128)(2,1)S(1)}, bf16[2,320,128]{2,1,0:T(8,128)(2,1)S(1)}, u32[]{:S(2)}, u32[]{:S(2)}) collective-permute-start(bf16[2,320,128]{2,1,0:T(8,128)(2,1)S(1)} %collective-permute-done.26.refs_5_), channel_id=1, source_target_pairs={{0,4},{2,6},{4,0},{6,2},{8,12},{10,14},{12,8},{14,10},{16,20},{18,... | collective-permute-start | bytes 491528 | tf_op jit(solution)/shard_map/ppermute | solution.py:263
  83.9 13.3 %collective-permute-start.31 = (bf16[2,320,128]{2,1,0:T(8,128)(2,1)S(1)}, bf16[2,320,128]{2,1,0:T(8,128)(2,1)S(1)}, u32[]{:S(2)}, u32[]{:S(2)}) collective-permute-start(bf16[2,320,128]{2,1,0:T(8,128)(2,1)S(1)} %collective-permute-done.29.refs_8_), channel_id=1, source_target_pairs={{0,2},{2,0},{4,6},{6,4},{8,10},{10,8},{12,14},{14,12},{16,18},{18,... | collective-permute-start | bytes 491528 | tf_op jit(solution)/shard_map/ppermute | solution.py:263
  87.8 9.5 %collective-permute-start.32 = (bf16[2,320,128]{2,1,0:T(8,128)(2,1)S(1)}, bf16[2,320,128]{2,1,0:T(8,128)(2,1)S(1)}, u32[]{:S(2)}, u32[]{:S(2)}) collective-permute-start(bf16[2,320,128]{2,1,0:T(8,128)(2,1)S(1)} %collective-permute-done.28.refs_7_), channel_id=1, source_target_pairs={{0,4},{2,6},{4,0},{6,2},{8,12},{10,14},{12,8},{14,10},{16,20},{18,... | collective-permute-start | bytes 491528 | tf_op jit(solution)/shard_map/ppermute | solution.py:263
  89.0 8.2 %collective-permute-start.17 = (f32[128,256]{1,0:T(8,128)S(1)}, f32[128,256]{1,0:T(8,128)S(1)}, u32[]{:S(2)}, u32[]{:S(2)}) collective-permute-start(f32[128,256]{1,0:T(8,128)S(1)} %get-tuple-element.26), channel_id=1, source_target_pairs={{0,8},{2,10},{4,12},{6,14},{8,0},{10,2},{12,4},{14,6},{16,24},{18,... | collective-permute-start | bytes 393224 | tf_op jit(solution)/shard_map/ppermute | solution.py:263
  90.9 10.0 %collective-permute-start.18 = (f32[128,256]{1,0:T(8,128)S(1)}, f32[128,256]{1,0:T(8,128)S(1)}, u32[]{:S(2)}, u32[]{:S(2)}) collective-permute-start(f32[128,256]{1,0:T(8,128)S(1)} %get-tuple-element.27), channel_id=1, source_target_pairs={{0,16},{2,18},{4,20},{6,22},{8,24},{10,26},{12,28},{14,30},{16,0},... | collective-permute-start | bytes 393224 | tf_op jit(solution)/shard_map/ppermute | solution.py:263
  93.6 7.3 %collective-permute-start.19 = (f32[128,256]{1,0:T(8,128)S(1)}, f32[128,256]{1,0:T(8,128)S(1)}, u32[]{:S(2)}, u32[]{:S(2)}) collective-permute-start(f32[128,256]{1,0:T(8,128)S(1)} %get-tuple-element.28), channel_id=1, source_target_pairs={{0,24},{2,26},{4,28},{6,30},{8,16},{10,18},{12,20},{14,22},{16,8},... | collective-permute-start | bytes 393224 | tf_op jit(solution)/shard_map/ppermute | solution.py:263
